TPU v7x, 32 devices: a whole 2x2x4 slice. The times are simulated.
32 devices in a mesh: seq: 4 (over z), fsdp: 8 (over y, x, core).
Axes of the slice: x: 2, y: 2, z: 4, core: 2. Of those that a mesh axis runs over, the one named last changes fastest.
Arguments:
- tokens: bfloat16 [8, 1024, 2048], P('fsdp', 'seq'), may hold values from -6 to 6
- attention_gain: bfloat16 [2048], P('fsdp'), may hold values from 0.099609375 to 1.8984375
- query_weight: bfloat16 [2048, 2048], P('fsdp'), may hold values from -0.125 to 0.125
- key_projection_weight: bfloat16 [2048, 1024], P('fsdp'), may hold values from -0.125 to 0.125
- value_projection_weight: bfloat16 [2048, 1024], P('fsdp'), may hold values from -0.125 to 0.125
- query_gain: bfloat16 [128], P('fsdp'), may hold values from 0.099609375 to 1.8984375
- key_gain: bfloat16 [128], P('fsdp'), may hold values from 0.099609375 to 1.8984375
- output_weight: bfloat16 [2048, 2048], P('fsdp'), may hold values from -2 to 2
- feed_gain: bfloat16 [2048], P('fsdp'), may hold values from 0.099609375 to 1.8984375
- gate_weight: bfloat16 [2048, 6144], P('fsdp'), may hold values from -0.125 to 0.125
- up_weight: bfloat16 [2048, 6144], P('fsdp'), may hold values from -0.125 to 0.125
- down_weight: bfloat16 [6144, 2048], P('fsdp'), may hold values from -0.078125 to 0.078125
- cotangent: bfloat16 [8, 1024, 2048], P('fsdp', 'seq'), may hold values from -6 to 6
- seq_lengths: int32 [24], replicated, may hold values from 256 to 512, as said below
- dealing: int32 [24], replicated, may hold values from 0 to 23, as said below
Outputs:
- mixed: bfloat16 [8, 1024, 2048], P('fsdp', 'seq')
- input_gradient: bfloat16 [8, 1024, 2048], P('fsdp', 'seq')
- attention_gain_gradient: float32 [2048], P('fsdp')
- query_weight_gradient: float32 [2048, 2048], P('fsdp')
- key_weight_gradient: float32 [2048, 1024], P('fsdp')
- value_weight_gradient: float32 [2048, 1024], P('fsdp')
- query_gain_gradient: float32 [128], P('fsdp')
- key_gain_gradient: float32 [128], P('fsdp')
- output_weight_gradient: float32 [2048, 2048], P('fsdp')
- feed_gain_gradient: float32 [2048], P('fsdp')
- gate_weight_gradient: float32 [2048, 6144], P('fsdp')
- up_weight_gradient: float32 [2048, 6144], P('fsdp')
- down_projection_gradient: float32 [6144, 2048], P('fsdp')
Inputs may be any that keep to these rules, and one draw needn't show every extreme that they name: `seq_lengths`: the sequences dealt to one group sum to at most 1024 tokens; in some group one sequence is 512 long and the group has no padding. A permutation of the 24 sequences; group g packs dealing[g * 3] to dealing[g * 3 + 2].
All inputs are finite; a program needn't handle non-finite values.
Results may differ from a plain program's by a relative error of at most 0.02.
Values may be sent and summed in bfloat16 or wider, within the bound.
No kernel may reach another device: no remote copies, remote signals or barrier semaphores. Data moves between devices by JAX's collectives and lax.ppermute only.
A program may use at most 512 MiB of HBM per device.

v0:
```python
import jax
import jax.numpy as jnp
from jax import lax
from jax.sharding import PartitionSpec as P

EPSILON = 1e-06
ROPE_BASE = 1000000.0
NEGATIVE = -1e30


def group_layout(seq_lengths, dealing, group_index, group_span, slot_count):
    dealt_ids = lax.dynamic_slice_in_dim(dealing, group_index * slot_count, slot_count)
    seq_numbers = jnp.arange(seq_lengths.shape[0], dtype=jnp.int32)
    dealt_lengths = jnp.sum(
        jnp.where(dealt_ids[:, None] == seq_numbers[None, :], seq_lengths[None, :], 0), axis=1
    )
    seq_ends = jnp.cumsum(dealt_lengths)
    seq_starts = jnp.concatenate([jnp.zeros((1,), jnp.int32), seq_ends])
    row_index = jnp.arange(group_span, dtype=jnp.int32)
    segment = jnp.sum((row_index[:, None] >= seq_ends[None, :]).astype(jnp.int32), axis=1)
    slot_marks = jnp.arange(slot_count + 1, dtype=jnp.int32)
    seq_begin = jnp.sum(
        jnp.where(segment[:, None] == slot_marks[None, :], seq_starts[None, :], 0), axis=1
    )
    return (segment, row_index - seq_begin)


def turned(values, position, direction):
    half_size = values.shape[-1] // 2
    exponent = jnp.arange(half_size, dtype=jnp.float32) * (2.0 / values.shape[-1])
    frequency = ROPE_BASE ** (-exponent)
    angles = position.astype(jnp.float32)[:, None] * frequency[None, :]
    cosine = jnp.cos(angles)[:, None, :]
    sine = jnp.sin(angles)[:, None, :]
    lower_half = values[..., :half_size]
    upper_half = values[..., half_size:]
    return jnp.concatenate(
        [
            lower_half * cosine - direction * upper_half * sine,
            upper_half * cosine + direction * lower_half * sine,
        ],
        axis=-1,
    )


def norm_back(gradient, unit_rows, inverse):
    return inverse * (gradient - unit_rows * jnp.mean(gradient * unit_rows, axis=-1, keepdims=True))


def block_scores(
    query_block, key_rows, segment_block, index_block, segment, row_index, score_scale
):
    scores = (
        jnp.einsum("qgrd,kgd->grqk", query_block, key_rows, preferred_element_type=jnp.float32)
        * score_scale
    )
    allowed = (segment_block[:, None] == segment[None, :]) & (
        index_block[:, None] >= row_index[None, :]
    )
    return jnp.where(allowed[None, None], scores, NEGATIVE)


def attend_forward(query_rows, key_rows, value_rows, segment, score_scale, block_rows):
    group_span, head_count, head_size = query_rows.shape
    kv_count = key_rows.shape[1]
    repeat_count = head_count // kv_count
    row_index = jnp.arange(group_span, dtype=jnp.int32)

    def one_block(first_row):
        query_block = lax.dynamic_slice_in_dim(query_rows, first_row, block_rows, 0).reshape(
            block_rows, kv_count, repeat_count, head_size
        )
        segment_block = lax.dynamic_slice_in_dim(segment, first_row, block_rows, 0)
        index_block = lax.dynamic_slice_in_dim(row_index, first_row, block_rows, 0)
        scores = block_scores(
            query_block, key_rows, segment_block, index_block, segment, row_index, score_scale
        )
        row_max = jnp.max(scores, axis=-1, keepdims=True)
        weights = jnp.exp(scores - row_max)
        row_total = jnp.sum(weights, axis=-1, keepdims=True)
        probabilities = (weights / row_total).astype(jnp.bfloat16)
        result = jnp.einsum(
            "grqk,kgd->qgrd", probabilities, value_rows, preferred_element_type=jnp.float32
        )
        log_total = (row_max + jnp.log(row_total))[..., 0]
        return (result.reshape(block_rows, head_count, head_size).astype(jnp.bfloat16), log_total)

    first_rows = jnp.arange(group_span // block_rows, dtype=jnp.int32) * block_rows
    results, log_totals = lax.map(one_block, first_rows)
    return (results.reshape(group_span, head_count, head_size), log_totals)


def attend_backward(
    query_rows, key_rows, value_rows, result_grad, log_totals, segment, score_scale, block_rows
):
    group_span, head_count, head_size = query_rows.shape
    kv_count = key_rows.shape[1]
    repeat_count = head_count // kv_count
    row_index = jnp.arange(group_span, dtype=jnp.int32)

    def one_block(sums_carry, pieces):
        key_sum, value_sum = sums_carry
        first_row, log_total = pieces
        query_block = lax.dynamic_slice_in_dim(query_rows, first_row, block_rows, 0).reshape(
            block_rows, kv_count, repeat_count, head_size
        )
        grad_block = lax.dynamic_slice_in_dim(result_grad, first_row, block_rows, 0).reshape(
            block_rows, kv_count, repeat_count, head_size
        )
        segment_block = lax.dynamic_slice_in_dim(segment, first_row, block_rows, 0)
        index_block = lax.dynamic_slice_in_dim(row_index, first_row, block_rows, 0)
        scores = block_scores(
            query_block, key_rows, segment_block, index_block, segment, row_index, score_scale
        )
        probabilities = jnp.exp(scores - log_total[..., None])
        prob_grad = jnp.einsum(
            "qgrd,kgd->grqk", grad_block, value_rows, preferred_element_type=jnp.float32
        )
        row_delta = jnp.sum(probabilities * prob_grad, axis=-1, keepdims=True)
        score_grad = (probabilities * (prob_grad - row_delta)).astype(jnp.bfloat16)
        query_part = (
            jnp.einsum("grqk,kgd->qgrd", score_grad, key_rows, preferred_element_type=jnp.float32)
            * score_scale
        )
        key_sum = (
            key_sum
            + jnp.einsum(
                "grqk,qgrd->kgd", score_grad, query_block, preferred_element_type=jnp.float32
            )
            * score_scale
        )
        value_sum = value_sum + jnp.einsum(
            "grqk,qgrd->kgd",
            probabilities.astype(jnp.bfloat16),
            grad_block,
            preferred_element_type=jnp.float32,
        )
        return ((key_sum, value_sum), query_part.reshape(block_rows, head_count, head_size))

    empty_sums = jnp.zeros(key_rows.shape, jnp.float32)
    first_rows = jnp.arange(group_span // block_rows, dtype=jnp.int32) * block_rows
    (key_grad, value_grad), query_parts = lax.scan(
        one_block, (empty_sums, empty_sums), (first_rows, log_totals)
    )
    return (query_parts.reshape(group_span, head_count, head_size), key_grad, value_grad)


def owned_sum(left, right):
    return lax.psum_scatter(
        jnp.einsum("tr,tc->rc", left, right, preferred_element_type=jnp.float32).astype(
            jnp.bfloat16
        ),
        "fsdp",
        scatter_dimension=0,
        tiled=True,
    ).astype(jnp.float32)


def body(
    tokens,
    attention_gain,
    query_weight,
    key_projection_weight,
    value_projection_weight,
    query_gain,
    key_gain,
    output_weight,
    feed_gain,
    gate_weight,
    up_weight,
    down_weight,
    cotangent,
    seq_lengths,
    dealing,
):
    local_rows = tokens.shape[1]
    group_span = local_rows * lax.axis_size("seq")
    slot_count = dealing.shape[0] // lax.axis_size("fsdp")
    head_size = query_gain.shape[0] * lax.axis_size("fsdp")
    segment, position = group_layout(
        seq_lengths, dealing, lax.axis_index("fsdp"), group_span, slot_count
    )
    own_position = lax.dynamic_slice_in_dim(
        position, lax.axis_index("seq") * local_rows, local_rows, 0
    )
    block_rows = min(512, group_span)
    score_scale = head_size ** (-0.5)
    inputs = tokens[0].astype(jnp.float32)
    gain_one, query_matrix, key_matrix, value_matrix, query_norm, key_norm, output_matrix = (
        lax.all_gather(attention_gain, "fsdp", axis=0, tiled=True),
        lax.all_gather(query_weight, "fsdp", axis=0, tiled=True),
        lax.all_gather(key_projection_weight, "fsdp", axis=0, tiled=True),
        lax.all_gather(value_projection_weight, "fsdp", axis=0, tiled=True),
        lax.all_gather(query_gain, "fsdp", axis=0, tiled=True),
        lax.all_gather(key_gain, "fsdp", axis=0, tiled=True),
        lax.all_gather(output_weight, "fsdp", axis=0, tiled=True),
    )
    query_heads = query_matrix.shape[1] // head_size
    key_heads = key_matrix.shape[1] // head_size
    inverse_one = lax.rsqrt(jnp.mean(inputs * inputs, axis=-1, keepdims=True) + EPSILON)
    unit_one = inputs * inverse_one
    normed_one = (unit_one * gain_one.astype(jnp.float32)).astype(jnp.bfloat16)
    query_proj = jnp.dot(normed_one, query_matrix, preferred_element_type=jnp.float32).reshape(
        local_rows, query_heads, head_size
    )
    key_proj = jnp.dot(normed_one, key_matrix, preferred_element_type=jnp.float32).reshape(
        local_rows, key_heads, head_size
    )
    value_send = (
        jnp.dot(normed_one, value_matrix, preferred_element_type=jnp.float32)
        .astype(jnp.bfloat16)
        .reshape(local_rows, key_heads, head_size)
    )
    query_inverse = lax.rsqrt(jnp.mean(query_proj * query_proj, axis=-1, keepdims=True) + EPSILON)
    query_unit = query_proj * query_inverse
    query_send = turned(query_unit * query_norm.astype(jnp.float32), own_position, 1.0).astype(
        jnp.bfloat16
    )
    key_inverse = lax.rsqrt(jnp.mean(key_proj * key_proj, axis=-1, keepdims=True) + EPSILON)
    key_unit = key_proj * key_inverse
    key_send = turned(key_unit * key_norm.astype(jnp.float32), own_position, 1.0).astype(
        jnp.bfloat16
    )
    query_group, key_group, value_group = (
        lax.all_to_all(query_send, "seq", split_axis=1, concat_axis=0, tiled=True),
        lax.all_to_all(key_send, "seq", split_axis=1, concat_axis=0, tiled=True),
        lax.all_to_all(value_send, "seq", split_axis=1, concat_axis=0, tiled=True),
    )
    head_result, log_totals = attend_forward(
        query_group, key_group, value_group, segment, score_scale, block_rows
    )
    attended = lax.all_to_all(head_result, "seq", split_axis=0, concat_axis=1, tiled=True).reshape(
        local_rows, query_heads * head_size
    )
    residual = inputs + jnp.dot(attended, output_matrix, preferred_element_type=jnp.float32)
    gain_two, gate_matrix, up_matrix, down_matrix = (
        lax.all_gather(feed_gain, "fsdp", axis=0, tiled=True),
        lax.all_gather(gate_weight, "fsdp", axis=0, tiled=True),
        lax.all_gather(up_weight, "fsdp", axis=0, tiled=True),
        lax.all_gather(down_weight, "fsdp", axis=0, tiled=True),
    )
    inverse_two = lax.rsqrt(jnp.mean(residual * residual, axis=-1, keepdims=True) + EPSILON)
    unit_two = residual * inverse_two
    normed_two = (unit_two * gain_two.astype(jnp.float32)).astype(jnp.bfloat16)
    gate_value = jnp.dot(normed_two, gate_matrix, preferred_element_type=jnp.float32)
    up_value = jnp.dot(normed_two, up_matrix, preferred_element_type=jnp.float32)
    sigmoid_gate = jax.nn.sigmoid(gate_value)
    hidden = (gate_value * sigmoid_gate * up_value).astype(jnp.bfloat16)
    mixed = (residual + jnp.dot(hidden, down_matrix, preferred_element_type=jnp.float32)).astype(
        jnp.bfloat16
    )
    gain_two, gate_matrix, up_matrix, down_matrix = (
        lax.all_gather(feed_gain, "fsdp", axis=0, tiled=True),
        lax.all_gather(gate_weight, "fsdp", axis=0, tiled=True),
        lax.all_gather(up_weight, "fsdp", axis=0, tiled=True),
        lax.all_gather(down_weight, "fsdp", axis=0, tiled=True),
    )
    out_grad = cotangent[0]
    hidden_grad = jnp.einsum("td,fd->tf", out_grad, down_matrix, preferred_element_type=jnp.float32)
    up_grad = (hidden_grad * gate_value * sigmoid_gate).astype(jnp.bfloat16)
    gate_grad = (
        hidden_grad * up_value * sigmoid_gate * (1.0 + gate_value * (1.0 - sigmoid_gate))
    ).astype(jnp.bfloat16)
    normed_two_grad = jnp.einsum(
        "tf,df->td", gate_grad, gate_matrix, preferred_element_type=jnp.float32
    )
    normed_two_grad = normed_two_grad + jnp.einsum(
        "tf,df->td", up_grad, up_matrix, preferred_element_type=jnp.float32
    )
    feed_gain_part = jnp.sum(normed_two_grad * unit_two, axis=0)
    residual_grad = out_grad.astype(jnp.float32) + norm_back(
        normed_two_grad * gain_two.astype(jnp.float32), unit_two, inverse_two
    )
    gate_term = owned_sum(normed_two, gate_grad)
    up_term = owned_sum(normed_two, up_grad)
    down_term = owned_sum(hidden, out_grad)
    gain_one, query_matrix, key_matrix, value_matrix, query_norm, key_norm, output_matrix = (
        lax.all_gather(attention_gain, "fsdp", axis=0, tiled=True),
        lax.all_gather(query_weight, "fsdp", axis=0, tiled=True),
        lax.all_gather(key_projection_weight, "fsdp", axis=0, tiled=True),
        lax.all_gather(value_projection_weight, "fsdp", axis=0, tiled=True),
        lax.all_gather(query_gain, "fsdp", axis=0, tiled=True),
        lax.all_gather(key_gain, "fsdp", axis=0, tiled=True),
        lax.all_gather(output_weight, "fsdp", axis=0, tiled=True),
    )
    branch_grad = residual_grad.astype(jnp.bfloat16)
    output_term = owned_sum(attended, branch_grad)
    attended_grad = (
        jnp.einsum("td,ed->te", branch_grad, output_matrix, preferred_element_type=jnp.float32)
        .astype(jnp.bfloat16)
        .reshape(local_rows, query_heads, head_size)
    )
    head_grad = lax.all_to_all(attended_grad, "seq", split_axis=1, concat_axis=0, tiled=True)
    query_back, key_back, value_back = attend_backward(
        query_group, key_group, value_group, head_grad, log_totals, segment, score_scale, block_rows
    )
    query_tokens, key_tokens, value_tokens = (
        lax.all_to_all(
            query_back.astype(jnp.bfloat16), "seq", split_axis=0, concat_axis=1, tiled=True
        ),
        lax.all_to_all(
            key_back.astype(jnp.bfloat16), "seq", split_axis=0, concat_axis=1, tiled=True
        ),
        lax.all_to_all(
            value_back.astype(jnp.bfloat16), "seq", split_axis=0, concat_axis=1, tiled=True
        ),
    )
    query_turned = turned(query_tokens.astype(jnp.float32), own_position, -1.0)
    query_norm_part = jnp.sum(query_turned * query_unit, axis=(0, 1))
    query_proj_grad = (
        norm_back(query_turned * query_norm.astype(jnp.float32), query_unit, query_inverse)
        .astype(jnp.bfloat16)
        .reshape(local_rows, query_heads * head_size)
    )
    key_turned = turned(key_tokens.astype(jnp.float32), own_position, -1.0)
    key_norm_part = jnp.sum(key_turned * key_unit, axis=(0, 1))
    key_proj_grad = (
        norm_back(key_turned * key_norm.astype(jnp.float32), key_unit, key_inverse)
        .astype(jnp.bfloat16)
        .reshape(local_rows, key_heads * head_size)
    )
    value_grad = value_tokens.reshape(local_rows, key_heads * head_size)
    normed_one_grad = jnp.einsum(
        "te,de->td", query_proj_grad, query_matrix, preferred_element_type=jnp.float32
    )
    normed_one_grad = normed_one_grad + jnp.einsum(
        "te,de->td", key_proj_grad, key_matrix, preferred_element_type=jnp.float32
    )
    normed_one_grad = normed_one_grad + jnp.einsum(
        "te,de->td", value_grad, value_matrix, preferred_element_type=jnp.float32
    )
    attention_gain_part = jnp.sum(normed_one_grad * unit_one, axis=0)
    input_gradient = (
        residual_grad
        + norm_back(normed_one_grad * gain_one.astype(jnp.float32), unit_one, inverse_one)
    ).astype(jnp.bfloat16)
    query_term = owned_sum(normed_one, query_proj_grad)
    key_term = owned_sum(normed_one, key_proj_grad)
    value_term = owned_sum(normed_one, value_grad)
    gain_parts = (
        lax.psum_scatter(attention_gain_part, "fsdp", scatter_dimension=0, tiled=True),
        lax.psum_scatter(query_norm_part, "fsdp", scatter_dimension=0, tiled=True),
        lax.psum_scatter(key_norm_part, "fsdp", scatter_dimension=0, tiled=True),
        lax.psum_scatter(feed_gain_part, "fsdp", scatter_dimension=0, tiled=True),
    )
    totals = (
        lax.psum(gain_parts[0].astype(jnp.bfloat16), "seq").astype(jnp.float32),
        lax.psum(query_term.astype(jnp.bfloat16), "seq").astype(jnp.float32),
        lax.psum(key_term.astype(jnp.bfloat16), "seq").astype(jnp.float32),
        lax.psum(value_term.astype(jnp.bfloat16), "seq").astype(jnp.float32),
        lax.psum(gain_parts[1].astype(jnp.bfloat16), "seq").astype(jnp.float32),
        lax.psum(gain_parts[2].astype(jnp.bfloat16), "seq").astype(jnp.float32),
        lax.psum(output_term.astype(jnp.bfloat16), "seq").astype(jnp.float32),
        lax.psum(gain_parts[3].astype(jnp.bfloat16), "seq").astype(jnp.float32),
        lax.psum(gate_term.astype(jnp.bfloat16), "seq").astype(jnp.float32),
        lax.psum(up_term.astype(jnp.bfloat16), "seq").astype(jnp.float32),
        lax.psum(down_term.astype(jnp.bfloat16), "seq").astype(jnp.float32),
    )
    return (mixed[None], input_gradient[None]) + tuple(totals)


def solution(mesh):
    placed = (
        P("fsdp", "seq", None),
        P("fsdp"),
        P("fsdp", None),
        P("fsdp", None),
        P("fsdp", None),
        P("fsdp"),
        P("fsdp"),
        P("fsdp", None),
        P("fsdp"),
        P("fsdp", None),
        P("fsdp", None),
        P("fsdp", None),
        P("fsdp", "seq", None),
        P(),
        P(),
    )
    return jax.shard_map(
        body,
        mesh=mesh,
        in_specs=placed,
        out_specs=(
            P("fsdp", "seq", None),
            P("fsdp", "seq", None),
            P("fsdp"),
            P("fsdp", None),
            P("fsdp", None),
            P("fsdp", None),
            P("fsdp"),
            P("fsdp"),
            P("fsdp", None),
            P("fsdp"),
            P("fsdp", None),
            P("fsdp", None),
            P("fsdp", None),
        ),
        check_vma=False,
    )
```

profile of v0, /device:TPU:0, one launch (start us, length us, event | category | flops | bytes accessed | tf_op | source)
XLA Modules:
  0.0 1938.2 jit_solution(14317714284067807112)
XLA Ops:
  12.4 10.4 all-gather
  24.6 13.3 all-reduce.7
  39.6 9.7 all-gather.12.cloned.1.call-done
  49.3 6.4 copy.113
  61.5 4.5 all-to-all-start.1
  66.1 21.7 %all-gather.14.cloned.1.call-done = bf16[2048,1024]{1,0:T(8,128)(2,1)} async-done(((bf16[256,1024]{1,0:T(8,128)(2,1)}), bf16[2048,1024]{1,0:T(8,128)(2,1)}) %all-gather.14.cloned.1.call-update) | async-done | bytes 4194320 | tf_op jit(solution)/shard_map/all_gather | solution.py:193
  92.1 51.8 %all-gather.10.cloned.1.call-done = bf16[2048,2048]{1,0:T(8,128)(2,1)} async-done(((bf16[256,2048]{1,0:T(8,128)(2,1)}), bf16[2048,2048]{1,0:T(8,128)(2,1)}) %all-gather.10.cloned.1.call-update) | async-done | bytes 8388624 | tf_op jit(solution)/shard_map/all_gather | solution.py:191
  143.9 12.5 copy.111
  156.4 5.9 multiply_reduce_fusion.5
  162.3 4.5 all-to-all-start.2
  168.7 13.2 all-to-all-done.2
  188.0 22.8 %all-to-all-done = bf16[256,16,128]{0,2,1:T(8,128)(2,1)S(1)} async-done(((bf16[256,16,128]{0,2,1:T(8,128)(2,1)}), bf16[256,16,128]{0,2,1:T(8,128)(2,1)S(1)}, u32[]{:S(2)}, u32[]{:S(2)}) %all-to-all-start) | async-done | bytes 1048608 | tf_op jit(solution)/shard_map/all_to_all | solution.py:225
  213.5 24.1 %while.29 = (s32[]{:T(128)}, bf16[2,512,4,128]{3,1,0,2:T(8,128)(2,1)}, f32[2,2,2,512]{3,2,1,0:T(2,128)S(1)}, s32[2]{0:T(128)S(1)}, s32[1024]{0:T(1024)S(1)}, /*i...) while((s32[]{:T(128)}, ...), condition=%wide.region_10.11_spmd.clone, body=%wide.region_7.10_spmd.clone.sunk | while | flops 1100740608 | bytes 39932148 | solution.py:89
  244.9 9.1 all-gather.1
  254.1 16.2 all-to-all-done.3
  274.9 6.2 multiply_reduce_fusion.4
  282.6 44.3 %all-gather.18.cloned.1.call-done = bf16[2048,6144]{1,0:T(8,128)(2,1)} async-done(((bf16[256,6144]{1,0:T(8,128)(2,1)}), bf16[2048,6144]{1,0:T(8,128)(2,1)}) %all-gather.18.cloned.1.call-update) | async-done | bytes 25165840 | tf_op jit(solution)/shard_map/all_gather | solution.py:238
  326.9 14.8 fusion.76
  341.7 112.1 %all-gather.20.cloned.1.call-done = bf16[2048,6144]{1,0:T(8,128)(2,1)} async-done(((bf16[256,6144]{1,0:T(8,128)(2,1)}), bf16[2048,6144]{1,0:T(8,128)(2,1)}) %all-gather.20.cloned.1.call-update) | async-done | bytes 25165840 | tf_op jit(solution)/shard_map/all_gather | solution.py:239
  453.9 14.8 fusion.77
  468.7 112.3 %all-gather.22.cloned.1.call-done = bf16[6144,2048]{1,0:T(8,128)(2,1)} async-done(((bf16[768,2048]{1,0:T(8,128)(2,1)}), bf16[6144,2048]{1,0:T(8,128)(2,1)}) %all-gather.22.cloned.1.call-update) | async-done | bytes 25165840 | tf_op jit(solution)/shard_map/all_gather | solution.py:240
  581.0 20.4 %multiply_convert_fusion = (bf16[256,6144]{1,0:T(8,128)(2,1)}, bf16[256,6144]{1,0:T(8,128)(2,1)}, bf16[256,6144]{1,0:T(8,128)(2,1)}) fusion(f32[256,6144]{1,0:T(8,128)} %fusion.76, f32[256,6144]{1,0:T(8,128)} %fusion.77, bf16[6144,2048]{1,0:T(8,128)(2,1)} %all-gather.22.cloned.1.call-done, bf16[1,256,2048]{2,1,0:T(8,128)(2,1)} %param.31), kind=kOutput, calls=%fused_computation.51 | convolution fusion | flops 6467616768 | bytes 48234496 | tf_op jit(solution)/shard_map/td,fd->tf/dot_general | solution.py:259
  601.3 13.9 fusion.78
  615.2 15.6 multiply_reduce_fusion
  633.6 6.5 fusion.52
  641.4 4.6 all-to-all-start.4
  646.0 26.2 %all-to-all-done.4 = bf16[256,16,128]{2,0,1:T(8,128)(2,1)} async-done(((bf16[256,16,128]{2,0,1:T(8,128)(2,1)}), bf16[256,16,128]{2,0,1:T(8,128)(2,1)}, u32[]{:S(2)}, u32[]{:S(2)}) %all-to-all-start.4) | async-done | bytes 1048608 | tf_op jit(solution)/shard_map/all_to_all | solution.py:293
  674.5 53.2 %while.30 = (s32[]{:T(128)}, f32[1024,2,128]{0,2,1:T(8,128)S(1)}, f32[1024,2,128]{0,2,1:T(8,128)}, bf16[2,512,4,128]{3,1,0,2:T(8,128)(2,1)}, s32[2]{0:T(128)S(1)...) while((s32[]{:T(128)}, f32[1024,2,128]{0,2,1:T(8,128)S(1)}, ...), condition=%wide.region_15.16_spmd.clone.clone, body=%wide.region_13.15_spmd.clone.clone.sunk | while | flops 2719217664 | bytes 194065008 | solution.py:142
  681.7 4.4 fusion.151
  708.2 4.4 fusion.151
  728.3 16.7 all_to_all.120
  752.3 16.5 all_to_all.121
  774.9 6.8 convolution_convert_fusion.3
  783.9 28.7 %all_to_all.122 = bf16[1024,4,128]{2,1,0:T(4,128)(2,1)S(1)} all-to-all(bf16[1024,4,128]{2,1,0:T(4,128)(2,1)S(1)} %copy.124), channel_id=1, replica_groups=mesh['seq'=4,'fsdp'=8] {'seq'}, dimensions={0} | all-to-all | bytes 2097152 | tf_op jit(solution)/shard_map/all_to_all | solution.py:298
  821.9 6.0 convolution_convert_fusion.4
  828.0 13.8 convolution_convert_fusion.2
  841.8 13.7 convolution_convert_fusion.1
  855.6 16.8 convolution_convert_fusion
  872.5 57.4 %reduce-scatter.14.cloned.1.call-done = bf16[256,2048]{1,0:T(8,128)(2,1)} async-done(((bf16[2048,2048]{1,0:T(8,128)(2,1)}), bf16[256,2048]{1,0:T(8,128)(2,1)}) %reduce-scatter.14.cloned.1.call-update) | async-done | bytes 1048592 | tf_op jit(solution)/shard_map/reduce_scatter | solution.py:149
  929.9 75.0 %reduce-scatter.8.cloned.1.call-done = bf16[256,2048]{1,0:T(8,128)(2,1)} async-done(((bf16[2048,2048]{1,0:T(8,128)(2,1)}), bf16[256,2048]{1,0:T(8,128)(2,1)}) %reduce-scatter.8.cloned.1.call-update) | async-done | bytes 1048592 | tf_op jit(solution)/shard_map/reduce_scatter | solution.py:149
  1004.9 159.8 %reduce-scatter.16.cloned.1.call-done = bf16[256,6144]{1,0:T(8,128)(2,1)} async-done(((bf16[2048,6144]{1,0:T(8,128)(2,1)}), bf16[256,6144]{1,0:T(8,128)(2,1)}) %reduce-scatter.16.cloned.1.call-update) | async-done | bytes 3145744 | tf_op jit(solution)/shard_map/reduce_scatter | solution.py:149
  1164.7 159.9 %reduce-scatter.18.cloned.1.call-done = bf16[256,6144]{1,0:T(8,128)(2,1)} async-done(((bf16[2048,6144]{1,0:T(8,128)(2,1)}), bf16[256,6144]{1,0:T(8,128)(2,1)}) %reduce-scatter.18.cloned.1.call-update) | async-done | bytes 3145744 | tf_op jit(solution)/shard_map/reduce_scatter | solution.py:149
  1324.7 159.8 %reduce-scatter.20.cloned.1.call-done = bf16[768,2048]{1,0:T(8,128)(2,1)} async-done(((bf16[6144,2048]{1,0:T(8,128)(2,1)}), bf16[768,2048]{1,0:T(8,128)(2,1)}) %reduce-scatter.20.cloned.1.call-update) | async-done | bytes 3145744 | tf_op jit(solution)/shard_map/reduce_scatter | solution.py:149
  1485.8 15.2 fusion.41
  1501.0 6.0 fusion.79
  1512.5 24.0 %all-reduce.6 = (bf16[2048]{0:T(1024)(128)(2,1)S(1)}, bf16[128]{0:T(256)(128)(2,1)S(1)}, bf16[128]{0:T(256)(128)(2,1)S(1)}, bf16[2048]{0:T(1024)(128)(2,1)S(1)}) all-reduce(f32[2048]{0:T(1024)S(1)} %get-tuple-element.229, f32[128]{0:T(128)S(1)} %get-tuple-element.225, ...), channel_id=2, replica_groups=mesh['seq'=4,'fsdp'=8] {'fsdp'}, use_global_device_ids=true, to_apply=%region_20.21.clone | all-reduce | flops 4352 | bytes 26112
  1536.8 13.8 all-reduce.8
  1556.0 358.3 %all-reduce.12.cloned.1.call-done = (bf16[256,2048]{1,0:T(8,128)(2,1)}, bf16[256,1024]{1,0:T(8,128)(2,1)}, bf16[256,1024]{1,0:T(8,128)(2,1)}, bf16[256,2048]{1,0...) async-done(((bf16[256,2048]{1,0:T(8,128)(2,1)}, bf16[256,1024]{1,0:T(8,128)(2,1)}, bf16[256,1024]{1,0:T(8,128)(2,1)}, ...) | async-done | bytes 12582928 | tf_op jit(solution)/shard_map/psum | solution.py:348
  (332 shorter events, 162.0 us)
Async XLA Ops:
  7.2 42.1 %all-gather.12.cloned.1.call-start = ((), (), s32[]{:S(2)}) async-start(), calls=%async_computation.16 | async-start | bytes 4718592 | tf_op jit(solution)/shard_map/all_gather | solution.py:192
  7.9 79.8 %all-gather.14.cloned.1.call-start = ((), (), s32[]{:S(2)}) async-start(), calls=%async_computation.17 | async-start | bytes 4718592 | tf_op jit(solution)/shard_map/all_gather | solution.py:193
  8.7 135.2 %all-gather.10.cloned.1.call-start = ((), (), s32[]{:S(2)}) async-start(), calls=%async_computation.15 | async-start | bytes 9437184 | tf_op jit(solution)/shard_map/all_gather | solution.py:191
  9.4 265.5 %all-gather.16.cloned.1.call-start = ((), (), s32[]{:S(2)}) async-start(), calls=%async_computation.18 | async-start | bytes 9437184 | tf_op jit(solution)/shard_map/all_gather | solution.py:196
  10.0 316.9 %all-gather.18.cloned.1.call-start = ((), (), s32[]{:S(2)}) async-start(), calls=%async_computation.19 | async-start | bytes 28311552 | tf_op jit(solution)/shard_map/all_gather | solution.py:238
  10.6 12.3 copy-start.58
  10.6 13.5 copy-start.62
  10.6 13.8 copy-start.63
  10.6 27.7 %copy-start.3 = (bf16[1,256,2048]{2,1,0:T(8,128)(2,1)S(1)}, bf16[1,256,2048]{2,1,0:T(8,128)(2,1)}, u32[]{:S(2)}) copy-start(bf16[1,256,2048]{2,1,0:T(8,128)(2,1)} %param.19) | copy-start | bytes 3145732
  10.6 443.2 %all-gather.20.cloned.1.call-start = ((), (), s32[]{:S(2)}) async-start(), calls=%async_computation.20 | async-start | bytes 28311552 | tf_op jit(solution)/shard_map/all_gather | solution.py:239
  11.2 569.7 %all-gather.22.cloned.1.call-start = ((), (), s32[]{:S(2)}) async-start(), calls=%async_computation.21 | async-start | bytes 28311552 | tf_op jit(solution)/shard_map/all_gather | solution.py:240
  22.9 133.5 %copy-start.34 = (f32[8,1,256]{2,1,0:T(1,128)}, f32[8,1,256]{2,1,0:T(1,128)S(1)}, u32[]{:S(2)}) copy-start(f32[8,1,256]{2,1,0:T(1,128)S(1)} %convert_element_type.300) | copy-start | bytes 24580
  37.9 128.9 %copy-start.54 = (f32[128]{0:T(128)}, f32[128]{0:T(128)S(1)}, u32[]{:S(2)}) copy-start(f32[128]{0:T(128)S(1)} %convert_element_type.236) | copy-start | bytes 1540
  38.0 21.4 %copy-start.56 = (f32[128]{0:T(128)}, f32[128]{0:T(128)S(1)}, u32[]{:S(2)}) copy-start(f32[128]{0:T(128)S(1)} %convert_element_type.238) | copy-start | bytes 1540
  38.6 117.7 %copy-start.49 = (f32[256]{0:T(256)}, f32[256]{0:T(256)S(1)}, u32[]{:S(2)}) copy-start(f32[256]{0:T(256)S(1)} %add_rsqrt_fusion.3) | copy-start | bytes 3076
  39.6 127.6 %copy-start.32 = (f32[256,64]{0,1:T(8,128)}, f32[256,64]{0,1:T(8,128)S(1)}, u32[]{:S(2)}) copy-start(f32[256,64]{0,1:T(8,128)S(1)} %get-tuple-element.311) | copy-start | bytes 196612
  61.5 100.7 %all-to-all-start.1 = ((bf16[256,8,128]{0,2,1:T(8,128)(2,1)}), bf16[256,8,128]{0,2,1:T(8,128)(2,1)}, u32[]{:S(2)}, u32[]{:S(2)}) async-start(bf16[256,8,128]{0,2,1:T(8,128)(2,1)} %pad_maximum_fusion.3), calls=%async_computation.1 | async-start | bytes 1048576 | tf_op jit(solution)/shard_map/all_to_all | solution.py:226
  162.2 5.3 copy-start.14
  162.3 19.6 %all-to-all-start.2 = ((bf16[256,8,128]{2,0,1:T(8,128)(2,1)}), bf16[256,8,128]{2,0,1:T(8,128)(2,1)}, u32[]{:S(2)}, u32[]{:S(2)}) async-start(bf16[256,8,128]{2,0,1:T(8,128)(2,1)} %bitcast.354), calls=%async_computation.2 | async-start | bytes 1048576 | tf_op jit(solution)/shard_map/all_to_all | solution.py:227
  181.8 29.0 %all-to-all-start = ((bf16[256,16,128]{0,2,1:T(8,128)(2,1)}), bf16[256,16,128]{0,2,1:T(8,128)(2,1)S(1)}, u32[]{:S(2)}, u32[]{:S(2)}) async-start(bf16[256,16,128]{0,2,1:T(8,128)(2,1)} %pad_maximum_fusion.1), calls=%async_computation | async-start | bytes 2097152 | tf_op jit(solution)/shard_map/all_to_all | solution.py:225
  237.6 7.3 copy-start.64
  240.7 29.6 %all-to-all-start.3 = ((bf16[1024,4,128]{2,1,0:T(4,128)(2,1)}), bf16[1024,4,128]{2,1,0:T(4,128)(2,1)}, u32[]{:S(2)}, u32[]{:S(2)}) async-start(bf16[1024,4,128]{2,1,0:T(4,128)(2,1)} %copy.118), calls=%async_computation.3 | async-start | bytes 2097152 | tf_op jit(solution)/shard_map/all_to_all | solution.py:232
  282.6 171.2 %copy-start.17 = (bf16[256,2048]{1,0:T(8,128)(2,1)}, bf16[256,2048]{1,0:T(8,128)(2,1)S(1)}, u32[]{:S(2)}) copy-start(bf16[256,2048]{1,0:T(8,128)(2,1)S(1)} %multiply_convert_fusion.4) | copy-start | bytes 3145732
  615.2 15.6 copy-start.24
  633.6 6.5 copy-start.7
  641.4 30.8 %all-to-all-start.4 = ((bf16[256,16,128]{2,0,1:T(8,128)(2,1)}), bf16[256,16,128]{2,0,1:T(8,128)(2,1)}, u32[]{:S(2)}, u32[]{:S(2)}) async-start(bf16[256,16,128]{2,0,1:T(8,128)(2,1)} %bitcast.259), calls=%async_computation.4 | async-start | bytes 2097152 | tf_op jit(solution)/shard_map/all_to_all | solution.py:293
  646.0 226.5 %reduce-scatter.10.cloned.1.call-start = ((), (), s32[]{:S(2)}) async-start(), calls=%async_computation.23 | async-start | bytes 4718592 | tf_op jit(solution)/shard_map/reduce_scatter | solution.py:149
  674.7 6.3 copy-start.5
  681.0 5.1 copy-start
  689.9 4.9 copy-start.37
  701.2 6.3 copy-start.5
  707.5 5.1 copy-start
  727.7 17.7 copy-start.33
  727.7 17.7 copy-start.44
  727.7 17.9 copy-start.19
  727.7 17.9 copy-start.52
  727.7 17.9 copy-start.57
  750.5 122.1 %reduce-scatter.12.cloned.1.call-start = ((), (), s32[]{:S(2)}) async-start(), calls=%async_computation.24 | async-start | bytes 4718592 | tf_op jit(solution)/shard_map/reduce_scatter | solution.py:149
  773.4 156.5 %reduce-scatter.14.cloned.1.call-start = ((), (), s32[]{:S(2)}) async-start(), calls=%async_computation.25 | async-start | bytes 9437184 | tf_op jit(solution)/shard_map/reduce_scatter | solution.py:149
  781.8 223.1 %reduce-scatter.8.cloned.1.call-start = ((), (), s32[]{:S(2)}) async-start(), calls=%async_computation.22 | async-start | bytes 9437184 | tf_op jit(solution)/shard_map/reduce_scatter | solution.py:149
  827.9 336.8 %reduce-scatter.16.cloned.1.call-start = ((), (), s32[]{:S(2)}) async-start(), calls=%async_computation.26 | async-start | bytes 28311552 | tf_op jit(solution)/shard_map/reduce_scatter | solution.py:149
  841.8 482.9 %reduce-scatter.18.cloned.1.call-start = ((), (), s32[]{:S(2)}) async-start(), calls=%async_computation.27 | async-start | bytes 28311552 | tf_op jit(solution)/shard_map/reduce_scatter | solution.py:149
  855.5 628.9 %reduce-scatter.20.cloned.1.call-start = ((), (), s32[]{:S(2)}) async-start(), calls=%async_computation.28 | async-start | bytes 28311552 | tf_op jit(solution)/shard_map/reduce_scatter | solution.py:149
  872.4 1041.8 %all-reduce.12.cloned.1.call-start = ((), (), s32[]{:S(2)}) async-start(), calls=%async_computation.29 | async-start | bytes 25165824 | tf_op jit(solution)/shard_map/psum | solution.py:348
  1485.8 15.3 copy-start.28
  1501.0 6.0 copy-start.16
  1501.0 6.1 copy-start.23
  1914.3 5.1 copy-start.36
  (52 other events, 126.3 us)
Sparse Core Ops, SparseCore 0:
  9.9 39.3 all-gather.11
  51.1 36.5 all-gather.13
  89.6 54.2 all-gather.9
  145.6 54.2 all-gather.15
  201.7 125.1 all-gather.17
  328.6 125.1 all-gather.19
  455.7 125.1 all-gather.21
  750.6 49.2 reduce-scatter.9
  803.8 51.1 reduce-scatter.11
  858.4 71.5 reduce-scatter.13
  933.4 71.4 reduce-scatter.7
  1008.4 156.2 reduce-scatter.15
  1168.3 156.2 reduce-scatter.17
  1328.1 156.2 reduce-scatter.19
  1487.7 426.4 all-reduce.11
where the time goes:
time: 1950 us; the launch traced here: 1940 us
  waiting for transfers between devices  1400 us (72%)
  matrix products  236 us (12%)
  blocking collectives  133 us (7%)
  local copies, waits for them, and re-layouts  66.8 us (3%)
  other arithmetic  50.5 us (3%)
  starting transfers between devices  22.2 us (1%)
    reduce_scatter x7, waiting for transfers between devices, owned_sum(): lax.psum_scatter(jnp.einsum('tr,tc->rc', left, right, preferred_element_t...  612 us
    psum x1, waiting for transfers between devices, body(): lax.psum(query_term.astype(jnp.bfloat16), 'seq').astype(jnp.float32)  358 us
    all_gather x1, waiting for transfers between devices, body(): lax.all_gather(down_weight, 'fsdp', axis=0, tiled=True)  112 us
    all_gather x1, waiting for transfers between devices, body(): lax.all_gather(up_weight, 'fsdp', axis=0, tiled=True)  112 us
    dot_general x7, matrix products, owned_sum(): jnp.einsum('tr,tc->rc', left, right, preferred_element_type=jnp.float32)  64 us
    all_gather x1, waiting for transfers between devices, body(): lax.all_gather(query_weight, 'fsdp', axis=0, tiled=True)  51.8 us
    all_gather x1, waiting for transfers between devices, body(): lax.all_gather(gate_weight, 'fsdp', axis=0, tiled=True)  44.3 us
  transfers between devices with their start and end apart: 20, of which 16 were waited for; matrix products, arithmetic and copies ran while one was open for 11% of the time, Pallas kernels for 0%

commit v1 on v0

v1 whole, which is shorter than its diff:
```python
import jax
import jax.numpy as jnp
from jax import lax
from jax.sharding import PartitionSpec as P

EPSILON = 1e-06
ROPE_BASE = 1000000.0
NEGATIVE = -1e30
F32 = jnp.float32
BF16 = jnp.bfloat16


def relocation(ns, nf):
    pairs = []
    for s in range(ns):
        for g in range(nf):
            p, c = divmod(g, 2)
            pairs.append((s * nf + g, p * nf + 2 * (p ^ s ^ (ns // 2 * c)) + c))
    return pairs


def move(values, pairs):
    return lax.ppermute(values, ("seq", "fsdp"), pairs)


def swap(values, k):
    n = lax.axis_size("fsdp")
    return lax.ppermute(values, "fsdp", [(i, i ^ k) for i in range(n)])


def exchange(piece_for, step=1):
    n, me = lax.axis_size("fsdp"), lax.axis_index("fsdp")
    got = {0: piece_for(me)}
    for k in range(step, n, step):
        got[k] = swap(piece_for(me ^ k), k)
    return got


def assembled(got, step=1):
    n, me = lax.axis_size("fsdp"), lax.axis_index("fsdp")
    buffer = jnp.zeros((n // step,) + got[0].shape, got[0].dtype)
    for k, piece in got.items():
        buffer = lax.dynamic_update_index_in_dim(buffer, piece, (me ^ k) // step, 0)
    return buffer


def pick(blocks, index):
    return lax.dynamic_index_in_dim(blocks, index, 0, keepdims=False)


def line_sums(chunks):
    ns = lax.axis_size("seq")
    if ns != 4:
        return [lax.psum(c, "seq") for c in chunks]
    me = lax.axis_index("seq")
    outer = (me == 0) | (me == 3)
    count = len(chunks)
    first, second, totals, sums = {}, {}, {}, [None] * count
    arrived, crossed = {}, {}
    token = None
    for step in range(count + 2):
        sends = []
        if step < count:
            sends.append(("a", step, chunks[step], [(0, 1), (3, 2)]))
        if 0 <= step - 1 < count:
            i = step - 1
            first[i] = (chunks[i].astype(F32) + arrived[i].astype(F32)).astype(BF16)
            sends.append(("b", i, first[i], [(1, 2), (2, 1)]))
        if 0 <= step - 2 < count:
            i = step - 2
            totals[i] = (first[i].astype(F32) + crossed[i].astype(F32)).astype(BF16)
            sends.append(("c", i, totals[i], [(1, 0), (2, 3)]))
        operands = [s[2] for s in sends]
        if token is not None:
            operands, _ = lax.optimization_barrier((operands, token))
        results = [lax.ppermute(o, "seq", s[3]) for o, s in zip(operands, sends)]
        token = [r[:1, :128] for r in results]
        for (kind, i, _, _), r in zip(sends, results):
            if kind == "a":
                arrived[i] = r
            elif kind == "b":
                crossed[i] = r
            else:
                sums[i] = jnp.where(outer, r, totals[i])
    return sums


def rope_tables(position, head):
    half = head // 2
    exponent = jnp.arange(half, dtype=F32) * (2.0 / head)
    frequency = ROPE_BASE ** (-exponent)
    angles = position.astype(F32)[:, None] * frequency[None, :]
    return jnp.cos(angles)[:, None, :], jnp.sin(angles)[:, None, :]


def turned(values, tables, direction):
    cosine, sine = tables
    half = values.shape[-1] // 2
    low, high = values[..., :half], values[..., half:]
    return jnp.concatenate(
        [low * cosine - direction * high * sine, high * cosine + direction * low * sine], axis=-1
    )


def norm_back(gradient, unit_rows, inverse):
    return inverse * (gradient - unit_rows * jnp.mean(gradient * unit_rows, axis=-1, keepdims=True))


def inverse_rms(values):
    return lax.rsqrt(jnp.mean(values * values, axis=-1, keepdims=True) + EPSILON)


def dot(left, right):
    return jnp.dot(left, right, preferred_element_type=F32)


def dot_nt(left, right):
    return jnp.einsum("ab,cb->ac", left, right, preferred_element_type=F32)


def dot_tn(left, right):
    return jnp.einsum("ta,tb->ab", left, right, preferred_element_type=F32)


def masked_scores(query, key, segment, index, scale):
    scores = jnp.einsum("grqd,gkd->grqk", query, key, preferred_element_type=F32) * scale
    allowed = (segment[:, :, None] == segment[:, None, :]) & (index[:, :, None] >= index[:, None, :])
    return jnp.where(allowed[:, None], scores, NEGATIVE)


def attend_forward(query, key, value, segment, index, scale):
    scores = masked_scores(query, key, segment, index, scale)
    row_max = jnp.max(scores, axis=-1, keepdims=True)
    weights = jnp.exp(scores - row_max)
    row_total = jnp.sum(weights, axis=-1, keepdims=True)
    probs = (weights / row_total).astype(BF16)
    result = jnp.einsum("grqk,gkd->grqd", probs, value, preferred_element_type=F32)
    return result.astype(BF16), row_max + jnp.log(row_total)


def attend_backward(query, key, value, grad, log_total, segment, index, scale):
    scores = masked_scores(query, key, segment, index, scale)
    probs = jnp.exp(scores - log_total)
    prob_grad = jnp.einsum("grqd,gkd->grqk", grad, value, preferred_element_type=F32)
    delta = jnp.sum(probs * prob_grad, axis=-1, keepdims=True)
    score_grad = (probs * (prob_grad - delta)).astype(BF16)
    query_grad = jnp.einsum("grqk,gkd->grqd", score_grad, key, preferred_element_type=F32) * scale
    key_grad = jnp.einsum("grqk,grqd->gkd", score_grad, query, preferred_element_type=F32) * scale
    value_grad = jnp.einsum(
        "grqk,grqd->gkd", probs.astype(BF16), grad, preferred_element_type=F32
    )
    return query_grad.astype(BF16), key_grad.astype(BF16), value_grad.astype(BF16)


def body(
    tokens,
    attention_gain,
    query_weight,
    key_projection_weight,
    value_projection_weight,
    query_gain,
    key_gain,
    output_weight,
    feed_gain,
    gate_weight,
    up_weight,
    down_weight,
    cotangent,
    seq_lengths,
    dealing,
):
    ns, nf = lax.axis_size("seq"), lax.axis_size("fsdp")
    plane, me = lax.axis_index("seq"), lax.axis_index("fsdp")
    rows, width = tokens.shape[1], tokens.shape[2]
    slots = dealing.shape[0] // nf
    head = query_gain.shape[0] * nf
    key_heads = key_projection_weight.shape[1] // head
    repeat = query_weight.shape[1] // head // key_heads
    share = nf // key_heads
    assert nf == 2 * ns and share in (1, 2) and key_heads * share == nf
    held = nf // share
    groups = 2 // share
    wide = repeat * head
    weight_rows = query_weight.shape[0]
    hidden_cols = gate_weight.shape[1] // nf
    scale = head ** (-0.5)
    pairs = relocation(ns, nf)
    back_pairs = [(b, a) for a, b in pairs]

    block_ids = jnp.arange(nf, dtype=jnp.int32)
    quarter = (block_ids // 2) ^ plane ^ (ns // 2 * (block_ids % 2))
    row_index = quarter[:, None] * rows + jnp.arange(rows, dtype=jnp.int32)[None, :]
    dealt = lax.dynamic_slice_in_dim(dealing, plane * 2 * slots, 2 * slots)
    numbers = jnp.arange(seq_lengths.shape[0], dtype=jnp.int32)
    lengths = jnp.sum(jnp.where(dealt[:, None] == numbers[None, :], seq_lengths[None, :], 0), axis=1)
    ends = jnp.cumsum(lengths.reshape(2, slots), axis=1)
    block_ends = jnp.where((block_ids % 2 == 0)[:, None], ends[0][None, :], ends[1][None, :])
    passed = row_index[:, :, None] >= block_ends[:, None, :]
    segment = jnp.sum(passed.astype(jnp.int32), axis=2)
    begin = jnp.max(jnp.where(passed, block_ends[:, None, :], 0), axis=2)
    position = row_index - begin

    def own(blocks):
        if share == 1:
            return blocks
        return pick(jnp.moveaxis(blocks.reshape((held, share) + blocks.shape[1:]), 1, 0), me % share)

    def by_group(values):
        heads = values.shape[1]
        split = values.reshape(held // groups, groups, rows, heads, -1)
        return split.transpose(1, 3, 0, 2, 4).reshape(groups, heads, -1, split.shape[-1])

    def from_group(values):
        heads = values.shape[1]
        split = values.reshape(groups, heads, held // groups, rows, -1)
        return split.transpose(2, 0, 3, 1, 4).reshape(held * rows, heads, -1)

    inputs = move(tokens[0], pairs).astype(F32)
    own_gradient = move(cotangent[0], pairs)

    small = jnp.concatenate([attention_gain, feed_gain, query_gain, key_gain])
    small = lax.all_gather(small, "fsdp", axis=0).astype(F32)
    cuts = [weight_rows, 2 * weight_rows, 2 * weight_rows + head // nf]
    gain_one, gain_two, query_norm, key_norm = (
        part.reshape(-1) for part in jnp.split(small, cuts, axis=1)
    )

    qkv_local = jnp.concatenate(
        [
            query_weight.reshape(weight_rows, key_heads, wide),
            key_projection_weight.reshape(weight_rows, key_heads, head),
            value_projection_weight.reshape(weight_rows, key_heads, head),
        ],
        axis=2,
    ).transpose(1, 0, 2)
    qkv_matrix = assembled(exchange(lambda d: pick(qkv_local, d // share))).reshape(
        width, wide + 2 * head
    )

    inverse_one = inverse_rms(inputs)
    unit_one = inputs * inverse_one
    normed_one = lax.all_gather(
        (unit_one * gain_one).astype(BF16), "fsdp", axis=0
    )
    normed_mine = own(normed_one).reshape(held * rows, width)
    mine_segment = own(segment)
    mine_index = own(row_index)
    tables = rope_tables(own(position).reshape(-1), head)

    projected = dot(normed_mine, qkv_matrix)
    query_proj = projected[:, :wide].reshape(-1, repeat, head)
    key_proj = projected[:, wide : wide + head].reshape(-1, 1, head)
    value_rows = projected[:, wide + head :].astype(BF16).reshape(-1, 1, head)
    query_inverse = inverse_rms(query_proj)
    query_unit = query_proj * query_inverse
    query_rows = turned(query_unit * query_norm, tables, 1.0).astype(BF16)
    key_inverse = inverse_rms(key_proj)
    key_unit = key_proj * key_inverse
    key_rows = turned(key_unit * key_norm, tables, 1.0).astype(BF16)

    group_segment = by_group(mine_segment.reshape(-1, 1, 1))[:, 0, :, 0]
    group_index = by_group(mine_index.reshape(-1, 1, 1))[:, 0, :, 0]
    group_query = by_group(query_rows)
    group_key = by_group(key_rows)[:, 0]
    group_value = by_group(value_rows)[:, 0]
    head_result, log_total = attend_forward(
        group_query, group_key, group_value, group_segment, group_index, scale
    )
    head_blocks = from_group(head_result).reshape(held, rows, wide)
    attended = assembled(exchange(lambda d: pick(head_blocks, d // share), share), share)
    attended = attended.transpose(1, 0, 2).reshape(rows, width)

    output_matrix = lax.all_gather(output_weight, "fsdp", axis=0, tiled=True)
    residual = inputs + dot(attended, output_matrix)

    gate_blocks = gate_weight.reshape(weight_rows, nf, hidden_cols).transpose(1, 0, 2)
    up_blocks = up_weight.reshape(weight_rows, nf, hidden_cols).transpose(1, 0, 2)
    gate_matrix = assembled(exchange(lambda d: pick(gate_blocks, d))).reshape(width, hidden_cols)
    up_matrix = assembled(exchange(lambda d: pick(up_blocks, d))).reshape(width, hidden_cols)
    out_gradient = lax.all_gather(own_gradient, "fsdp", axis=0, tiled=True)
    hidden_grad = dot_nt(out_gradient, down_weight)

    inverse_two = inverse_rms(residual)
    unit_two = residual * inverse_two
    normed_two = lax.all_gather((unit_two * gain_two).astype(BF16), "fsdp", axis=0, tiled=True)
    gate_value = dot(normed_two, gate_matrix)
    up_value = dot(normed_two, up_matrix)
    sigmoid_gate = jax.nn.sigmoid(gate_value)
    hidden = (gate_value * sigmoid_gate * up_value).astype(BF16)
    up_grad = (hidden_grad * gate_value * sigmoid_gate).astype(BF16)
    gate_grad = (
        hidden_grad * up_value * sigmoid_gate * (1.0 + gate_value * (1.0 - sigmoid_gate))
    ).astype(BF16)
    normed_two_part = dot_nt(gate_grad, gate_matrix) + dot_nt(up_grad, up_matrix)
    normed_two_grad = lax.psum_scatter(
        normed_two_part.astype(BF16), "fsdp", scatter_dimension=0, tiled=True
    ).astype(F32)
    feed_gain_part = jnp.sum(normed_two_grad * unit_two, axis=0)
    residual_grad = own_gradient.astype(F32) + norm_back(
        normed_two_grad * gain_two, unit_two, inverse_two
    )
    mixed_part = lax.psum_scatter(
        dot(hidden, down_weight).astype(BF16), "fsdp", scatter_dimension=0, tiled=True
    )
    mixed = move((residual + mixed_part.astype(F32)).astype(BF16), back_pairs)

    down_term = dot_tn(hidden, out_gradient).astype(BF16)
    gate_term = dot_tn(normed_two, gate_grad).astype(BF16).reshape(nf, weight_rows, hidden_cols)
    up_term = dot_tn(normed_two, up_grad).astype(BF16).reshape(nf, weight_rows, hidden_cols)
    gate_got = exchange(lambda d: pick(gate_term, d))
    up_got = exchange(lambda d: pick(up_term, d))

    branch_grad = residual_grad.astype(BF16)
    output_term = lax.psum_scatter(
        dot_tn(attended, branch_grad).astype(BF16), "fsdp", scatter_dimension=0, tiled=True
    )
    attended_grad = dot_nt(branch_grad, output_matrix).astype(BF16)
    attended_grad = attended_grad.reshape(rows, key_heads, wide).transpose(1, 0, 2)
    head_grad = assembled(exchange(lambda d: pick(attended_grad, d // share), share), share)
    group_grad = by_group(head_grad.reshape(held * rows, repeat, head))
    query_back, key_back, value_back = attend_backward(
        group_query, group_key, group_value, group_grad, log_total, group_segment, group_index, scale
    )
    query_turned = turned(from_group(query_back).astype(F32), tables, -1.0)
    query_norm_part = jnp.sum(query_turned * query_unit, axis=(0, 1))
    query_proj_grad = norm_back(query_turned * query_norm, query_unit, query_inverse).astype(BF16)
    key_turned = turned(from_group(key_back[:, None]).astype(F32), tables, -1.0)
    key_norm_part = jnp.sum(key_turned * key_unit, axis=(0, 1))
    key_proj_grad = norm_back(key_turned * key_norm, key_unit, key_inverse).astype(BF16)
    qkv_grad = jnp.concatenate(
        [
            query_proj_grad.reshape(-1, wide),
            key_proj_grad.reshape(-1, head),
            from_group(value_back[:, None]).reshape(-1, head),
        ],
        axis=1,
    )
    qkv_term = dot_tn(normed_mine, qkv_grad).astype(BF16).reshape(nf, weight_rows, -1)
    qkv_got = exchange(lambda d: pick(qkv_term, d))
    if share == 2:
        qkv_got = {
            k: (qkv_got[k].astype(F32) + qkv_got[k + 1].astype(F32)).astype(BF16)
            for k in range(0, nf, 2)
        }
    normed_one_part = dot_nt(qkv_grad, qkv_matrix).astype(BF16)
    if share == 2:
        normed_one_part = normed_one_part.reshape(held, 1, rows, width)
        empty = jnp.zeros_like(normed_one_part)
        mine_first = jnp.concatenate([normed_one_part, empty], axis=1)
        mine_last = jnp.concatenate([empty, normed_one_part], axis=1)
        normed_one_part = jnp.where(me % 2 == 0, mine_first, mine_last).reshape(nf * rows, width)
    normed_one_grad = lax.psum_scatter(
        normed_one_part, "fsdp", scatter_dimension=0, tiled=True
    ).astype(F32)
    attention_gain_part = jnp.sum(normed_one_grad * unit_one, axis=0)
    input_gradient = (
        residual_grad + norm_back(normed_one_grad * gain_one, unit_one, inverse_one)
    ).astype(BF16)
    input_gradient = move(input_gradient, back_pairs)

    down_pieces = 4
    down_chunks = list(down_term.reshape(down_pieces, -1, width))
    gate_keys, qkv_keys = list(gate_got), list(qkv_got)
    sums = line_sums(
        down_chunks
        + [gate_got[k] for k in gate_keys]
        + [up_got[k] for k in gate_keys]
        + [output_term]
        + [qkv_got[k] for k in qkv_keys]
    )
    down_total = jnp.concatenate(sums[:down_pieces], axis=0).astype(F32)
    sums = sums[down_pieces:]
    gate_total = assembled(dict(zip(gate_keys, sums))).transpose(1, 0, 2)
    sums = sums[nf:]
    up_total = assembled(dict(zip(gate_keys, sums))).transpose(1, 0, 2)
    sums = sums[nf:]
    output_total = sums[0].astype(F32)
    qkv_total = assembled(dict(zip(qkv_keys, sums[1:])), share).transpose(1, 0, 2).astype(F32)

    gains = lax.psum(
        jnp.concatenate([attention_gain_part, feed_gain_part, query_norm_part, key_norm_part]),
        ("seq", "fsdp"),
    )

    def owned(start, size):
        return lax.dynamic_slice_in_dim(gains, start + me * size, size)

    return (
        mixed[None],
        input_gradient[None],
        owned(0, weight_rows),
        qkv_total[:, :, :wide].reshape(weight_rows, -1),
        qkv_total[:, :, wide : wide + head].reshape(weight_rows, -1),
        qkv_total[:, :, wide + head :].reshape(weight_rows, -1),
        owned(2 * width, head // nf),
        owned(2 * width + head, head // nf),
        output_total,
        owned(width, weight_rows),
        gate_total.astype(F32).reshape(weight_rows, -1),
        up_total.astype(F32).reshape(weight_rows, -1),
        down_total,
    )


def solution(mesh):
    tokens, vector, matrix = P("fsdp", "seq", None), P("fsdp"), P("fsdp", None)
    placed = (tokens, vector, matrix, matrix, matrix, vector, vector, matrix)
    placed += (vector, matrix, matrix, matrix, tokens, P(), P())
    results = (tokens, tokens, vector, matrix, matrix, matrix, vector, vector, matrix)
    results += (vector, matrix, matrix, matrix)
    return jax.shard_map(body, mesh=mesh, in_specs=placed, out_specs=results, check_vma=False)
```

time: 1950 us -> 1430 us (0.73)
  waiting for transfers between devices: 1400 us -> 348 us
  starting transfers between devices: 22.2 us -> 380 us
  local copies, waits for them, and re-layouts: 66.8 us -> 229 us
  other arithmetic: 50.5 us -> 148 us
  matrix products: 236 us -> 197 us
  blocking collectives: 133 us -> 99.7 us
    reduce_scatter x7 -> x4, waiting for transfers between devices: 612 us -> 0.03 us  [the longest x1 0.02 us: body(): lax.psum_scatter(dot_tn(attended, branch_grad).astype(BF16), 'fsdp', scat...]
    ppermute x0 -> x147, starting transfers between devices: none -> 380 us  [the longest x87 205 us: line_sums(): results = [lax.ppermute(o, 'seq', s[3]) for o, s in zip(operands, sends)]]
    psum x1 -> x0, waiting for transfers between devices: 358 us -> none  [body(): lax.psum(query_term.astype(jnp.bfloat16), 'seq').astype(jnp.float32)]
    all_gather x7 -> x4, waiting for transfers between devices: 352 us -> 0.01 us  [the longest x1 0.01 us: body(): lax.all_gather((unit_one * gain_one).astype(BF16), 'fsdp', axis=0)]
    ppermute x0 -> x147, waiting for transfers between devices: none -> 347 us  [the longest x87 215 us: line_sums(): results = [lax.ppermute(o, 'seq', s[3]) for o, s in zip(operands, sends)]]
    all_to_all x5 -> x0, waiting for transfers between devices: 78.4 us -> none  [the longest x1 26.2 us: body(): lax.all_to_all(attended_grad, 'seq', split_axis=1, concat_axis=0, tiled=T...]
    another operation x0 -> x40, local copies, waits for them, and re-layouts: none -> 68.4 us
    all_to_all x3 -> x0, blocking collectives: 61.9 us -> none  [the longest x1 28.7 us: body(): lax.all_to_all(query_back.astype(jnp.bfloat16), 'seq', split_axis=0, conc...]
  transfers between devices with their start and end apart: 20 -> 155, of which waited for: 16 -> 61; matrix products, arithmetic and copies ran while one was open for 11% -> 34% of each run, Pallas kernels for 0% -> 0%
where the time goes in v1:
time: 1430 us; the launch traced here: 1420 us
  starting transfers between devices  380 us (27%)
  waiting for transfers between devices  348 us (24%)
  local copies, waits for them, and re-layouts  229 us (16%)
  matrix products  197 us (14%)
  other arithmetic  148 us (10%)
  blocking collectives  99.7 us (7%)
  between operations  17.6 us (1%)
    ppermute x87, waiting for transfers between devices, line_sums(): results = [lax.ppermute(o, 'seq', s[3]) for o, s in zip(operands, sends)]  215 us
    ppermute x87, starting transfers between devices, line_sums(): results = [lax.ppermute(o, 'seq', s[3]) for o, s in zip(operands, sends)]  205 us
    ppermute x56, starting transfers between devices, swap(): return lax.ppermute(values, 'fsdp', [(i, i ^ k) for i in range(n)])  152 us
    ppermute x56, waiting for transfers between devices, swap(): return lax.ppermute(values, 'fsdp', [(i, i ^ k) for i in range(n)])  132 us
    psum x1, blocking collectives, body(): lax.psum(jnp.concatenate([attention_gain_part, feed_gain_part, query_norm...  66 us
    another operation x35, local copies, waits for them, and re-layouts  61.8 us
    unnamed x228, local copies, waits for them, and re-layouts  54.2 us
    dot_general x5, matrix products, dot_nt(): return jnp.einsum('ab,cb->ac', left, right, preferred_element_type=F32)  53.4 us
  transfers between devices with their start and end apart: 155, of which 61 were waited for; matrix products, arithmetic and copies ran while one was open for 34% of the time, Pallas kernels for 0%

profile of v1, /device:TPU:0, one launch (start us, length us, event | category | flops | bytes accessed | tf_op | source)
XLA Modules:
  0.0 1419.8 jit_solution(15672962199626284085)
XLA Ops:
  7.2 9.7 collective-permute-start
  19.9 33.7 %all-reduce = bf16[4352]{0:T(1024)(128)(2,1)S(1)} all-reduce(bf16[4352]{0:T(1024)(128)(2,1)S(1)} %dynamic-update-slice), channel_id=2, replica_groups=mesh['seq'=4,'fsdp'=8] {'fsdp'}, use_global_device_ids=true, to_apply=%add | all-reduce | flops 4352 | bytes 17408
  75.2 26.3 %collective-permute-start.2 = (bf16[256,512]{1,0:T(8,128)(2,1)}, bf16[256,512]{1,0:T(8,128)(2,1)}, u32[]{:S(2)}, u32[]{:S(2)}) collective-permute-start(bf16[256,512]{1,0:T(8,128)(2,1)} %bitcast.462), channel_id=1, source_target_pairs={{0,2},{1,3},{2,0},{3,1},{4,6},{5,7},{6,4},{7,5},{8,10},{9,11},{10,... | collective-permute-start | bytes 786440 | tf_op jit(solution)/shard_map/ppermute | solution.py:28
  106.3 9.5 collective-permute-start.30
  121.6 11.2 collective-permute-start.5
  152.3 42.7 %collective-permute-start.7 = (bf16[256,512]{1,0:T(8,128)(2,1)}, bf16[256,512]{1,0:T(8,128)(2,1)S(1)}, u32[]{:S(2)}, u32[]{:S(2)}) collective-permute-start(bf16[256,512]{1,0:T(8,128)(2,1)} %bitcast.465), channel_id=1, source_target_pairs={{0,7},{1,6},{2,5},{3,4},{4,3},{5,2},{6,1},{7,0},{8,15},{9,14},{10,... | collective-permute-start | bytes 786440 | tf_op jit(solution)/shard_map/ppermute | solution.py:28
  207.8 7.6 fusion.71
  249.6 8.2 fusion.70
  257.9 8.0 fusion
  265.9 11.3 fusion.27
  388.0 14.6 %collective-permute-done.28 = bf16[256,768]{1,0:T(8,128)(2,1)S(1)} collective-permute-done((bf16[256,768]{1,0:T(8,128)(2,1)S(1)}, bf16[256,768]{1,0:T(8,128)(2,1)S(1)}, u32[]{:S(2)}, u32[]{:S(2)}) %collective-permute-start.28) | collective-permute-done | bytes 393248 | tf_op jit(solution)/shard_map/ppermute | solution.py:28
  408.5 10.9 collective-permute-done.16
  421.5 8.1 collective-permute-done.17
  431.9 7.6 collective-permute-done.20
  440.3 7.1 collective-permute-done.21
  448.2 10.8 fusion.73
  458.9 11.8 fusion.72
  470.7 14.2 multiply_convert_fusion.2
  484.9 13.9 fusion.74
  498.8 13.3 add_convert_fusion
  512.1 10.1 convolution_convert_fusion.3
  525.7 17.4 %collective-permute-done.55 = bf16[192,2048]{1,0:T(8,128)(2,1)S(1)} collective-permute-done((bf16[192,2048]{1,0:T(8,128)(2,1)S(1)}, bf16[192,2048]{1,0:T(8,128)(2,1)S(1)}, u32[]{:S(2)}, u32[]{:S(2)}) %collective-permute-start.55) | collective-permute-done | bytes 786464 | tf_op jit(solution)/shard_map/ppermute | solution.py:76
  544.1 7.8 collective-permute-start.56
  553.1 15.1 %collective-permute-done.56 = bf16[192,2048]{1,0:T(8,128)(2,1)S(1)} collective-permute-done((bf16[192,2048]{1,0:T(8,128)(2,1)S(1)}, bf16[192,2048]{1,0:T(8,128)(2,1)S(1)}, u32[]{:S(2)}, u32[]{:S(2)}) %collective-permute-start.56) | collective-permute-done | bytes 786464 | tf_op jit(solution)/shard_map/ppermute | solution.py:76
  576.8 9.6 convolution_convert_fusion.2
  601.0 9.9 convolution_convert_fusion.4
  630.0 11.7 collective-permute-start.64
  647.1 11.1 collective-permute-done.53
  685.3 12.3 collective-permute-done.51
  698.3 9.5 convolution_convert_fusion.5
  720.6 7.3 collective-permute-start.72
  767.2 8.3 collective-permute-start.76
  777.7 7.1 convolution_convert_fusion.7
  805.4 7.2 collective-permute-done.32
  813.3 8.2 collective-permute-done.33
  835.6 7.6 collective-permute-done.36
  844.1 8.9 collective-permute-done.37
  857.3 10.8 multiply_reduce_fusion
  868.1 12.1 multiply_convert_fusion
  905.3 8.9 fusion.33
  925.6 8.4 convolution_convert_fusion.1
  1105.4 7.6 collective-permute-start.94
  1113.0 8.5 convolution_convert_fusion.6
  1125.3 11.5 collective-permute-done.94
  1150.4 13.8 collective-permute-start.105
  1182.8 7.8 collective-permute-start.102
  1198.7 66.0 %psum.7 = f32[4352]{0:T(1024)S(1)} all-reduce(f32[4352]{0:T(1024)S(1)} %pad_maximum_fusion.7), channel_id=1, replica_groups=mesh['seq'=4,'fsdp'=8] {'seq','fsdp'}, use_global_device_ids=true, to_apply=%region_23.24 | all-reduce | flops 4352 | bytes 34816 | tf_op jit(solution)/shard_map/psum | solution.py:380
  1331.2 19.3 %collective-permute-done.104 = bf16[256,512]{1,0:T(8,128)(2,1)S(1)} collective-permute-done((bf16[256,512]{1,0:T(8,128)(2,1)}, bf16[256,512]{1,0:T(8,128)(2,1)S(1)}, u32[]{:S(2)}, u32[]{:S(2)}) %collective-permute-start.104) | collective-permute-done | bytes 262176 | tf_op jit(solution)/shard_map/ppermute | solution.py:76
  (785 shorter events, 777.9 us)
Async XLA Ops:
  7.2 200.6 %all-gather.13.cloned.1.call-start = ((), (), s32[]{:S(2)}) async-start(), calls=%async_computation.11 | async-start | bytes 9437184 | tf_op jit(solution)/shard_map/all_gather | solution.py:242
  7.2 46.5 %collective-permute-start = (bf16[256,2048]{1,0:T(8,128)(2,1)}, bf16[256,2048]{1,0:T(8,128)(2,1)}, u32[]{:S(2)}, u32[]{:S(2)}) collective-permute-start(bf16[256,2048]{1,0:T(8,128)(2,1)} %bitcast.485), channel_id=1, source_target_pairs={{0,0},{1,5},{2,10},{3,15},{4,20},{5,17},{6,30},{7,27},{8,2},{9,7},... | collective-permute-start | bytes 3145736 | tf_op jit(solution)/shard_map/ppermute | solution.py:23
  57.8 248.7 %all-gather.7.cloned.1.call-start = ((), (), s32[]{:S(2)}) async-start(), calls=%async_computation.4 | async-start | bytes 9437184 | tf_op jit(solution)/shard_map/all_gather | solution.py:273
  58.5 389.6 %all-gather.11.cloned.1.call-start = ((), (), s32[]{:S(2)}) async-start(), calls=%async_computation.7 | async-start | bytes 9437184 | tf_op jit(solution)/shard_map/all_gather | solution.py:280
  69.7 74.2 %collective-permute-start.1 = (bf16[256,512]{1,0:T(8,128)(2,1)}, bf16[256,512]{1,0:T(8,128)(2,1)}, u32[]{:S(2)}, u32[]{:S(2)}) collective-permute-start(bf16[256,512]{1,0:T(8,128)(2,1)} %bitcast.463), channel_id=1, source_target_pairs={{0,1},{1,0},{2,3},{3,2},{4,5},{5,4},{6,7},{7,6},{8,9},{9,8},{10,11... | collective-permute-start | bytes 786440 | tf_op jit(solution)/shard_map/ppermute | solution.py:28
  75.2 77.1 %collective-permute-start.2 = (bf16[256,512]{1,0:T(8,128)(2,1)}, bf16[256,512]{1,0:T(8,128)(2,1)}, u32[]{:S(2)}, u32[]{:S(2)}) collective-permute-start(bf16[256,512]{1,0:T(8,128)(2,1)} %bitcast.462), channel_id=1, source_target_pairs={{0,2},{1,3},{2,0},{3,1},{4,6},{5,7},{6,4},{7,5},{8,10},{9,11},{10,... | collective-permute-start | bytes 786440 | tf_op jit(solution)/shard_map/ppermute | solution.py:28
  103.3 93.4 %collective-permute-start.3 = (bf16[256,512]{1,0:T(8,128)(2,1)}, bf16[256,512]{1,0:T(8,128)(2,1)}, u32[]{:S(2)}, u32[]{:S(2)}) collective-permute-start(bf16[256,512]{1,0:T(8,128)(2,1)} %bitcast.461), channel_id=1, source_target_pairs={{0,3},{1,2},{2,1},{3,0},{4,7},{5,6},{6,5},{7,4},{8,11},{9,10},{10,... | collective-permute-start | bytes 786440 | tf_op jit(solution)/shard_map/ppermute | solution.py:28
  105.2 93.2 %collective-permute-start.4 = (bf16[256,512]{1,0:T(8,128)(2,1)}, bf16[256,512]{1,0:T(8,128)(2,1)}, u32[]{:S(2)}, u32[]{:S(2)}) collective-permute-start(bf16[256,512]{1,0:T(8,128)(2,1)} %bitcast.460), channel_id=1, source_target_pairs={{0,4},{1,5},{2,6},{3,7},{4,0},{5,1},{6,2},{7,3},{8,12},{9,13},{10,... | collective-permute-start | bytes 786440 | tf_op jit(solution)/shard_map/ppermute | solution.py:28
  121.6 78.4 %collective-permute-start.5 = (bf16[256,512]{1,0:T(8,128)(2,1)}, bf16[256,512]{1,0:T(8,128)(2,1)}, u32[]{:S(2)}, u32[]{:S(2)}) collective-permute-start(bf16[256,512]{1,0:T(8,128)(2,1)} %bitcast.464), channel_id=1, source_target_pairs={{0,5},{1,4},{2,7},{3,6},{4,1},{5,0},{6,3},{7,2},{8,13},{9,12},{10,... | collective-permute-start | bytes 786440 | tf_op jit(solution)/shard_map/ppermute | solution.py:28
  132.8 326.1 %all-gather.9.cloned.1.call-start = ((), (), s32[]{:S(2)}) async-start(), calls=%async_computation.5 | async-start | bytes 9437184 | tf_op jit(solution)/shard_map/all_gather | solution.py:285
  144.0 57.7 %collective-permute-start.6 = (bf16[256,512]{1,0:T(8,128)(2,1)}, bf16[256,512]{1,0:T(8,128)(2,1)S(1)}, u32[]{:S(2)}, u32[]{:S(2)}) collective-permute-start(bf16[256,512]{1,0:T(8,128)(2,1)} %bitcast.466), channel_id=1, source_target_pairs={{0,6},{1,7},{2,4},{3,5},{4,2},{5,3},{6,0},{7,1},{8,14},{9,15},{10,... | collective-permute-start | bytes 786440 | tf_op jit(solution)/shard_map/ppermute | solution.py:28
  152.3 54.8 %collective-permute-start.7 = (bf16[256,512]{1,0:T(8,128)(2,1)}, bf16[256,512]{1,0:T(8,128)(2,1)S(1)}, u32[]{:S(2)}, u32[]{:S(2)}) collective-permute-start(bf16[256,512]{1,0:T(8,128)(2,1)} %bitcast.465), channel_id=1, source_target_pairs={{0,7},{1,6},{2,5},{3,4},{4,3},{5,2},{6,1},{7,0},{8,15},{9,14},{10,... | collective-permute-start | bytes 786440 | tf_op jit(solution)/shard_map/ppermute | solution.py:28
  315.6 436.7 %reduce-scatter.7.cloned.1.call-start = ((), (), s32[]{:S(2)}) async-start(), calls=%async_computation.8 | async-start | bytes 9437184 | tf_op jit(solution)/shard_map/reduce_scatter | solution.py:295
  332.4 38.0 %collective-permute-start.22 = (bf16[256,768]{1,0:T(8,128)(2,1)}, bf16[256,768]{1,0:T(8,128)(2,1)}, u32[]{:S(2)}, u32[]{:S(2)}) collective-permute-start(bf16[256,768]{1,0:T(8,128)(2,1)} %bitcast.459), channel_id=1, source_target_pairs={{0,1},{1,0},{2,3},{3,2},{4,5},{5,4},{6,7},{7,6},{8,9},{9,8},{10,11... | collective-permute-start | bytes 1179656 | tf_op jit(solution)/shard_map/ppermute | solution.py:28
  334.3 39.7 %collective-permute-start.23 = (bf16[256,768]{1,0:T(8,128)(2,1)}, bf16[256,768]{1,0:T(8,128)(2,1)}, u32[]{:S(2)}, u32[]{:S(2)}) collective-permute-start(bf16[256,768]{1,0:T(8,128)(2,1)} %bitcast.458), channel_id=1, source_target_pairs={{0,2},{1,3},{2,0},{3,1},{4,6},{5,7},{6,4},{7,5},{8,10},{9,11},{10,... | collective-permute-start | bytes 1179656 | tf_op jit(solution)/shard_map/ppermute | solution.py:28
  343.3 39.4 %collective-permute-start.26 = (bf16[256,768]{1,0:T(8,128)(2,1)}, bf16[256,768]{1,0:T(8,128)(2,1)}, u32[]{:S(2)}, u32[]{:S(2)}) collective-permute-start(bf16[256,768]{1,0:T(8,128)(2,1)} %bitcast.455), channel_id=1, source_target_pairs={{0,5},{1,4},{2,7},{3,6},{4,1},{5,0},{6,3},{7,2},{8,13},{9,12},{10,... | collective-permute-start | bytes 1179656 | tf_op jit(solution)/shard_map/ppermute | solution.py:28
  379.0 40.4 %collective-permute-start.16 = (bf16[256,768]{1,0:T(8,128)(2,1)S(1)}, bf16[256,768]{1,0:T(8,128)(2,1)S(1)}, u32[]{:S(2)}, u32[]{:S(2)}) collective-permute-start(bf16[256,768]{1,0:T(8,128)(2,1)S(1)} %bitcast.451), channel_id=1, source_target_pairs={{0,2},{1,3},{2,0},{3,1},{4,6},{5,7},{6,4},{7,5},{8,10},{9,11},{10,... | collective-permute-start | bytes 1179656 | tf_op jit(solution)/shard_map/ppermute | solution.py:28
  382.7 46.9 %collective-permute-start.17 = (bf16[256,768]{1,0:T(8,128)(2,1)S(1)}, bf16[256,768]{1,0:T(8,128)(2,1)S(1)}, u32[]{:S(2)}, u32[]{:S(2)}) collective-permute-start(bf16[256,768]{1,0:T(8,128)(2,1)S(1)} %bitcast.450), channel_id=1, source_target_pairs={{0,3},{1,2},{2,1},{3,0},{4,7},{5,6},{6,5},{7,4},{8,11},{9,10},{10,... | collective-permute-start | bytes 1179656 | tf_op jit(solution)/shard_map/ppermute | solution.py:28
  385.9 44.5 %collective-permute-start.18 = (bf16[256,768]{1,0:T(8,128)(2,1)S(1)}, bf16[256,768]{1,0:T(8,128)(2,1)S(1)}, u32[]{:S(2)}, u32[]{:S(2)}) collective-permute-start(bf16[256,768]{1,0:T(8,128)(2,1)S(1)} %bitcast.449), channel_id=1, source_target_pairs={{0,4},{1,5},{2,6},{3,7},{4,0},{5,1},{6,2},{7,3},{8,12},{9,13},{10,... | collective-permute-start | bytes 1179656 | tf_op jit(solution)/shard_map/ppermute | solution.py:28
  512.1 243.5 %reduce-scatter.5.cloned.1.call-start = ((), (), s32[]{:S(2)}) async-start(), calls=%async_computation.6 | async-start | bytes 9437184 | tf_op jit(solution)/shard_map/reduce_scatter | solution.py:302
  586.5 518.2 %reduce-scatter.11.cloned.1.call-start = ((), (), s32[]{:S(2)}) async-start(), calls=%async_computation.10 | async-start | bytes 9437184 | tf_op jit(solution)/shard_map/reduce_scatter | solution.py:314
  678.6 41.2 %collective-permute-start.50 = (bf16[256,768]{1,0:T(8,128)(2,1)}, bf16[256,768]{1,0:T(8,128)(2,1)S(1)}, u32[]{:S(2)}, u32[]{:S(2)}) collective-permute-start(bf16[256,768]{1,0:T(8,128)(2,1)} %get-tuple-element.246), channel_id=1, source_target_pairs={{0,5},{1,4},{2,7},{3,6},{4,1},{5,0},{6,3},{7,2},{8,13},{9,12},{10,... | collective-permute-start | bytes 1179656 | tf_op jit(solution)/shard_map/ppermute | solution.py:28
  678.6 55.7 %collective-permute-start.49 = (bf16[256,768]{1,0:T(8,128)(2,1)}, bf16[256,768]{1,0:T(8,128)(2,1)S(1)}, u32[]{:S(2)}, u32[]{:S(2)}) collective-permute-start(bf16[256,768]{1,0:T(8,128)(2,1)} %get-tuple-element.247), channel_id=1, source_target_pairs={{0,6},{1,7},{2,4},{3,5},{4,2},{5,3},{6,0},{7,1},{8,14},{9,15},{10,... | collective-permute-start | bytes 1179656 | tf_op jit(solution)/shard_map/ppermute | solution.py:28
  680.0 40.5 %collective-permute-start.143 = (bf16[192,2048]{1,0:T(8,128)(2,1)S(1)}, bf16[192,2048]{1,0:T(8,128)(2,1)S(1)}, u32[]{:S(2)}, u32[]{:S(2)}) collective-permute-start(bf16[192,2048]{1,0:T(8,128)(2,1)S(1)} %copy-done.20), channel_id=1, source_target_pairs={{8,0},{16,24},{9,1},{17,25},{10,2},{18,26},{11,3},{19,27},{12,4},{... | collective-permute-start | bytes 2359304 | tf_op jit(solution)/shard_map/ppermute | solution.py:76
  712.1 38.8 %collective-permute-start.48 = (bf16[256,768]{1,0:T(8,128)(2,1)S(1)}, bf16[256,768]{1,0:T(8,128)(2,1)}, u32[]{:S(2)}, u32[]{:S(2)}) collective-permute-start(bf16[256,768]{1,0:T(8,128)(2,1)S(1)} %copy-done.67), channel_id=1, source_target_pairs={{0,7},{1,6},{2,5},{3,4},{4,3},{5,2},{6,1},{7,0},{8,15},{9,14},{10,... | collective-permute-start | bytes 1179656 | tf_op jit(solution)/shard_map/ppermute | solution.py:28
  728.9 224.1 %collective-permute-start.47 = (bf16[256,768]{1,0:T(8,128)(2,1)}, bf16[256,768]{1,0:T(8,128)(2,1)}, u32[]{:S(2)}, u32[]{:S(2)}) collective-permute-start(bf16[256,768]{1,0:T(8,128)(2,1)} %get-tuple-element.250), channel_id=1, source_target_pairs={{0,1},{1,0},{2,3},{3,2},{4,5},{5,4},{6,7},{7,6},{8,9},{9,8},{10,11... | collective-permute-start | bytes 1179656 | tf_op jit(solution)/shard_map/ppermute | solution.py:28
  734.2 235.6 %collective-permute-start.46 = (bf16[256,768]{1,0:T(8,128)(2,1)}, bf16[256,768]{1,0:T(8,128)(2,1)}, u32[]{:S(2)}, u32[]{:S(2)}) collective-permute-start(bf16[256,768]{1,0:T(8,128)(2,1)} %get-tuple-element.251), channel_id=1, source_target_pairs={{0,2},{1,3},{2,0},{3,1},{4,6},{5,7},{6,4},{7,5},{8,10},{9,11},{10,... | collective-permute-start | bytes 1179656 | tf_op jit(solution)/shard_map/ppermute | solution.py:28
  742.8 191.3 %collective-permute-start.145 = (bf16[192,2048]{1,0:T(8,128)(2,1)}, bf16[192,2048]{1,0:T(8,128)(2,1)}, u32[]{:S(2)}, u32[]{:S(2)}) collective-permute-start(bf16[192,2048]{1,0:T(8,128)(2,1)} %add_convert_fusion.5), channel_id=1, source_target_pairs={{8,0},{16,24},{9,1},{17,25},{10,2},{18,26},{11,3},{19,27},{12,4},{... | collective-permute-start | bytes 2359304 | tf_op jit(solution)/shard_map/ppermute | solution.py:76
  748.8 204.9 %collective-permute-start.146 = (bf16[192,2048]{1,0:T(8,128)(2,1)}, bf16[192,2048]{1,0:T(8,128)(2,1)}, u32[]{:S(2)}, u32[]{:S(2)}) collective-permute-start(bf16[192,2048]{1,0:T(8,128)(2,1)} %add_convert_fusion.4), channel_id=1, source_target_pairs={{8,0},{16,24},{9,1},{17,25},{10,2},{18,26},{11,3},{19,27},{12,4},{... | collective-permute-start | bytes 2359304 | tf_op jit(solution)/shard_map/ppermute | solution.py:76
  767.2 400.3 %reduce-scatter.9.cloned.1.call-start = ((), (), s32[]{:S(2)}) async-start(), calls=%async_computation.9 | async-start | bytes 9437184 | tf_op jit(solution)/shard_map/reduce_scatter | solution.py:352
  852.9 84.0 %collective-permute-start.127 = (bf16[256,768]{1,0:T(8,128)(2,1)}, bf16[256,768]{1,0:T(8,128)(2,1)}, u32[]{:S(2)}, u32[]{:S(2)}) collective-permute-start(bf16[256,768]{1,0:T(8,128)(2,1)} %add_convert_fusion.42), channel_id=1, source_target_pairs={{8,0},{16,24},{9,1},{17,25},{10,2},{18,26},{11,3},{19,27},{12,4},{... | collective-permute-start | bytes 1179656 | tf_op jit(solution)/shard_map/ppermute | solution.py:76
  945.2 46.5 %collective-permute-start.45 = (bf16[256,768]{1,0:T(8,128)(2,1)S(1)}, bf16[256,768]{1,0:T(8,128)(2,1)S(1)}, u32[]{:S(2)}, u32[]{:S(2)}) collective-permute-start(bf16[256,768]{1,0:T(8,128)(2,1)S(1)} %copy-done.66), channel_id=1, source_target_pairs={{0,3},{1,2},{2,1},{3,0},{4,7},{5,6},{6,5},{7,4},{8,11},{9,10},{10,... | collective-permute-start | bytes 1179656 | tf_op jit(solution)/shard_map/ppermute | solution.py:28
  952.3 59.8 %collective-permute-start.44 = (bf16[256,768]{1,0:T(8,128)(2,1)S(1)}, bf16[256,768]{1,0:T(8,128)(2,1)S(1)}, u32[]{:S(2)}, u32[]{:S(2)}) collective-permute-start(bf16[256,768]{1,0:T(8,128)(2,1)S(1)} %copy-done.65), channel_id=1, source_target_pairs={{0,4},{1,5},{2,6},{3,7},{4,0},{5,1},{6,2},{7,3},{8,12},{9,13},{10,... | collective-permute-start | bytes 1179656 | tf_op jit(solution)/shard_map/ppermute | solution.py:28
  962.0 71.0 %collective-permute-start.43 = (bf16[256,768]{1,0:T(8,128)(2,1)S(1)}, bf16[256,768]{1,0:T(8,128)(2,1)S(1)}, u32[]{:S(2)}, u32[]{:S(2)}) collective-permute-start(bf16[256,768]{1,0:T(8,128)(2,1)S(1)} %copy-done.64), channel_id=1, source_target_pairs={{0,5},{1,4},{2,7},{3,6},{4,1},{5,0},{6,3},{7,2},{8,13},{9,12},{10,... | collective-permute-start | bytes 1179656 | tf_op jit(solution)/shard_map/ppermute | solution.py:28
  991.7 62.4 %collective-permute-start.42 = (bf16[256,768]{1,0:T(8,128)(2,1)S(1)}, bf16[256,768]{1,0:T(8,128)(2,1)}, u32[]{:S(2)}, u32[]{:S(2)}) collective-permute-start(bf16[256,768]{1,0:T(8,128)(2,1)S(1)} %copy-done.63), channel_id=1, source_target_pairs={{0,6},{1,7},{2,4},{3,5},{4,2},{5,3},{6,0},{7,1},{8,14},{9,15},{10,... | collective-permute-start | bytes 1179656 | tf_op jit(solution)/shard_map/ppermute | solution.py:28
  1012.2 76.4 %collective-permute-start.41 = (bf16[256,768]{1,0:T(8,128)(2,1)}, bf16[256,768]{1,0:T(8,128)(2,1)}, u32[]{:S(2)}, u32[]{:S(2)}) collective-permute-start(bf16[256,768]{1,0:T(8,128)(2,1)} %get-tuple-element.256), channel_id=1, source_target_pairs={{0,7},{1,6},{2,5},{3,4},{4,3},{5,2},{6,1},{7,0},{8,15},{9,14},{10,... | collective-permute-start | bytes 1179656 | tf_op jit(solution)/shard_map/ppermute | solution.py:28
  1038.2 42.3 %collective-permute-start.135 = (bf16[256,768]{1,0:T(8,128)(2,1)}, bf16[256,768]{1,0:T(8,128)(2,1)}, u32[]{:S(2)}, u32[]{:S(2)}) collective-permute-start(bf16[256,768]{1,0:T(8,128)(2,1)} %add_convert_fusion.26), channel_id=1, source_target_pairs={{8,0},{16,24},{9,1},{17,25},{10,2},{18,26},{11,3},{19,27},{12,4},{... | collective-permute-start | bytes 1179656 | tf_op jit(solution)/shard_map/ppermute | solution.py:76
  1090.2 47.8 %collective-permute-start.138 = (bf16[256,768]{1,0:T(8,128)(2,1)S(1)}, bf16[256,768]{1,0:T(8,128)(2,1)}, u32[]{:S(2)}, u32[]{:S(2)}) collective-permute-start(bf16[256,768]{1,0:T(8,128)(2,1)S(1)} %add_convert_fusion.20), channel_id=1, source_target_pairs={{8,0},{16,24},{9,1},{17,25},{10,2},{18,26},{11,3},{19,27},{12,4},{... | collective-permute-start | bytes 1179656 | tf_op jit(solution)/shard_map/ppermute | solution.py:76
  1098.9 40.9 %collective-permute-start.139 = (bf16[256,768]{1,0:T(8,128)(2,1)}, bf16[256,768]{1,0:T(8,128)(2,1)}, u32[]{:S(2)}, u32[]{:S(2)}) collective-permute-start(bf16[256,768]{1,0:T(8,128)(2,1)} %add_convert_fusion.18), channel_id=1, source_target_pairs={{8,0},{16,24},{9,1},{17,25},{10,2},{18,26},{11,3},{19,27},{12,4},{... | collective-permute-start | bytes 1179656 | tf_op jit(solution)/shard_map/ppermute | solution.py:76
  1100.2 45.9 %collective-permute-start.140 = (bf16[256,768]{1,0:T(8,128)(2,1)}, bf16[256,768]{1,0:T(8,128)(2,1)}, u32[]{:S(2)}, u32[]{:S(2)}) collective-permute-start(bf16[256,768]{1,0:T(8,128)(2,1)} %add_convert_fusion.16), channel_id=1, source_target_pairs={{8,0},{16,24},{9,1},{17,25},{10,2},{18,26},{11,3},{19,27},{12,4},{... | collective-permute-start | bytes 1179656 | tf_op jit(solution)/shard_map/ppermute | solution.py:76
  1149.9 47.4 %collective-permute-start.101 = (bf16[256,512]{1,0:T(8,128)(2,1)}, bf16[256,512]{1,0:T(8,128)(2,1)}, u32[]{:S(2)}, u32[]{:S(2)}) collective-permute-start(bf16[256,512]{1,0:T(8,128)(2,1)} %get-tuple-element.281), channel_id=1, source_target_pairs={{0,3},{1,2},{2,1},{3,0},{4,7},{5,6},{6,5},{7,4},{8,11},{9,10},{10,... | collective-permute-start | bytes 786440 | tf_op jit(solution)/shard_map/ppermute | solution.py:28
  1150.4 124.2 %collective-permute-start.105 = (bf16[256,512]{1,0:T(8,128)(2,1)}, bf16[256,512]{1,0:T(8,128)(2,1)}, u32[]{:S(2)}, u32[]{:S(2)}) collective-permute-start(bf16[256,512]{1,0:T(8,128)(2,1)} %get-tuple-element.280), channel_id=1, source_target_pairs={{0,4},{1,5},{2,6},{3,7},{4,0},{5,1},{6,2},{7,3},{8,12},{9,13},{10,... | collective-permute-start | bytes 786440 | tf_op jit(solution)/shard_map/ppermute | solution.py:28
  1175.0 120.5 %collective-permute-start.109 = (bf16[256,512]{1,0:T(8,128)(2,1)}, bf16[256,512]{1,0:T(8,128)(2,1)}, u32[]{:S(2)}, u32[]{:S(2)}) collective-permute-start(bf16[256,512]{1,0:T(8,128)(2,1)} %get-tuple-element.279), channel_id=1, source_target_pairs={{0,5},{1,4},{2,7},{3,6},{4,1},{5,0},{6,3},{7,2},{8,13},{9,12},{10,... | collective-permute-start | bytes 786440 | tf_op jit(solution)/shard_map/ppermute | solution.py:28
  1193.5 89.7 %collective-permute-start.38 = (bf16[256,2048]{1,0:T(8,128)(2,1)}, bf16[256,2048]{1,0:T(8,128)(2,1)S(1)}, u32[]{:S(2)}, u32[]{:S(2)}) collective-permute-start(bf16[256,2048]{1,0:T(8,128)(2,1)} %fusion.15), channel_id=1, source_target_pairs={{0,0},{5,1},{10,2},{15,3},{20,4},{17,5},{30,6},{27,7},{2,8},{7,9},... | collective-permute-start | bytes 3145736 | tf_op jit(solution)/shard_map/ppermute | solution.py:23
  1197.3 70.4 %collective-permute-start.107 = (bf16[256,512]{1,0:T(8,128)(2,1)S(1)}, bf16[256,512]{1,0:T(8,128)(2,1)}, u32[]{:S(2)}, u32[]{:S(2)}) collective-permute-start(bf16[256,512]{1,0:T(8,128)(2,1)S(1)} %add_convert_fusion.57), channel_id=1, source_target_pairs={{8,16},{16,8},{9,17},{17,9},{10,18},{18,10},{11,19},{19,11},{12,20... | collective-permute-start | bytes 786440 | tf_op jit(solution)/shard_map/ppermute | solution.py:76
  1274.6 56.0 %collective-permute-start.113 = (bf16[256,512]{1,0:T(8,128)(2,1)}, bf16[256,512]{1,0:T(8,128)(2,1)}, u32[]{:S(2)}, u32[]{:S(2)}) collective-permute-start(bf16[256,512]{1,0:T(8,128)(2,1)} %get-tuple-element.278), channel_id=1, source_target_pairs={{0,6},{1,7},{2,4},{3,5},{4,2},{5,3},{6,0},{7,1},{8,14},{9,15},{10,... | collective-permute-start | bytes 786440 | tf_op jit(solution)/shard_map/ppermute | solution.py:28
  1283.2 79.7 %collective-permute-start.117 = (bf16[256,512]{1,0:T(8,128)(2,1)}, bf16[256,512]{1,0:T(8,128)(2,1)}, u32[]{:S(2)}, u32[]{:S(2)}) collective-permute-start(bf16[256,512]{1,0:T(8,128)(2,1)} %get-tuple-element.277), channel_id=1, source_target_pairs={{0,7},{1,6},{2,5},{3,4},{4,3},{5,2},{6,1},{7,0},{8,15},{9,14},{10,... | collective-permute-start | bytes 786440 | tf_op jit(solution)/shard_map/ppermute | solution.py:28
  1315.2 54.5 %collective-permute-start.126 = (bf16[256,2048]{1,0:T(8,128)(2,1)S(1)}, bf16[256,2048]{1,0:T(8,128)(2,1)S(1)}, u32[]{:S(2)}, u32[]{:S(2)}) collective-permute-start(bf16[256,2048]{1,0:T(8,128)(2,1)S(1)} %add_convert_fusion.1), channel_id=1, source_target_pairs={{8,0},{16,24},{9,1},{17,25},{10,2},{18,26},{11,3},{19,27},{12,4},{... | collective-permute-start | bytes 3145736 | tf_op jit(solution)/shard_map/ppermute | solution.py:76
  (210 other events, 3978.5 us)
Sparse Core Ops, SparseCore 0:
  57.9 148.6 all-gather.12
  208.5 61.6 all-gather.6
  272.0 64.5 all-gather.10
  339.0 94.0 all-gather.8
  512.2 71.5 reduce-scatter.6
  587.1 75.6 reduce-scatter.4
  767.3 86.5 reduce-scatter.10
  934.2 96.2 reduce-scatter.8

commit v2 on v1

v2 whole, which is shorter than its diff:
```python
import functools

import jax
import jax.numpy as jnp
from jax import lax
from jax.experimental import pallas as pl
from jax.experimental.pallas import tpu as pltpu
from jax.sharding import PartitionSpec as P

EPSILON = 1e-06
ROPE_BASE = 1000000.0
NEGATIVE = -1e30
F32 = jnp.float32
BF16 = jnp.bfloat16


def relocation(ns, nf):
    pairs = []
    for s in range(ns):
        for g in range(nf):
            p, c = divmod(g, 2)
            pairs.append((s * nf + g, p * nf + 2 * (p ^ s ^ (ns // 2 * c)) + c))
    return pairs


def block_of(group, quarter, plane, ns):
    return 2 * (quarter ^ plane ^ (ns // 2 * group)) + group


def move(values, pairs):
    return lax.ppermute(values, ("seq", "fsdp"), pairs)


def pick(blocks, index):
    return lax.dynamic_index_in_dim(blocks, index, 0, keepdims=False)


def after(value, *others):
    return lax.optimization_barrier((value, others))[0]


def head_swap(values, share):
    nf = lax.axis_size("fsdp")
    among = None
    if share > 1:
        among = [[d for d in range(nf) if d % share == j] for j in range(share)]
    return lax.all_to_all(values, "fsdp", 0, 0, axis_index_groups=among, tiled=True)


def spread(values):
    return lax.all_to_all(values, "fsdp", 0, 0, tiled=True)


def line_sums(chunks):
    ns = lax.axis_size("seq")
    if ns != 4:
        return [lax.psum(c, "seq") for c in chunks]
    me = lax.axis_index("seq")
    outer = (me == 0) | (me == 3)
    inward, outward = [(0, 1), (3, 2)], [(1, 0), (2, 3)]
    count = len(chunks)
    part, total, sums = {}, {}, [None] * count
    token = None
    for step in range(count + 2):
        sends = []
        new = chunks[step] if step < count else None
        old = total[step - 2] if step >= 2 else None
        if new is not None and old is not None and new.shape == old.shape:
            sends.append((jnp.where(outer, new, old), inward + outward, ("in", "out")))
        else:
            if new is not None:
                sends.append((new, inward, ("in",)))
            if old is not None:
                sends.append((old, outward, ("out",)))
        if 1 <= step <= count:
            sends.append((part[step - 1], [(1, 2), (2, 1)], ("across",)))
        operands = [send[0] for send in sends]
        if token is not None:
            operands, _ = lax.optimization_barrier((operands, token))
        token = []
        for operand, (_, pairs, roles) in zip(operands, sends):
            got = lax.ppermute(operand, "seq", pairs)
            token.append(got)
            if "in" in roles:
                part[step] = add_rounded(new, got)
            if "out" in roles:
                sums[step - 2] = (got, old)
            if "across" in roles:
                total[step - 1] = add_rounded(part[step - 1], got)
    return [jnp.where(outer, got, mine) for got, mine in sums]


def add_rounded(left, right):
    return (left.astype(F32) + right.astype(F32)).astype(BF16)


def dot(left, right):
    return jnp.dot(left, right, preferred_element_type=F32)


def dot_nt(left, right):
    return lax.dot_general(left, right, (((1,), (1,)), ((), ())), preferred_element_type=F32)


def dot_tn(left, right):
    return lax.dot_general(left, right, (((0,), (0,)), ((), ())), preferred_element_type=F32)


def norm_back(gradient, unit_rows, inverse):
    return inverse * (gradient - unit_rows * jnp.mean(gradient * unit_rows, axis=-1, keepdims=True))


def inverse_rms(values):
    return lax.rsqrt(jnp.mean(values * values, axis=-1, keepdims=True) + EPSILON)


def rope_tables(position, head):
    half = head // 2
    exponent = jnp.arange(half, dtype=F32) * (2.0 / head)
    angles = position.astype(F32)[:, None] * (ROPE_BASE ** (-exponent))[None, :]
    cosine, sine = jnp.cos(angles), jnp.sin(angles)
    return jnp.concatenate([cosine, cosine], axis=1), jnp.concatenate([-sine, sine], axis=1)


def half_turn(values):
    return pltpu.roll(values, values.shape[1] // 2, 1)


def column(values, part, head):
    return values[:, part * head : (part + 1) * head]


def allowed_keys(begin, i, j, rows):
    shape = (begin.shape[0], rows)
    key_index = j * rows + lax.broadcasted_iota(jnp.int32, shape, 1)
    row = lax.broadcasted_iota(jnp.int32, (rows, 1), 0)
    query_index = i * rows + jnp.concatenate([row] * (begin.shape[0] // rows), axis=0)
    return (key_index >= begin) & (key_index <= query_index)


def attend_kernel(
    repeat, scale, lead_ref, x_ref, w_ref, qg_ref, kg_ref, cos_ref, sin_ref, begin_ref,
    proj_ref, qkv_ref, out_ref, key_all, value_all, score_all,
):
    rows, head = cos_ref.shape
    i, ns = pl.program_id(1), pl.num_programs(1)
    low = lead_ref[2 + pl.program_id(0) * ns + i]
    proj = dot(x_ref[...], w_ref[...])
    cosine, sine = cos_ref[...], sin_ref[...]

    def turned(part, gain):
        values = column(proj, part, head)
        normed = values * inverse_rms(values) * gain
        return (normed * cosine + half_turn(normed) * sine).astype(BF16)

    queries = [turned(part, qg_ref[...]) for part in range(repeat)]
    key = turned(repeat, kg_ref[...])
    value = column(proj, repeat + 1, head).astype(BF16)
    proj_ref[...] = proj[:, : (repeat + 1) * head]
    qkv_ref[...] = jnp.concatenate(queries + [key, value], axis=1)
    own = pl.ds(pl.multiple_of(i * rows, rows), rows)
    key_all[own, :] = key
    value_all[own, :] = value
    query = jnp.concatenate(queries, axis=0)
    begin = jnp.concatenate([begin_ref[...]] * repeat, axis=0)

    def score(j, top):
        keys = key_all[pl.ds(pl.multiple_of(j * rows, rows), rows), :]
        scores = jnp.where(allowed_keys(begin, i, j, rows), dot_nt(query, keys) * scale, NEGATIVE)
        score_all[j] = scores
        return jnp.maximum(top, jnp.max(scores, axis=1, keepdims=True))

    top = lax.fori_loop(low, i + 1, score, jnp.full((repeat * rows, 1), NEGATIVE, F32))

    def gather(j, carry):
        total, result = carry
        weights = jnp.exp(score_all[j] - top)
        values = value_all[pl.ds(pl.multiple_of(j * rows, rows), rows), :]
        total = total + jnp.sum(weights, axis=1, keepdims=True)
        return total, result + dot(weights.astype(BF16), values)

    start = (jnp.zeros((repeat * rows, 1), F32), jnp.zeros((repeat * rows, head), F32))
    total, result = lax.fori_loop(low, i + 1, gather, start)
    result = (result / total).astype(BF16)
    out_ref[...] = jnp.concatenate(
        [result[part * rows : (part + 1) * rows] for part in range(repeat)], axis=1
    )


def attend_back_kernel(
    repeat, scale, share, lead_ref, grad_ref, qkv_ref, proj_ref, w_ref, qg_ref, kg_ref, cos_ref,
    sin_ref, begin_ref, dqkv_ref, part_ref, gain_ref, score_all, prob_all, key_sum, value_sum,
):
    rows, head = cos_ref.shape
    c, ns = pl.program_id(0), pl.num_programs(1)
    i = ns - 1 - pl.program_id(1)
    low = lead_ref[2 + c * ns + i]
    cosine, sine = cos_ref[...], sin_ref[...]

    @pl.when(pl.program_id(1) == 0)
    def _():
        key_sum[...] = jnp.zeros_like(key_sum)
        value_sum[...] = jnp.zeros_like(value_sum)

    @pl.when((pl.program_id(1) == 0) & (c == 0))
    def _():
        gain_ref[...] = jnp.zeros_like(gain_ref)

    def block(j, part):
        slot = block_of(c + lead_ref[1], j, lead_ref[0], ns) // share
        place = pl.ds(pl.multiple_of(slot * rows, rows), rows)
        return qkv_ref[place, part * head : (part + 1) * head]

    query = jnp.concatenate([block(i, part) for part in range(repeat)], axis=0)
    grad = jnp.concatenate([column(grad_ref, part, head) for part in range(repeat)], axis=0)
    begin = jnp.concatenate([begin_ref[...]] * repeat, axis=0)

    def score(j, top):
        scores = dot_nt(query, block(j, repeat)) * scale
        scores = jnp.where(allowed_keys(begin, i, j, rows), scores, NEGATIVE)
        score_all[j] = scores
        prob_all[j] = dot_nt(grad, block(j, repeat + 1))
        return jnp.maximum(top, jnp.max(scores, axis=1, keepdims=True))

    top = lax.fori_loop(low, i + 1, score, jnp.full((repeat * rows, 1), NEGATIVE, F32))

    def weigh(j, carry):
        total, delta = carry
        weights = jnp.exp(score_all[j] - top)
        score_all[j] = weights
        total = total + jnp.sum(weights, axis=1, keepdims=True)
        return total, delta + jnp.sum(weights * prob_all[j], axis=1, keepdims=True)

    zero = jnp.zeros((repeat * rows, 1), F32)
    total, delta = lax.fori_loop(low, i + 1, weigh, (zero, zero))
    inverse_total = 1.0 / total
    delta = delta * inverse_total

    def back(j, query_sum):
        place = pl.ds(pl.multiple_of(j * rows, rows), rows)
        probs = score_all[j] * inverse_total
        score_grad = (probs * (prob_all[j] - delta)).astype(BF16)
        key_sum[place, :] += dot_tn(score_grad, query)
        value_sum[place, :] += dot_tn(probs.astype(BF16), grad)
        return query_sum + dot(score_grad, block(j, repeat))

    query_grad = lax.fori_loop(low, i + 1, back, jnp.zeros((repeat * rows, head), F32)) * scale
    own = pl.ds(pl.multiple_of(i * rows, rows), rows)
    key_grad = key_sum[own, :] * scale

    def unturned(gradient, part, gain):
        values = column(proj_ref, part, head)
        inverse = inverse_rms(values)
        unit = values * inverse
        turned = gradient * cosine - half_turn(gradient) * sine
        gained = jnp.sum(turned * unit, axis=0, keepdims=True)
        return norm_back(turned * gain, unit, inverse).astype(BF16), gained

    pieces, query_gained = [], 0.0
    for part in range(repeat):
        piece, gained = unturned(
            query_grad[part * rows : (part + 1) * rows], part, qg_ref[...]
        )
        pieces.append(piece)
        query_gained = query_gained + gained
    piece, key_gained = unturned(key_grad, repeat, kg_ref[...])
    gain_ref[0:1, :] += query_gained
    gain_ref[1:2, :] += key_gained
    dqkv = jnp.concatenate(pieces + [piece, value_sum[own, :].astype(BF16)], axis=1)
    dqkv_ref[...] = dqkv
    part_ref[...] = dot_nt(dqkv, w_ref[...]).astype(BF16)


def attention_calls(ns, share, rows, width, repeat, head, scale):
    groups, held = 2 // share, 2 * ns // share
    columns = (repeat + 2) * head
    span = ns * rows

    def inside(flip, divide):
        def index(c, t, lead):
            quarter = ns - 1 - t if flip else t
            return block_of(c + lead[1], quarter, lead[0], ns) // divide, 0

        return index

    def whole(shape):
        return pl.BlockSpec(shape, lambda c, t, lead: (0, 0))

    def specs(flip):
        held_block = lambda size: pl.BlockSpec((rows, size), inside(flip, share))
        common = [whole((1, head)), whole((1, head)), held_block(head), held_block(head), held_block(1)]
        return held_block, common

    scores = pltpu.VMEM((ns, repeat * rows, rows), F32)
    held_block, common = specs(False)
    flops = 2 * held * rows * width * columns
    forward = pl.pallas_call(
        functools.partial(attend_kernel, repeat, scale),
        grid_spec=pltpu.PrefetchScalarGridSpec(
            num_scalar_prefetch=1,
            grid=(groups, ns),
            in_specs=[pl.BlockSpec((rows, width), inside(False, 1)), whole((width, columns))] + common,
            out_specs=[held_block((repeat + 1) * head), held_block(columns), held_block(repeat * head)],
            scratch_shapes=[pltpu.VMEM((span, head), BF16), pltpu.VMEM((span, head), BF16), scores],
        ),
        out_shape=[
            jax.ShapeDtypeStruct((held * rows, (repeat + 1) * head), F32),
            jax.ShapeDtypeStruct((held * rows, columns), BF16),
            jax.ShapeDtypeStruct((held * rows, repeat * head), BF16),
        ],
        cost_estimate=pl.CostEstimate(flops=2 * flops, bytes_accessed=20 << 20, transcendentals=4 << 20),
        name="attend",
    )
    held_block, common = specs(True)
    backward = pl.pallas_call(
        functools.partial(attend_back_kernel, repeat, scale, share),
        grid_spec=pltpu.PrefetchScalarGridSpec(
            num_scalar_prefetch=1,
            grid=(groups, ns),
            in_specs=[
                held_block(repeat * head),
                whole((held * rows, columns)),
                held_block((repeat + 1) * head),
                whole((width, columns)),
            ]
            + common,
            out_specs=[held_block(columns), held_block(width), whole((8, head))],
            scratch_shapes=[scores, scores, pltpu.VMEM((span, head), F32), pltpu.VMEM((span, head), F32)],
        ),
        out_shape=[
            jax.ShapeDtypeStruct((held * rows, columns), BF16),
            jax.ShapeDtypeStruct((held * rows, width), BF16),
            jax.ShapeDtypeStruct((8, head), F32),
        ],
        cost_estimate=pl.CostEstimate(flops=4 * flops, bytes_accessed=30 << 20, transcendentals=4 << 20),
        name="attend_back",
    )
    return forward, backward


def body(
    tokens,
    attention_gain,
    query_weight,
    key_projection_weight,
    value_projection_weight,
    query_gain,
    key_gain,
    output_weight,
    feed_gain,
    gate_weight,
    up_weight,
    down_weight,
    cotangent,
    seq_lengths,
    dealing,
):
    ns, nf = lax.axis_size("seq"), lax.axis_size("fsdp")
    plane, me = lax.axis_index("seq"), lax.axis_index("fsdp")
    rows, width = tokens.shape[1], tokens.shape[2]
    slots = dealing.shape[0] // nf
    head = query_gain.shape[0] * nf
    key_heads = key_projection_weight.shape[1] // head
    repeat = query_weight.shape[1] // head // key_heads
    share = nf // key_heads
    assert nf == 2 * ns and share in (1, 2) and key_heads * share == nf
    held = nf // share
    wide = repeat * head
    columns = wide + 2 * head
    weight_rows = query_weight.shape[0]
    hidden_cols = gate_weight.shape[1] // nf
    pairs = relocation(ns, nf)
    back_pairs = [(b, a) for a, b in pairs]
    attend, attend_back = attention_calls(ns, share, rows, width, repeat, head, head ** (-0.5))

    inputs = move(tokens[0], pairs).astype(F32)
    own_gradient = move(after(cotangent[0], inputs[:8, :128]), pairs)

    gains = jnp.concatenate([attention_gain, feed_gain, query_gain, key_gain])
    gains = jnp.pad(gains, (0, -gains.shape[0] % 128))
    gains = lax.all_gather(gains, "fsdp", axis=0, tiled=True).reshape(nf, -1).astype(F32)
    cuts = [weight_rows, 2 * weight_rows, 2 * weight_rows + head // nf, 2 * weight_rows + 2 * head // nf]
    gain_one, gain_two, query_norm, key_norm = (
        part.reshape(1, -1) for part in jnp.split(gains, cuts, axis=1)[:4]
    )

    qkv_local = jnp.concatenate(
        [
            query_weight.reshape(weight_rows, key_heads, wide),
            key_projection_weight.reshape(weight_rows, key_heads, head),
            value_projection_weight.reshape(weight_rows, key_heads, head),
        ],
        axis=2,
    ).transpose(1, 0, 2)
    qkv_matrix = spread(jnp.repeat(qkv_local, share, axis=0)).reshape(width, columns)
    output_matrix = lax.all_gather(output_weight, "fsdp", axis=0, tiled=True)

    block_ids = jnp.arange(nf, dtype=jnp.int32)
    if share == 2:
        block_ids = 2 * jnp.arange(held, dtype=jnp.int32) + me % 2
    parity = block_ids % 2
    quarter = (block_ids // 2) ^ plane ^ (ns // 2 * parity)
    row_index = quarter[:, None] * rows + jnp.arange(rows, dtype=jnp.int32)[None, :]
    dealt = lax.dynamic_slice_in_dim(dealing, plane * 2 * slots, 2 * slots)
    numbers = jnp.arange(seq_lengths.shape[0], dtype=jnp.int32)
    lengths = jnp.sum(jnp.where(dealt[:, None] == numbers[None, :], seq_lengths[None, :], 0), axis=1)
    ends = jnp.cumsum(lengths.reshape(2, slots), axis=1)

    def begins(index, group_ends):
        passed = index[:, :, None] >= group_ends[:, None, :]
        return jnp.max(jnp.where(passed, group_ends[:, None, :], 0), axis=2)

    begin = begins(row_index, jnp.where((parity == 0)[:, None], ends[0][None, :], ends[1][None, :]))
    cosine, sine = rope_tables((row_index - begin).reshape(-1), head)
    begin = begin.reshape(-1, 1)
    firsts = jnp.broadcast_to(jnp.arange(ns, dtype=jnp.int32)[None, :] * rows, (2, ns))
    lows = begins(firsts, ends) // rows
    first_group = me % 2 if share == 2 else jnp.zeros((), jnp.int32)
    if share == 2:
        lows = pick(lows, first_group)
    lead = jnp.concatenate([plane[None], first_group[None], lows.reshape(-1)]).astype(jnp.int32)

    inverse_one = inverse_rms(inputs)
    unit_one = inputs * inverse_one
    normed_one = lax.all_gather((unit_one * gain_one).astype(BF16), "fsdp", axis=0, tiled=True)

    proj, qkv, head_result = attend(
        lead, normed_one, qkv_matrix, query_norm, key_norm, cosine, sine, begin
    )
    attended = head_swap(head_result.reshape(held, rows, wide), share)
    attended = attended.transpose(1, 0, 2).reshape(rows, key_heads * wide)
    residual = inputs + dot(attended, output_matrix)

    inner_local = jnp.concatenate(
        [
            gate_weight.reshape(weight_rows, nf, hidden_cols),
            up_weight.reshape(weight_rows, nf, hidden_cols),
        ],
        axis=2,
    ).transpose(1, 0, 2)
    inner_matrix = spread(after(inner_local, normed_one[:8, :128])).reshape(width, 2 * hidden_cols)
    out_gradient = lax.all_gather(
        after(own_gradient, normed_one[:8, :128]), "fsdp", axis=0, tiled=True
    )
    hidden_grad = dot_nt(out_gradient, down_weight)

    inverse_two = inverse_rms(residual)
    unit_two = residual * inverse_two
    normed_two = lax.all_gather((unit_two * gain_two).astype(BF16), "fsdp", axis=0, tiled=True)
    inner = dot(normed_two, inner_matrix)
    gate_value, up_value = inner[:, :hidden_cols], inner[:, hidden_cols:]
    sigmoid_gate = jax.nn.sigmoid(gate_value)
    hidden = (gate_value * sigmoid_gate * up_value).astype(BF16)
    up_grad = (hidden_grad * gate_value * sigmoid_gate).astype(BF16)
    gate_grad = (
        hidden_grad * up_value * sigmoid_gate * (1.0 + gate_value * (1.0 - sigmoid_gate))
    ).astype(BF16)
    inner_grad = jnp.concatenate([gate_grad, up_grad], axis=1)
    normed_two_part = dot_nt(inner_grad, inner_matrix).astype(BF16)
    normed_two_grad = lax.psum_scatter(
        normed_two_part, "fsdp", scatter_dimension=0, tiled=True
    ).astype(F32)
    feed_gain_part = jnp.sum(normed_two_grad * unit_two, axis=0)
    residual_grad = own_gradient.astype(F32) + norm_back(
        normed_two_grad * gain_two, unit_two, inverse_two
    )

    down_term = dot_tn(after(hidden, normed_two_part[:8, :128]), out_gradient).astype(BF16)
    inner_term = dot_tn(after(normed_two, down_term[:8, :128]), inner_grad).astype(BF16)
    inner_got = spread(inner_term.reshape(nf, weight_rows, 2 * hidden_cols))
    mixed_part = dot(after(hidden, inner_term[:8, :128]), down_weight).astype(BF16)

    branch_grad = residual_grad.astype(BF16)
    attended_grad = dot_nt(branch_grad, output_matrix).astype(BF16)
    attended_grad = attended_grad.reshape(rows, key_heads, wide).transpose(1, 0, 2)
    head_grad = head_swap(attended_grad, share).reshape(held * rows, wide)
    output_term = lax.psum_scatter(
        dot_tn(attended, branch_grad).astype(BF16), "fsdp", scatter_dimension=0, tiled=True
    )
    qkv_grad, normed_one_part, norm_parts = attend_back(
        lead, head_grad, qkv, proj, qkv_matrix, query_norm, key_norm, cosine, sine, begin
    )
    normed_mine = normed_one
    if share == 2:
        normed_mine = pick(
            normed_one.reshape(held, 2, rows, width).transpose(1, 0, 2, 3), first_group
        ).reshape(held * rows, width)
        normed_one_part = normed_one_part.reshape(held, 1, rows, width)
        empty = jnp.zeros_like(normed_one_part)
        mine_first = jnp.concatenate([normed_one_part, empty], axis=1)
        mine_last = jnp.concatenate([empty, normed_one_part], axis=1)
        normed_one_part = jnp.where(me % 2 == 0, mine_first, mine_last).reshape(nf * rows, width)
    normed_one_grad = lax.psum_scatter(
        normed_one_part, "fsdp", scatter_dimension=0, tiled=True
    ).astype(F32)
    qkv_term = dot_tn(normed_mine, qkv_grad).astype(BF16)
    qkv_got = spread(qkv_term.reshape(nf, weight_rows, columns))
    if share == 2:
        qkv_got = qkv_got.astype(F32).reshape(key_heads, 2, weight_rows, columns)
        qkv_got = jnp.sum(qkv_got, axis=1).astype(BF16)
    attention_gain_part = jnp.sum(normed_one_grad * unit_one, axis=0)
    input_gradient = (
        residual_grad + norm_back(normed_one_grad * gain_one, unit_one, inverse_one)
    ).astype(BF16)
    input_gradient = move(input_gradient, back_pairs)
    mixed_part = lax.psum_scatter(
        after(mixed_part, normed_one_grad[:8, :128]), "fsdp", scatter_dimension=0, tiled=True
    )
    mixed = move((residual + mixed_part.astype(F32)).astype(BF16), back_pairs)

    down_pieces, inner_pieces, qkv_pieces = 2, 4, 2
    sums = line_sums(
        list(down_term.reshape(down_pieces, -1, width))
        + list(inner_got.reshape(inner_pieces, -1, 2 * hidden_cols))
        + [output_term]
        + list(qkv_got.reshape(qkv_pieces, -1, columns))
    )
    down_total = jnp.concatenate(sums[:down_pieces], axis=0).astype(F32)
    sums = sums[down_pieces:]
    inner_total = jnp.concatenate(sums[:inner_pieces], axis=0).reshape(nf, weight_rows, -1)
    inner_total = inner_total.transpose(1, 0, 2).astype(F32)
    sums = sums[inner_pieces:]
    output_total = sums[0].astype(F32)
    qkv_total = jnp.concatenate(sums[1:], axis=0).reshape(key_heads, weight_rows, columns)
    qkv_total = qkv_total.transpose(1, 0, 2).astype(F32)

    parts = jnp.concatenate(
        [attention_gain_part, feed_gain_part, norm_parts[0], norm_parts[1]]
    ).reshape(-1, 128)
    parts = lax.all_gather(parts, ("seq", "fsdp"), axis=0)
    gain_sums = jnp.sum(parts, axis=0).reshape(-1)

    def owned(start, size):
        return lax.dynamic_slice_in_dim(gain_sums, start + me * size, size)

    return (
        mixed[None],
        input_gradient[None],
        owned(0, weight_rows),
        qkv_total[:, :, :wide].reshape(weight_rows, -1),
        qkv_total[:, :, wide : wide + head].reshape(weight_rows, -1),
        qkv_total[:, :, wide + head :].reshape(weight_rows, -1),
        owned(2 * width, head // nf),
        owned(2 * width + head, head // nf),
        output_total,
        owned(width, weight_rows),
        inner_total[:, :, :hidden_cols].reshape(weight_rows, -1),
        inner_total[:, :, hidden_cols:].reshape(weight_rows, -1),
        down_total,
    )


def solution(mesh):
    tokens, vector, matrix = P("fsdp", "seq", None), P("fsdp"), P("fsdp", None)
    placed = (tokens, vector, matrix, matrix, matrix, vector, vector, matrix)
    placed += (vector, matrix, matrix, matrix, tokens, P(), P())
    results = (tokens, tokens, vector, matrix, matrix, matrix, vector, vector, matrix)
    results += (vector, matrix, matrix, matrix)
    return jax.shard_map(body, mesh=mesh, in_specs=placed, out_specs=results, check_vma=False)
```

time: 1430 us -> 1300 us (0.909)
  starting transfers between devices: 380 us -> 196 us
  blocking collectives: 99.7 us -> 232 us
  local copies, waits for them, and re-layouts: 229 us -> 99 us
  waiting for transfers between devices: 348 us -> 474 us
  matrix products: 197 us -> 117 us
  Pallas kernels: 0 us -> 58.1 us
  other arithmetic: 148 us -> 94.7 us
    ppermute x143 -> x25, starting transfers between devices: 357 us -> 97.7 us  [line_sums(): got = lax.ppermute(operand, 'seq', pairs)]
    all_to_all x0 -> x1, blocking collectives: none -> 168 us  [spread(): return lax.all_to_all(values, 'fsdp', 0, 0, tiled=True)]
    reduce_scatter x2, waiting for transfers between devices: 0.01 us -> 131 us  [the longest x1 72.7 us: body(): lax.psum_scatter(after(mixed_part, normed_one_grad[:8, :128]), 'fsdp', sc...]
    ppermute x143 -> x25, waiting for transfers between devices: 347 us -> 244 us  [line_sums(): got = lax.ppermute(operand, 'seq', pairs)]
    all_to_all x0 -> x5, starting transfers between devices: none -> 75.5 us  [the longest x3 67.7 us: spread(): return lax.all_to_all(values, 'fsdp', 0, 0, tiled=True)]
    dot_general x16 -> x7, matrix products: 148 us -> 80.8 us  [the longest x3 40.6 us: dot_nt(): lax.dot_general(left, right, (((1,), (1,)), ((), ())), preferred_element_...]
    psum x1 -> x0, blocking collectives: 66 us -> none  [body(): lax.psum(jnp.concatenate([attention_gain_part, feed_gain_part, query_norm...]
    all_gather x0 -> x2, blocking collectives: none -> 64.7 us  [the longest x1 48.1 us: body(): parts = lax.all_gather(parts, ('seq', 'fsdp'), axis=0)]
  transfers between devices with their start and end apart: 155 -> 42, of which waited for: 61 -> 16; matrix products, arithmetic and copies ran while one was open for 34% -> 18% of each run, Pallas kernels for 0% -> 5%
where the time goes in v2:
time: 1300 us; the launch traced here: 1290 us
  waiting for transfers between devices  474 us (36%)
  blocking collectives  232 us (18%)
  starting transfers between devices  196 us (15%)
  matrix products  117 us (9%)
  local copies, waits for them, and re-layouts  99 us (8%)
  other arithmetic  94.7 us (7%)
  Pallas kernels  58.1 us (4%)
  between operations  15.3 us (1%)
    ppermute x25, waiting for transfers between devices, line_sums(): got = lax.ppermute(operand, 'seq', pairs)  244 us
    all_to_all x1, blocking collectives, spread(): return lax.all_to_all(values, 'fsdp', 0, 0, tiled=True)  168 us
    ppermute x25, starting transfers between devices, line_sums(): got = lax.ppermute(operand, 'seq', pairs)  97.7 us
    reduce_scatter x1, waiting for transfers between devices, body(): lax.psum_scatter(after(mixed_part, normed_one_grad[:8, :128]), 'fsdp', sc...  72.7 us
    all_to_all x3, starting transfers between devices, spread(): return lax.all_to_all(values, 'fsdp', 0, 0, tiled=True)  67.7 us
    reduce_scatter x1, waiting for transfers between devices, body(): lax.psum_scatter(normed_two_part, 'fsdp', scatter_dimension=0, tiled=True)  58.3 us
    all_gather x1, blocking collectives, body(): parts = lax.all_gather(parts, ('seq', 'fsdp'), axis=0)  48.1 us
    unnamed x111, local copies, waits for them, and re-layouts  45.2 us
  transfers between devices with their start and end apart: 42, of which 16 were waited for; matrix products, arithmetic and copies ran while one was open for 18% of the time, Pallas kernels for 5%

profile of v2, /device:TPU:0, one launch (start us, length us, event | category | flops | bytes accessed | tf_op | source)
XLA Modules:
  0.0 1287.5 jit_solution(2560187234618212706)
XLA Ops:
  10.1 16.6 %all-gather = bf16[8,1,640]{2,1,0:T(2,128)(2,1)S(1)} all-gather(bf16[1,1,640]{2,1,0:T(2,128)(2,1)S(1)} %reshape.295), channel_id=1, replica_groups=mesh['seq'=4,'fsdp'=8] {'fsdp'}, dimensions={0}, use_global_device_ids=true | all-gather | bytes 11520 | tf_op jit(solution)/shard_map/all_gather | solution.py:381
  33.2 58.2 %all-to-all-start = ((bf16[8,256,512]{2,1,0:T(8,128)(2,1)}), bf16[8,256,512]{2,1,0:T(8,128)(2,1)}, u32[]{:S(2)}, u32[]{:S(2)}) async-start(bf16[8,256,512]{2,1,0:T(8,128)(2,1)} %maximum_bitcast_fusion.1), calls=%async_computation | async-start | bytes 4194304 | tf_op jit(solution)/shard_map/all_to_all | solution.py:51
  101.3 28.2 %all-to-all-done = bf16[8,256,512]{2,1,0:T(8,128)(2,1)} async-done(((bf16[8,256,512]{2,1,0:T(8,128)(2,1)}), bf16[8,256,512]{2,1,0:T(8,128)(2,1)}, u32[]{:S(2)}, u32[]{:S(2)}) %all-to-all-start) | async-done | bytes 2097184 | tf_op jit(solution)/shard_map/all_to_all | solution.py:51
  129.6 30.7 %all-gather.6.cloned.1.call-done.x_ref = bf16[2048,2048]{1,0:T(8,128)(2,1)} async-done(((bf16[256,2048]{1,0:T(8,128)(2,1)}), bf16[2048,2048]{1,0:T(8,128)(2,1)}) %all-gather.6.cloned.1.call-update) | async-done | bytes 8388624 | tf_op jit(solution)/shard_map/all_gather | solution.py:425
  160.3 21.7 %attend.1 = (f32[2048,384]{1,0:T(8,128)}, bf16[2048,512]{1,0:T(8,128)(2,1)}, bf16[2048,256]{1,0:T(8,128)(2,1)}) custom-call(s32[10]{0:T(128)} %pad_add_fusion.lead_ref, bf16[2048,2048]{1,0:T(8,128)(2,1)} %all-gather.6.cloned.1.call-done.x_ref, bf16[2048,512]{1,0:T(8,128)(2,1)} %bitcast.3.w_ref, f32[1,128]{1,0:T(1,128)} %reshape.275.qg_ref, ...), custom_call_target="tpu_custom_call" | custom-call | flops 8589934592 | bytes 20971520 | tf_op jit(solution)/shard_map/attend/pallas_call | solution.py:427
  188.6 38.7 %all-gather.8.cloned.1.call-done = bf16[2048,2048]{1,0:T(8,128)(2,1)} async-done(((bf16[256,2048]{1,0:T(8,128)(2,1)}), bf16[2048,2048]{1,0:T(8,128)(2,1)}) %all-gather.8.cloned.1.call-update) | async-done | bytes 8388624 | tf_op jit(solution)/shard_map/all_gather | solution.py:396
  227.4 6.4 multiply_reduce_fusion
  236.3 9.6 collective-permute-start.2
  246.2 4.6 copy.86
  250.8 4.6 copy.85
  258.7 167.7 %all_to_all.30 = bf16[8,256,1536]{1,2,0:T(8,128)(2,1)} all-to-all(bf16[8,256,1536]{1,2,0:T(8,128)(2,1)S(1)} %maximum_bitcast_fusion), channel_id=1, replica_groups=mesh['seq'=4,'fsdp'=8] {'fsdp'}, dimensions={0} | all-to-all | bytes 12582912 | tf_op jit(solution)/shard_map/all_to_all | solution.py:51
  426.4 8.6 copy.87
  435.0 19.0 %fusion.42 = f32[2048,1536]{0,1:T(8,128)} fusion(bf16[2048,2048]{1,0:T(8,128)(2,1)} %all-gather.10.cloned.1.call-done, bf16[2048,1536]{1,0:T(8,128)(2,1)} %bitcast.119), kind=kOutput, calls=%fused_computation.140 | convolution fusion | flops 12884901888 | bytes 27262976 | tf_op jit(solution)/shard_map/dot_general | solution.py:98
  454.0 16.1 %multiply_convert_fusion.1 = (bf16[2048,768]{0,1:T(8,128)(2,1)S(1)}, bf16[2048,768]{0,1:T(8,128)(2,1)}, bf16[2048,768]{0,1:T(8,128)(2,1)}) fusion(f32[2048,1536]{0,1:T(8,128)} %fusion.42, bf16[2048,2048]{1,0:T(8,128)(2,1)} %all-gather.12.cloned.1.call-done, bf16[768,2048]{1,0:T(8,128)(2,1)S(1)} %copy-done), kind=kOutput, calls=%fused_computation.9 | convolution fusion | flops 6467616768 | bytes 33554432 | tf_op jit(solution)/shard_map/dot_general | solution.py:102
  471.8 18.8 %convolution_convert_fusion.1 = bf16[2048,2048]{1,0:T(8,128)(2,1)} fusion(bf16[2048,1536]{1,0:T(8,128)(2,1)} %bitcast.120, bf16[2048,768]{0,1:T(8,128)(2,1)} %get-tuple-element.121, bf16[2048,768]{0,1:T(8,128)(2,1)S(1)} %get-tuple-element.120), kind=kOutput, calls=%fused_computation.2 | convolution fusion | flops 12901679104 | bytes 20971520 | tf_op jit(solution)/shard_map/dot_general | solution.py:102
  490.7 11.1 convolution_convert_fusion.2
  502.3 58.3 %reduce-scatter.7.cloned.1.call-done = bf16[256,2048]{1,0:T(8,128)(2,1)} async-done(((bf16[2048,2048]{1,0:T(8,128)(2,1)}), bf16[256,2048]{1,0:T(8,128)(2,1)}) %reduce-scatter.7.cloned.1.call-update) | async-done | bytes 1048592 | tf_op jit(solution)/shard_map/reduce_scatter | solution.py:460
  562.7 72.7 %reduce-scatter.5.cloned.1.call-done = bf16[256,2048]{1,0:T(8,128)(2,1)} async-done(((bf16[2048,2048]{1,0:T(8,128)(2,1)}), bf16[256,2048]{1,0:T(8,128)(2,1)}) %reduce-scatter.5.cloned.1.call-update) | async-done | bytes 1048592 | tf_op jit(solution)/shard_map/reduce_scatter | solution.py:506
  640.2 6.9 convolution_convert_fusion
  649.0 18.3 %convolution_convert_fusion.3 = bf16[2048,1536]{1,0:T(8,128)(2,1)} fusion(bf16[2048,2048]{1,0:T(8,128)(2,1)} %all-gather.10.cloned.1.call-done, bf16[2048,768]{0,1:T(8,128)(2,1)} %get-tuple-element.121, bf16[2048,768]{0,1:T(8,128)(2,1)S(1)} %copy-done.44), kind=kOutput, calls=%fused_computation.4 | convolution fusion | flops 12900630528 | bytes 20971520 | tf_op jit(solution)/shard_map/dot_general | solution.py:106
  667.3 5.2 all-to-all-start.5
  672.5 9.3 convolution_convert_fusion.4
  685.8 33.9 %collective-permute-done.4 = bf16[384,2048]{1,0:T(8,128)(2,1)S(1)} collective-permute-done((bf16[384,2048]{1,0:T(8,128)(2,1)S(1)}, bf16[384,2048]{1,0:T(8,128)(2,1)S(1)}, u32[]{:S(2)}, u32[]{:S(2)}) %collective-permute-start.4) | collective-permute-done | bytes 1572896 | tf_op jit(solution)/shard_map/ppermute | solution.py:82
  727.9 31.4 %collective-permute-done.5 = bf16[384,2048]{1,0:T(8,128)(2,1)S(1)} collective-permute-done((bf16[384,2048]{1,0:T(8,128)(2,1)S(1)}, bf16[384,2048]{1,0:T(8,128)(2,1)S(1)}, u32[]{:S(2)}, u32[]{:S(2)}) %collective-permute-start.5) | collective-permute-done | bytes 1572896 | tf_op jit(solution)/shard_map/ppermute | solution.py:82
  761.0 5.7 convolution_convert_fusion.6
  775.9 5.8 fusion.35
  781.7 4.8 collective-permute-start.8
  789.3 36.4 %attend_back.1 = (bf16[2048,512]{1,0:T(8,128)(2,1)}, bf16[2048,2048]{1,0:T(8,128)(2,1)}, f32[8,128]{1,0:T(8,128)}) custom-call(s32[10]{0:T(128)} %pad_add_fusion.lead_ref, bf16[2048,256]{1,0:T(8,128)(2,1)} %bitcast.130, bf16[2048,512]{1,0:T(8,128)(2,1)} %get-tuple-element.48.qkv_ref, f32[2048,384]{1,0:T(8,128)} %get-tuple-element.49.proj_ref, ...), custom_call_target="tpu_custom_call" | custom-call | flops 17179869184 | bytes 31457280 | tf_op jit(solution)/shard_map/attend_back/pallas_call | solution.py:480
  834.2 30.2 %collective-permute-done.9 = bf16[384,2048]{1,0:T(8,128)(2,1)} collective-permute-done((bf16[384,2048]{1,0:T(8,128)(2,1)}, bf16[384,2048]{1,0:T(8,128)(2,1)}, u32[]{:S(2)}, u32[]{:S(2)}) %collective-permute-start.9) | collective-permute-done | bytes 1572896 | tf_op jit(solution)/shard_map/ppermute | solution.py:82
  870.4 29.1 %collective-permute-done.10 = bf16[512,1536]{1,0:T(8,128)(2,1)} collective-permute-done((bf16[512,1536]{1,0:T(8,128)(2,1)}, bf16[512,1536]{1,0:T(8,128)(2,1)}, u32[]{:S(2)}, u32[]{:S(2)}) %collective-permute-start.10) | collective-permute-done | bytes 1572896 | tf_op jit(solution)/shard_map/ppermute | solution.py:82
  917.0 25.6 %collective-permute-done.14 = bf16[512,1536]{1,0:T(8,128)(2,1)} collective-permute-done((bf16[512,1536]{1,0:T(8,128)(2,1)}, bf16[512,1536]{1,0:T(8,128)(2,1)}, u32[]{:S(2)}, u32[]{:S(2)}) %collective-permute-start.14) | collective-permute-done | bytes 1572896 | tf_op jit(solution)/shard_map/ppermute | solution.py:82
  955.0 5.7 convolution_convert_fusion.5
  965.1 16.9 %collective-permute-done.15 = bf16[512,1536]{1,0:T(8,128)(2,1)} collective-permute-done((bf16[512,1536]{1,0:T(8,128)(2,1)}, bf16[512,1536]{1,0:T(8,128)(2,1)}, u32[]{:S(2)}, u32[]{:S(2)}) %collective-permute-start.15) | collective-permute-done | bytes 1572896 | tf_op jit(solution)/shard_map/ppermute | solution.py:82
  999.1 24.8 %collective-permute-start.18 = (bf16[256,2048]{1,0:T(8,128)(2,1)}, bf16[256,2048]{1,0:T(8,128)(2,1)}, u32[]{:S(2)}, u32[]{:S(2)}) collective-permute-start(bf16[256,2048]{1,0:T(8,128)(2,1)} %reduce-scatter.11.cloned.1.call-done), channel_id=1, source_target_pairs={{0,8},{24,16},{1,9},{25,17},{2,10},{26,18},{3,11},{27,19},{4,12},{... | collective-permute-start | bytes 3145736 | tf_op jit(solution)/shard_map/ppermute | solution.py:82
  1029.5 9.6 collective-permute-start.3
  1039.2 7.6 collective-permute-done.18
  1052.4 26.5 %collective-permute-start.20 = (bf16[1024,512]{1,0:T(8,128)(2,1)}, bf16[1024,512]{1,0:T(8,128)(2,1)}, u32[]{:S(2)}, u32[]{:S(2)}) collective-permute-start(bf16[1024,512]{1,0:T(8,128)(2,1)} %bitcast.23), channel_id=1, source_target_pairs={{0,8},{24,16},{1,9},{25,17},{2,10},{26,18},{3,11},{27,19},{4,12},{... | collective-permute-start | bytes 3145736 | tf_op jit(solution)/shard_map/ppermute | solution.py:82
  1078.9 48.1 %all_gather.23 = f32[32,34,128]{2,1,0:T(8,128)S(1)} all-gather(f32[1,34,128]{2,1,0:T(8,128)S(1)} %maximum_bitcast_fusion.2), channel_id=1, replica_groups=mesh['seq'=4,'fsdp'=8] {'seq','fsdp'}, dimensions={0}, use_global_device_ids=true | all-gather | bytes 574464 | tf_op jit(solution)/shard_map/all_gather | solution.py:530
  1134.5 31.3 %collective-permute-done.22 = bf16[512,1536]{1,0:T(8,128)(2,1)S(1)} collective-permute-done((bf16[512,1536]{1,0:T(8,128)(2,1)}, bf16[512,1536]{1,0:T(8,128)(2,1)S(1)}, u32[]{:S(2)}, u32[]{:S(2)}) %collective-permute-start.22) | collective-permute-done | bytes 1572896 | tf_op jit(solution)/shard_map/ppermute | solution.py:82
  1167.3 4.7 collective-permute-start.24
  1173.5 20.2 %collective-permute-done.24 = bf16[1024,512]{1,0:T(8,128)(2,1)S(1)} collective-permute-done((bf16[1024,512]{1,0:T(8,128)(2,1)S(1)}, bf16[1024,512]{1,0:T(8,128)(2,1)S(1)}, u32[]{:S(2)}, u32[]{:S(2)}) %collective-permute-start.24) | collective-permute-done | bytes 1048608 | tf_op jit(solution)/shard_map/ppermute | solution.py:82
  1197.4 6.4 convert_bitcast_fusion
  1204.1 17.7 %collective-permute-done.26 = bf16[1024,512]{1,0:T(8,128)(2,1)S(1)} collective-permute-done((bf16[1024,512]{1,0:T(8,128)(2,1)S(1)}, bf16[1024,512]{1,0:T(8,128)(2,1)S(1)}, u32[]{:S(2)}, u32[]{:S(2)}) %collective-permute-start.26) | collective-permute-done | bytes 1048608 | tf_op jit(solution)/shard_map/ppermute | solution.py:82
  1224.0 10.6 fusion.34
  1234.6 6.6 copy.93
  1241.2 6.6 copy.98
  1247.7 6.6 copy.94
  1254.3 6.6 copy.99
  (261 shorter events, 181.4 us)
Async XLA Ops:
  7.2 446.9 %copy-start = (bf16[768,2048]{1,0:T(8,128)(2,1)S(1)}, bf16[768,2048]{1,0:T(8,128)(2,1)}, u32[]{:S(2)}) copy-start(bf16[768,2048]{1,0:T(8,128)(2,1)} %param.26) | copy-start | bytes 9437188
  7.2 153.1 %all-gather.6.cloned.1.call-start = ((), (), s32[]{:S(2)}) async-start(), calls=%async_computation.10 | async-start | bytes 9437184 | tf_op jit(solution)/shard_map/all_gather | solution.py:425
  7.2 19.6 %collective-permute-start = (bf16[256,2048]{1,0:T(8,128)(2,1)}, bf16[256,2048]{1,0:T(8,128)(2,1)S(1)}, u32[]{:S(2)}, u32[]{:S(2)}) collective-permute-start(bf16[256,2048]{1,0:T(8,128)(2,1)} %bitcast.148), channel_id=1, source_target_pairs={{0,0},{1,5},{2,10},{3,15},{4,20},{5,17},{6,30},{7,27},{8,2},{9,7},... | collective-permute-start | bytes 3145736 | tf_op jit(solution)/shard_map/ppermute | solution.py:31
  29.1 198.2 %all-gather.8.cloned.1.call-start = ((), (), s32[]{:S(2)}) async-start(), calls=%async_computation.11 | async-start | bytes 9437184 | tf_op jit(solution)/shard_map/all_gather | solution.py:396
  33.2 58.2 %copy-start.39 = (s32[24]{0:T(128)S(1)}, s32[24]{0:T(128)}, u32[]{:S(2)}) copy-start(s32[24]{0:T(128)} %param.29) | copy-start | bytes 292
  33.2 58.2 %copy-start.40 = (s32[24]{0:T(128)S(1)}, s32[24]{0:T(128)}, u32[]{:S(2)}) copy-start(s32[24]{0:T(128)} %param.28) | copy-start | bytes 292
  33.2 96.4 %all-to-all-start = ((bf16[8,256,512]{2,1,0:T(8,128)(2,1)}), bf16[8,256,512]{2,1,0:T(8,128)(2,1)}, u32[]{:S(2)}, u32[]{:S(2)}) async-start(bf16[8,256,512]{2,1,0:T(8,128)(2,1)} %maximum_bitcast_fusion.1), calls=%async_computation | async-start | bytes 4194304 | tf_op jit(solution)/shard_map/all_to_all | solution.py:51
  184.3 43.0 %all-to-all-start.1 = ((bf16[8,256,256]{1,2,0:T(8,128)(2,1)}), bf16[8,256,256]{1,2,0:T(8,128)(2,1)}, u32[]{:S(2)}, u32[]{:S(2)}) async-start(bf16[8,256,256]{1,2,0:T(8,128)(2,1)} %copy.84), calls=%async_computation.1 | async-start | bytes 2097152 | tf_op jit(solution)/shard_map/all_to_all | solution.py:47
  188.6 246.4 %all-gather.10.cloned.1.call-start = ((), (), s32[]{:S(2)}) async-start(), calls=%async_computation.12 | async-start | bytes 9437184 | tf_op jit(solution)/shard_map/all_gather | solution.py:449
  236.3 217.8 %all-gather.12.cloned.1.call-start = ((), (), s32[]{:S(2)}) async-start(), calls=%async_computation.14 | async-start | bytes 9437184 | tf_op jit(solution)/shard_map/all_gather | solution.py:442
  236.3 9.6 collective-permute-start.2
  245.9 314.6 %reduce-scatter.7.cloned.1.call-start = ((), (), s32[]{:S(2)}) async-start(), calls=%async_computation.15 | async-start | bytes 9437184 | tf_op jit(solution)/shard_map/reduce_scatter | solution.py:460
  490.6 144.8 %reduce-scatter.5.cloned.1.call-start = ((), (), s32[]{:S(2)}) async-start(), calls=%async_computation.13 | async-start | bytes 9437184 | tf_op jit(solution)/shard_map/reduce_scatter | solution.py:506
  501.8 58.8 %copy-start.3 = (f32[256,2048]{1,0:T(8,128)S(1)}, f32[256,2048]{1,0:T(8,128)}, u32[]{:S(2)}) copy-start(f32[256,2048]{1,0:T(8,128)} %copy-done.2) | copy-start | bytes 6291460
  501.8 496.0 %reduce-scatter.11.cloned.1.call-start = ((), (), s32[]{:S(2)}) async-start(), calls=%async_computation.17 | async-start | bytes 9437184 | tf_op jit(solution)/shard_map/reduce_scatter | solution.py:477
  560.6 74.8 %copy-start.25 = (bf16[256,2048]{1,0:T(8,128)(2,1)S(1)}, bf16[256,2048]{1,0:T(8,128)(2,1)}, u32[]{:S(2)}) copy-start(bf16[256,2048]{1,0:T(8,128)(2,1)} %reduce-scatter.7.cloned.1.call-done) | copy-start | bytes 3145732
  667.3 101.2 %all-to-all-start.5 = ((bf16[8,256,1536]{2,1,0:T(8,128)(2,1)}), bf16[8,256,1536]{2,1,0:T(8,128)(2,1)}, u32[]{:S(2)}, u32[]{:S(2)}) async-start(bf16[8,256,1536]{2,1,0:T(8,128)(2,1)} %bitcast.118), calls=%async_computation.8 | async-start | bytes 12582912 | tf_op jit(solution)/shard_map/all_to_all | solution.py:51
  682.0 37.7 %collective-permute-start.4 = (bf16[384,2048]{1,0:T(8,128)(2,1)S(1)}, bf16[384,2048]{1,0:T(8,128)(2,1)S(1)}, u32[]{:S(2)}, u32[]{:S(2)}) collective-permute-start(bf16[384,2048]{1,0:T(8,128)(2,1)S(1)} %get-tuple-element.131), channel_id=1, source_target_pairs={{0,8},{24,16},{1,9},{25,17},{2,10},{26,18},{3,11},{27,19},{4,12},{... | collective-permute-start | bytes 4718600 | tf_op jit(solution)/shard_map/ppermute | solution.py:82
  721.5 37.8 %collective-permute-start.5 = (bf16[384,2048]{1,0:T(8,128)(2,1)S(1)}, bf16[384,2048]{1,0:T(8,128)(2,1)S(1)}, u32[]{:S(2)}, u32[]{:S(2)}) collective-permute-start(bf16[384,2048]{1,0:T(8,128)(2,1)S(1)} %get-tuple-element.53), channel_id=1, source_target_pairs={{0,8},{24,16},{1,9},{25,17},{2,10},{26,18},{3,11},{27,19},{4,12},{... | collective-permute-start | bytes 4718600 | tf_op jit(solution)/shard_map/ppermute | solution.py:82
  726.1 46.1 %collective-permute-start.6 = (bf16[384,2048]{1,0:T(8,128)(2,1)}, bf16[384,2048]{1,0:T(8,128)(2,1)}, u32[]{:S(2)}, u32[]{:S(2)}) collective-permute-start(bf16[384,2048]{1,0:T(8,128)(2,1)} %add_convert_fusion.11), channel_id=1, source_target_pairs={{8,16},{16,8},{9,17},{17,9},{10,18},{18,10},{11,19},{19,11},{12,20... | collective-permute-start | bytes 4718600 | tf_op jit(solution)/shard_map/ppermute | solution.py:82
  768.5 19.8 %all-to-all-start.3 = ((bf16[8,256,256]{2,1,0:T(8,128)(2,1)}), bf16[8,256,256]{2,1,0:T(8,128)(2,1)S(1)}, u32[]{:S(2)}, u32[]{:S(2)}) async-start(bf16[8,256,256]{2,1,0:T(8,128)(2,1)} %bitcast.108), calls=%async_computation.5 | async-start | bytes 2097152 | tf_op jit(solution)/shard_map/all_to_all | solution.py:47
  772.1 253.6 %reduce-scatter.9.cloned.1.call-start = ((), (), s32[]{:S(2)}) async-start(), calls=%async_computation.16 | async-start | bytes 9437184 | tf_op jit(solution)/shard_map/reduce_scatter | solution.py:493
  781.7 49.1 %collective-permute-start.8 = (bf16[512,1536]{1,0:T(8,128)(2,1)}, bf16[512,1536]{1,0:T(8,128)(2,1)}, u32[]{:S(2)}, u32[]{:S(2)}) collective-permute-start(bf16[512,1536]{1,0:T(8,128)(2,1)} %bitcast.27), channel_id=1, source_target_pairs={{0,8},{24,16},{1,9},{25,17},{2,10},{26,18},{3,11},{27,19},{4,12},{... | collective-permute-start | bytes 4718600 | tf_op jit(solution)/shard_map/ppermute | solution.py:82
  786.5 40.5 %collective-permute-start.7 = (bf16[384,2048]{1,0:T(8,128)(2,1)}, bf16[384,2048]{1,0:T(8,128)(2,1)}, u32[]{:S(2)}, u32[]{:S(2)}) collective-permute-start(bf16[384,2048]{1,0:T(8,128)(2,1)} %add_convert_fusion.10), channel_id=1, source_target_pairs={{8,16},{16,8},{9,17},{17,9},{10,18},{18,10},{11,19},{19,11},{12,20... | collective-permute-start | bytes 4718600 | tf_op jit(solution)/shard_map/ppermute | solution.py:82
  825.7 38.7 %collective-permute-start.9 = (bf16[384,2048]{1,0:T(8,128)(2,1)}, bf16[384,2048]{1,0:T(8,128)(2,1)}, u32[]{:S(2)}, u32[]{:S(2)}) collective-permute-start(bf16[384,2048]{1,0:T(8,128)(2,1)} %add_convert_fusion.9), channel_id=1, source_target_pairs={{8,0},{16,24},{9,1},{17,25},{10,2},{18,26},{11,3},{19,27},{12,4},{... | collective-permute-start | bytes 4718600 | tf_op jit(solution)/shard_map/ppermute | solution.py:82
  864.4 35.0 %collective-permute-start.10 = (bf16[512,1536]{1,0:T(8,128)(2,1)}, bf16[512,1536]{1,0:T(8,128)(2,1)}, u32[]{:S(2)}, u32[]{:S(2)}) collective-permute-start(bf16[512,1536]{1,0:T(8,128)(2,1)} %bitcast.26), channel_id=1, source_target_pairs={{0,8},{24,16},{1,9},{25,17},{2,10},{26,18},{3,11},{27,19},{4,12},{... | collective-permute-start | bytes 4718600 | tf_op jit(solution)/shard_map/ppermute | solution.py:82
  867.1 35.8 %collective-permute-start.11 = (bf16[512,1536]{1,0:T(8,128)(2,1)}, bf16[512,1536]{1,0:T(8,128)(2,1)}, u32[]{:S(2)}, u32[]{:S(2)}) collective-permute-start(bf16[512,1536]{1,0:T(8,128)(2,1)} %add_convert_fusion.7), channel_id=1, source_target_pairs={{8,16},{16,8},{9,17},{17,9},{10,18},{18,10},{11,19},{19,11},{12,20... | collective-permute-start | bytes 4718600 | tf_op jit(solution)/shard_map/ppermute | solution.py:82
  868.9 37.7 %collective-permute-start.12 = (bf16[384,2048]{1,0:T(8,128)(2,1)}, bf16[384,2048]{1,0:T(8,128)(2,1)}, u32[]{:S(2)}, u32[]{:S(2)}) collective-permute-start(bf16[384,2048]{1,0:T(8,128)(2,1)} %add_convert_fusion.8), channel_id=1, source_target_pairs={{8,0},{16,24},{9,1},{17,25},{10,2},{18,26},{11,3},{19,27},{12,4},{... | collective-permute-start | bytes 4718600 | tf_op jit(solution)/shard_map/ppermute | solution.py:82
  906.6 36.0 %collective-permute-start.14 = (bf16[512,1536]{1,0:T(8,128)(2,1)}, bf16[512,1536]{1,0:T(8,128)(2,1)}, u32[]{:S(2)}, u32[]{:S(2)}) collective-permute-start(bf16[512,1536]{1,0:T(8,128)(2,1)} %bitcast_select_fusion), channel_id=1, source_target_pairs={{0,8},{24,16},{8,0},{16,24},{1,9},{25,17},{9,1},{17,25},{2,10},{26... | collective-permute-start | bytes 4718600 | tf_op jit(solution)/shard_map/ppermute | solution.py:82
  909.1 36.4 %collective-permute-start.13 = (bf16[512,1536]{1,0:T(8,128)(2,1)}, bf16[512,1536]{1,0:T(8,128)(2,1)S(1)}, u32[]{:S(2)}, u32[]{:S(2)}) collective-permute-start(bf16[512,1536]{1,0:T(8,128)(2,1)} %add_convert_fusion.6), channel_id=1, source_target_pairs={{8,16},{16,8},{9,17},{17,9},{10,18},{18,10},{11,19},{19,11},{12,20... | collective-permute-start | bytes 4718600 | tf_op jit(solution)/shard_map/ppermute | solution.py:82
  947.4 34.7 %collective-permute-start.15 = (bf16[512,1536]{1,0:T(8,128)(2,1)}, bf16[512,1536]{1,0:T(8,128)(2,1)}, u32[]{:S(2)}, u32[]{:S(2)}) collective-permute-start(bf16[512,1536]{1,0:T(8,128)(2,1)} %bitcast_select_fusion.1), channel_id=1, source_target_pairs={{0,8},{24,16},{8,0},{16,24},{1,9},{25,17},{9,1},{17,25},{2,10},{26... | collective-permute-start | bytes 4718600 | tf_op jit(solution)/shard_map/ppermute | solution.py:82
  949.1 37.2 %collective-permute-start.16 = (bf16[512,1536]{1,0:T(8,128)(2,1)}, bf16[512,1536]{1,0:T(8,128)(2,1)}, u32[]{:S(2)}, u32[]{:S(2)}) collective-permute-start(bf16[512,1536]{1,0:T(8,128)(2,1)} %add_convert_fusion.3), channel_id=1, source_target_pairs={{8,16},{16,8},{9,17},{17,9},{10,18},{18,10},{11,19},{19,11},{12,20... | collective-permute-start | bytes 4718600 | tf_op jit(solution)/shard_map/ppermute | solution.py:82
  960.8 33.9 %all-to-all-start.4 = ((bf16[8,256,512]{2,1,0:T(8,128)(2,1)}), bf16[8,256,512]{2,1,0:T(8,128)(2,1)}, u32[]{:S(2)}, u32[]{:S(2)}) async-start(bf16[8,256,512]{2,1,0:T(8,128)(2,1)} %bitcast.125), calls=%async_computation.7 | async-start | bytes 4194304 | tf_op jit(solution)/shard_map/all_to_all | solution.py:51
  985.5 8.2 collective-permute-start.1
  997.8 54.6 %collective-permute-start.19 = (bf16[512,1536]{1,0:T(8,128)(2,1)}, bf16[512,1536]{1,0:T(8,128)(2,1)}, u32[]{:S(2)}, u32[]{:S(2)}) collective-permute-start(bf16[512,1536]{1,0:T(8,128)(2,1)} %add_convert_fusion.1), channel_id=1, source_target_pairs={{8,0},{16,24},{9,1},{17,25},{10,2},{18,26},{11,3},{19,27},{12,4},{... | collective-permute-start | bytes 4718600 | tf_op jit(solution)/shard_map/ppermute | solution.py:82
  999.1 47.6 %collective-permute-start.18 = (bf16[256,2048]{1,0:T(8,128)(2,1)}, bf16[256,2048]{1,0:T(8,128)(2,1)}, u32[]{:S(2)}, u32[]{:S(2)}) collective-permute-start(bf16[256,2048]{1,0:T(8,128)(2,1)} %reduce-scatter.11.cloned.1.call-done), channel_id=1, source_target_pairs={{0,8},{24,16},{1,9},{25,17},{2,10},{26,18},{3,11},{27,19},{4,12},{... | collective-permute-start | bytes 3145736 | tf_op jit(solution)/shard_map/ppermute | solution.py:82
  1023.9 25.4 %collective-permute-start.17 = (bf16[512,1536]{1,0:T(8,128)(2,1)}, bf16[512,1536]{1,0:T(8,128)(2,1)}, u32[]{:S(2)}, u32[]{:S(2)}) collective-permute-start(bf16[512,1536]{1,0:T(8,128)(2,1)} %add_convert_fusion.2), channel_id=1, source_target_pairs={{8,16},{16,8},{9,17},{17,9},{10,18},{18,10},{11,19},{19,11},{12,20... | collective-permute-start | bytes 4718600 | tf_op jit(solution)/shard_map/ppermute | solution.py:82
  1029.5 102.6 %collective-permute-start.3 = (bf16[256,2048]{1,0:T(8,128)(2,1)}, bf16[256,2048]{1,0:T(8,128)(2,1)}, u32[]{:S(2)}, u32[]{:S(2)}) collective-permute-start(bf16[256,2048]{1,0:T(8,128)(2,1)} %fusion.9), channel_id=1, source_target_pairs={{0,0},{5,1},{10,2},{15,3},{20,4},{17,5},{30,6},{27,7},{2,8},{7,9},... | collective-permute-start | bytes 3145736 | tf_op jit(solution)/shard_map/ppermute | solution.py:31
  1049.3 81.2 %copy-start.15 = (bf16[512,1536]{1,0:T(8,128)(2,1)S(1)}, bf16[512,1536]{1,0:T(8,128)(2,1)}, u32[]{:S(2)}) copy-start(bf16[512,1536]{1,0:T(8,128)(2,1)} %add_convert_fusion.1) | copy-start | bytes 4718596
  1052.4 79.7 %collective-permute-start.20 = (bf16[1024,512]{1,0:T(8,128)(2,1)}, bf16[1024,512]{1,0:T(8,128)(2,1)}, u32[]{:S(2)}, u32[]{:S(2)}) collective-permute-start(bf16[1024,512]{1,0:T(8,128)(2,1)} %bitcast.23), channel_id=1, source_target_pairs={{0,8},{24,16},{1,9},{25,17},{2,10},{26,18},{3,11},{27,19},{4,12},{... | collective-permute-start | bytes 3145736 | tf_op jit(solution)/shard_map/ppermute | solution.py:82
  1127.0 38.7 %collective-permute-start.22 = (bf16[512,1536]{1,0:T(8,128)(2,1)}, bf16[512,1536]{1,0:T(8,128)(2,1)S(1)}, u32[]{:S(2)}, u32[]{:S(2)}) collective-permute-start(bf16[512,1536]{1,0:T(8,128)(2,1)} %add_convert_fusion), channel_id=1, source_target_pairs={{8,0},{16,24},{9,1},{17,25},{10,2},{18,26},{11,3},{19,27},{12,4},{... | collective-permute-start | bytes 4718600 | tf_op jit(solution)/shard_map/ppermute | solution.py:82
  1128.3 5.8 collective-permute-start.21
  1165.8 28.6 %collective-permute-start.25 = (bf16[256,2048]{1,0:T(8,128)(2,1)S(1)}, bf16[256,2048]{1,0:T(8,128)(2,1)S(1)}, u32[]{:S(2)}, u32[]{:S(2)}) collective-permute-start(bf16[256,2048]{1,0:T(8,128)(2,1)S(1)} %add_convert_fusion.15), channel_id=1, source_target_pairs={{8,0},{16,24},{9,1},{17,25},{10,2},{18,26},{11,3},{19,27},{12,4},{... | collective-permute-start | bytes 3145736 | tf_op jit(solution)/shard_map/ppermute | solution.py:82
  1167.3 26.4 %collective-permute-start.24 = (bf16[1024,512]{1,0:T(8,128)(2,1)S(1)}, bf16[1024,512]{1,0:T(8,128)(2,1)S(1)}, u32[]{:S(2)}, u32[]{:S(2)}) collective-permute-start(bf16[1024,512]{1,0:T(8,128)(2,1)S(1)} %bitcast.121), channel_id=1, source_target_pairs={{0,8},{24,16},{1,9},{25,17},{2,10},{26,18},{3,11},{27,19},{4,12},{... | collective-permute-start | bytes 3145736 | tf_op jit(solution)/shard_map/ppermute | solution.py:82
  1172.0 22.1 %collective-permute-start.23 = (bf16[1024,512]{1,0:T(8,128)(2,1)S(1)}, bf16[1024,512]{1,0:T(8,128)(2,1)S(1)}, u32[]{:S(2)}, u32[]{:S(2)}) collective-permute-start(bf16[1024,512]{1,0:T(8,128)(2,1)S(1)} %add_convert_fusion.16), channel_id=1, source_target_pairs={{8,16},{16,8},{9,17},{17,9},{10,18},{18,10},{11,19},{19,11},{12,20... | collective-permute-start | bytes 3145736 | tf_op jit(solution)/shard_map/ppermute | solution.py:82
  1195.4 26.4 %collective-permute-start.26 = (bf16[1024,512]{1,0:T(8,128)(2,1)S(1)}, bf16[1024,512]{1,0:T(8,128)(2,1)S(1)}, u32[]{:S(2)}, u32[]{:S(2)}) collective-permute-start(bf16[1024,512]{1,0:T(8,128)(2,1)S(1)} %add_convert_fusion.14), channel_id=1, source_target_pairs={{8,0},{16,24},{9,1},{17,25},{10,2},{18,26},{11,3},{19,27},{12,4},{... | collective-permute-start | bytes 3145736 | tf_op jit(solution)/shard_map/ppermute | solution.py:82
  1196.6 7.1 collective-permute-start.27
  1222.7 41.2 %collective-permute-start.28 = (bf16[1024,512]{1,0:T(8,128)(2,1)S(1)}, bf16[1024,512]{1,0:T(8,128)(2,1)}, u32[]{:S(2)}, u32[]{:S(2)}) collective-permute-start(bf16[1024,512]{1,0:T(8,128)(2,1)S(1)} %add_convert_fusion.12), channel_id=1, source_target_pairs={{8,0},{16,24},{9,1},{17,25},{10,2},{18,26},{11,3},{19,27},{12,4},{... | collective-permute-start | bytes 3145736 | tf_op jit(solution)/shard_map/ppermute | solution.py:82
  (41 other events, 538.9 us)
Sparse Core Ops, SparseCore 0:
  29.2 131.0 all-gather.5
  162.2 65.1 all-gather.7
  236.4 99.2 all-gather.9
  337.4 94.6 all-gather.11
  490.7 69.8 reduce-scatter.6
  563.9 71.4 reduce-scatter.4
  647.3 132.2 reduce-scatter.10
  825.8 70.1 reduce-scatter.8

commit v3 on v2

--- a/solution.py
+++ b/solution.py
@@ -14,11 +14,15 @@
 BF16 = jnp.bfloat16
 
 
+def plane_of(group, ns):
+    return group // 2 if group % 2 == 0 else ns - 1 - group // 2
+
+
 def relocation(ns, nf):
     pairs = []
     for s in range(ns):
         for g in range(nf):
-            p, c = divmod(g, 2)
+            p, c = plane_of(g, ns), g % 2
             pairs.append((s * nf + g, p * nf + 2 * (p ^ s ^ (ns // 2 * c)) + c))
     return pairs
 
@@ -36,7 +40,15 @@
 
 
 def after(value, *others):
-    return lax.optimization_barrier((value, others))[0]
+    return pl.pallas_call(
+        lambda *refs: None,
+        out_shape=jax.ShapeDtypeStruct(value.shape, value.dtype),
+        in_specs=[pl.BlockSpec(memory_space=pl.ANY)] * (1 + len(others)),
+        out_specs=pl.BlockSpec(memory_space=pl.ANY),
+        input_output_aliases={0: 0},
+        cost_estimate=pl.CostEstimate(flops=0, bytes_accessed=0, transcendentals=0),
+        name="after",
+    )(value, *others)
 
 
 def head_swap(values, share):
@@ -51,20 +63,49 @@
     return lax.all_to_all(values, "fsdp", 0, 0, tiled=True)
 
 
-def line_sums(chunks):
+def gather_by_permutes(values):
+    nf, me = lax.axis_size("fsdp"), lax.axis_index("fsdp")
+    kept = {0: values}
+    for k in range(2, nf, 2):
+        kept[k] = swap(values, k)
+    crossed = swap(jnp.stack([kept[k] for k in sorted(kept)]), 1)
+    buffer = jnp.zeros((nf,) + values.shape, values.dtype)
+    for number, k in enumerate(sorted(kept)):
+        buffer = lax.dynamic_update_index_in_dim(buffer, kept[k], me ^ k, 0)
+        buffer = lax.dynamic_update_index_in_dim(buffer, crossed[number], me ^ k ^ 1, 0)
+    return buffer.reshape((-1,) + values.shape[1:])
+
+
+def swap(values, k):
+    n = lax.axis_size("fsdp")
+    return lax.ppermute(values, "fsdp", [(i, i ^ k) for i in range(n)])
+
+
+def share_over_seq(piece):
+    ns, me = lax.axis_size("seq"), lax.axis_index("seq")
+    buffer = jnp.zeros((ns,) + piece.shape, piece.dtype)
+    buffer = lax.dynamic_update_index_in_dim(buffer, piece, me, 0)
+    for r in range(1, ns):
+        got = lax.ppermute(piece, "seq", [(i, (i + r) % ns) for i in range(ns)])
+        buffer = lax.dynamic_update_index_in_dim(buffer, got, (me + ns - r) % ns, 0)
+    return buffer
+
+
+def line_sums(chunks, lanes=2):
     ns = lax.axis_size("seq")
     if ns != 4:
-        return [lax.psum(c, "seq") for c in chunks]
+        totals = [lax.psum(c, "seq") for c in chunks]
+        return [(t, t) for t in totals]
     me = lax.axis_index("seq")
     outer = (me == 0) | (me == 3)
     inward, outward = [(0, 1), (3, 2)], [(1, 0), (2, 3)]
     count = len(chunks)
     part, total, sums = {}, {}, [None] * count
-    token = None
-    for step in range(count + 2):
+    tokens = {}
+    for step in range(count + 2 * lanes):
         sends = []
         new = chunks[step] if step < count else None
-        old = total[step - 2] if step >= 2 else None
+        old = total.get(step - 2 * lanes)
         if new is not None and old is not None and new.shape == old.shape:
             sends.append((jnp.where(outer, new, old), inward + outward, ("in", "out")))
         else:
@@ -72,22 +113,62 @@
                 sends.append((new, inward, ("in",)))
             if old is not None:
                 sends.append((old, outward, ("out",)))
-        if 1 <= step <= count:
-            sends.append((part[step - 1], [(1, 2), (2, 1)], ("across",)))
-        operands = [send[0] for send in sends]
-        if token is not None:
-            operands, _ = lax.optimization_barrier((operands, token))
-        token = []
-        for operand, (_, pairs, roles) in zip(operands, sends):
+        if step - lanes in part:
+            sends.append((part[step - lanes], [(1, 2), (2, 1)], ("across",)))
+        waited = tokens.get(step - lanes)
+        tokens[step] = []
+        for operand, pairs, roles in sends:
+            if waited:
+                operand = after(operand, *waited)
             got = lax.ppermute(operand, "seq", pairs)
-            token.append(got)
+            tokens[step].append(got)
             if "in" in roles:
                 part[step] = add_rounded(new, got)
             if "out" in roles:
-                sums[step - 2] = (got, old)
+                sums[step - 2 * lanes] = (got, old)
             if "across" in roles:
-                total[step - 1] = add_rounded(part[step - 1], got)
-    return [jnp.where(outer, got, mine) for got, mine in sums]
+                total[step - lanes] = add_rounded(part[step - lanes], got)
+    return sums
+
+
+def finish_kernel(sizes, lead_ref, got_ref, mine_ref, *refs):
+    start = 0
+    take = lead_ref[0] == 1
+    for size, out in zip(sizes, refs[-len(sizes) :]):
+        got = got_ref[0, :, start : start + size].astype(F32)
+        mine = mine_ref[0, :, start : start + size].astype(F32)
+        out[...] = jnp.where(take, got, mine)
+        start += size
+
+
+def finished(chunks, sizes, blocks):
+    ns, me = lax.axis_size("seq"), lax.axis_index("seq")
+    take = ((me == 0) | (me == ns - 1)).astype(jnp.int32)[None]
+    first, outs = 0, None
+    for got, mine in chunks:
+        count, rows, width = got.shape
+        taken = pl.BlockSpec((1, rows, width), lambda b, lead: (b, 0, 0))
+        held = [] if outs is None else list(outs)
+        outs = pl.pallas_call(
+            functools.partial(finish_kernel, sizes),
+            grid_spec=pltpu.PrefetchScalarGridSpec(
+                num_scalar_prefetch=1,
+                grid=(count,),
+                in_specs=[taken, taken] + [pl.BlockSpec(memory_space=pl.ANY)] * len(held),
+                out_specs=[
+                    pl.BlockSpec((rows, size), lambda b, lead, first=first: (0, first + b))
+                    for size in sizes
+                ],
+            ),
+            out_shape=[jax.ShapeDtypeStruct((rows, blocks * size), F32) for size in sizes],
+            input_output_aliases={3 + i: i for i in range(len(held))},
+            cost_estimate=pl.CostEstimate(
+                flops=0, bytes_accessed=8 * count * rows * width, transcendentals=0
+            ),
+            name="finish",
+        )(take, got, mine, *held)
+        first += count
+    return outs
 
 
 def add_rounded(left, right):
@@ -373,12 +454,14 @@
     back_pairs = [(b, a) for a, b in pairs]
     attend, attend_back = attention_calls(ns, share, rows, width, repeat, head, head ** (-0.5))
 
-    inputs = move(tokens[0], pairs).astype(F32)
-    own_gradient = move(after(cotangent[0], inputs[:8, :128]), pairs)
+    moved = move(tokens[0], pairs)
+    inputs = moved.astype(F32)
+    own_gradient = move(after(cotangent[0], moved), pairs)
 
     gains = jnp.concatenate([attention_gain, feed_gain, query_gain, key_gain])
     gains = jnp.pad(gains, (0, -gains.shape[0] % 128))
-    gains = lax.all_gather(gains, "fsdp", axis=0, tiled=True).reshape(nf, -1).astype(F32)
+    gains = spread(jnp.broadcast_to(gains[None, None, :], (nf, 1, gains.shape[0])))
+    gains = gains.reshape(nf, -1).astype(F32)
     cuts = [weight_rows, 2 * weight_rows, 2 * weight_rows + head // nf, 2 * weight_rows + 2 * head // nf]
     gain_one, gain_two, query_norm, key_norm = (
         part.reshape(1, -1) for part in jnp.split(gains, cuts, axis=1)[:4]
@@ -392,7 +475,14 @@
         ],
         axis=2,
     ).transpose(1, 0, 2)
-    qkv_matrix = spread(jnp.repeat(qkv_local, share, axis=0)).reshape(width, columns)
+    qkv_matrix = spread(after(jnp.repeat(qkv_local, share, axis=0))).reshape(width, columns)
+
+    part_cols = 2 * hidden_cols // ns
+    inner_local = jnp.where(plane < ns // 2, gate_weight, up_weight)
+    inner_local = lax.dynamic_index_in_dim(
+        inner_local.reshape(weight_rows, nf, ns // 2, part_cols), plane % (ns // 2), 2, keepdims=False
+    ).transpose(1, 0, 2)
+    inner_part = spread(after(inner_local)).reshape(width, part_cols)
     output_matrix = lax.all_gather(output_weight, "fsdp", axis=0, tiled=True)
 
     block_ids = jnp.arange(nf, dtype=jnp.int32)
@@ -401,7 +491,12 @@
     parity = block_ids % 2
     quarter = (block_ids // 2) ^ plane ^ (ns // 2 * parity)
     row_index = quarter[:, None] * rows + jnp.arange(rows, dtype=jnp.int32)[None, :]
-    dealt = lax.dynamic_slice_in_dim(dealing, plane * 2 * slots, 2 * slots)
+    dealt = jnp.concatenate(
+        [
+            lax.dynamic_slice_in_dim(dealing, plane * 2 * slots, slots),
+            lax.dynamic_slice_in_dim(dealing, (ns - 1 - plane) * 2 * slots + slots, slots),
+        ]
+    )
     numbers = jnp.arange(seq_lengths.shape[0], dtype=jnp.int32)
     lengths = jnp.sum(jnp.where(dealt[:, None] == numbers[None, :], seq_lengths[None, :], 0), axis=1)
     ends = jnp.cumsum(lengths.reshape(2, slots), axis=1)
@@ -422,7 +517,12 @@
 
     inverse_one = inverse_rms(inputs)
     unit_one = inputs * inverse_one
-    normed_one = lax.all_gather((unit_one * gain_one).astype(BF16), "fsdp", axis=0, tiled=True)
+    normed_own = after((unit_one * gain_one).astype(BF16), qkv_matrix, inner_part)
+    normed_one = lax.all_gather(normed_own, "fsdp", axis=0, tiled=True)
+    inner_matrix = share_over_seq(after(inner_part, own_gradient))
+    inner_matrix = inner_matrix.transpose(1, 0, 2).reshape(width, 2 * hidden_cols)
+    out_gradient = gather_by_permutes(after(own_gradient, normed_one))
+    hidden_grad = dot_nt(out_gradient, down_weight)
 
     proj, qkv, head_result = attend(
         lead, normed_one, qkv_matrix, query_norm, key_norm, cosine, sine, begin
@@ -430,19 +530,6 @@
     attended = head_swap(head_result.reshape(held, rows, wide), share)
     attended = attended.transpose(1, 0, 2).reshape(rows, key_heads * wide)
     residual = inputs + dot(attended, output_matrix)
-
-    inner_local = jnp.concatenate(
-        [
-            gate_weight.reshape(weight_rows, nf, hidden_cols),
-            up_weight.reshape(weight_rows, nf, hidden_cols),
-        ],
-        axis=2,
-    ).transpose(1, 0, 2)
-    inner_matrix = spread(after(inner_local, normed_one[:8, :128])).reshape(width, 2 * hidden_cols)
-    out_gradient = lax.all_gather(
-        after(own_gradient, normed_one[:8, :128]), "fsdp", axis=0, tiled=True
-    )
-    hidden_grad = dot_nt(out_gradient, down_weight)
 
     inverse_two = inverse_rms(residual)
     unit_two = residual * inverse_two
@@ -457,18 +544,17 @@
     ).astype(BF16)
     inner_grad = jnp.concatenate([gate_grad, up_grad], axis=1)
     normed_two_part = dot_nt(inner_grad, inner_matrix).astype(BF16)
+    down_term = dot_tn(hidden, out_gradient).astype(BF16)
+    inner_term = dot_tn(normed_two, inner_grad).astype(BF16)
     normed_two_grad = lax.psum_scatter(
         normed_two_part, "fsdp", scatter_dimension=0, tiled=True
-    ).astype(F32)
+    )
+    normed_two_grad = after(normed_two_grad, down_term, inner_term).astype(F32)
+    inner_got = spread(inner_term.reshape(nf, weight_rows, 2 * hidden_cols))
     feed_gain_part = jnp.sum(normed_two_grad * unit_two, axis=0)
     residual_grad = own_gradient.astype(F32) + norm_back(
         normed_two_grad * gain_two, unit_two, inverse_two
     )
-
-    down_term = dot_tn(after(hidden, normed_two_part[:8, :128]), out_gradient).astype(BF16)
-    inner_term = dot_tn(after(normed_two, down_term[:8, :128]), inner_grad).astype(BF16)
-    inner_got = spread(inner_term.reshape(nf, weight_rows, 2 * hidden_cols))
-    mixed_part = dot(after(hidden, inner_term[:8, :128]), down_weight).astype(BF16)
 
     branch_grad = residual_grad.astype(BF16)
     attended_grad = dot_nt(branch_grad, output_matrix).astype(BF16)
@@ -503,49 +589,59 @@
         residual_grad + norm_back(normed_one_grad * gain_one, unit_one, inverse_one)
     ).astype(BF16)
     input_gradient = move(input_gradient, back_pairs)
-    mixed_part = lax.psum_scatter(
-        after(mixed_part, normed_one_grad[:8, :128]), "fsdp", scatter_dimension=0, tiled=True
-    )
+    mixed_part = dot(after(hidden, normed_one_part), down_weight).astype(BF16)
+    mixed_part = lax.psum_scatter(mixed_part, "fsdp", scatter_dimension=0, tiled=True)
     mixed = move((residual + mixed_part.astype(F32)).astype(BF16), back_pairs)
 
-    down_pieces, inner_pieces, qkv_pieces = 2, 4, 2
+    down_pieces, inner_pieces, qkv_pieces = 4, nf, 4
     sums = line_sums(
         list(down_term.reshape(down_pieces, -1, width))
-        + list(inner_got.reshape(inner_pieces, -1, 2 * hidden_cols))
+        + list(inner_got.reshape(inner_pieces, -1, weight_rows, 2 * hidden_cols))
         + [output_term]
-        + list(qkv_got.reshape(qkv_pieces, -1, columns))
-    )
-    down_total = jnp.concatenate(sums[:down_pieces], axis=0).astype(F32)
+        + list(qkv_got.reshape(qkv_pieces, -1, weight_rows, columns))
+    )
+    outer = (plane == 0) | (plane == ns - 1)
+
+    def settled(pairs_of):
+        return jnp.concatenate([jnp.where(outer, g, m) for g, m in pairs_of], axis=0).astype(F32)
+
+    down_total = settled(sums[:down_pieces])
     sums = sums[down_pieces:]
-    inner_total = jnp.concatenate(sums[:inner_pieces], axis=0).reshape(nf, weight_rows, -1)
-    inner_total = inner_total.transpose(1, 0, 2).astype(F32)
+    gate_total, up_total = finished(sums[:inner_pieces], [hidden_cols, hidden_cols], nf)
     sums = sums[inner_pieces:]
-    output_total = sums[0].astype(F32)
-    qkv_total = jnp.concatenate(sums[1:], axis=0).reshape(key_heads, weight_rows, columns)
-    qkv_total = qkv_total.transpose(1, 0, 2).astype(F32)
+    output_total = settled(sums[:1])
+    query_total, key_total, value_total = finished(sums[1:], [wide, head, head], key_heads)
 
     parts = jnp.concatenate(
-        [attention_gain_part, feed_gain_part, norm_parts[0], norm_parts[1]]
-    ).reshape(-1, 128)
-    parts = lax.all_gather(parts, ("seq", "fsdp"), axis=0)
-    gain_sums = jnp.sum(parts, axis=0).reshape(-1)
-
-    def owned(start, size):
-        return lax.dynamic_slice_in_dim(gain_sums, start + me * size, size)
+        [
+            part.reshape(nf, -1)
+            for part in (attention_gain_part, feed_gain_part, norm_parts[0], norm_parts[1])
+        ],
+        axis=1,
+    )
+    parts = jnp.pad(parts, ((0, 0), (0, -parts.shape[1] % 128)))
+    parts = jnp.broadcast_to(parts[None], (ns,) + parts.shape).reshape(ns * nf, 1, -1)
+    parts = lax.all_to_all(parts, ("seq", "fsdp"), 0, 0, tiled=True)
+    gain_sums = jnp.sum(parts, axis=(0, 1))
+    sizes = [weight_rows, weight_rows, head // nf, head // nf]
+    ends_at = [sum(sizes[: i + 1]) for i in range(4)]
+    attention_gain_total, feed_gain_total, query_gain_total, key_gain_total = (
+        gain_sums[end - size : end] for end, size in zip(ends_at, sizes)
+    )
 
     return (
         mixed[None],
         input_gradient[None],
-        owned(0, weight_rows),
-        qkv_total[:, :, :wide].reshape(weight_rows, -1),
-        qkv_total[:, :, wide : wide + head].reshape(weight_rows, -1),
-        qkv_total[:, :, wide + head :].reshape(weight_rows, -1),
-        owned(2 * width, head // nf),
-        owned(2 * width + head, head // nf),
+        attention_gain_total,
+        query_total,
+        key_total,
+        value_total,
+        query_gain_total,
+        key_gain_total,
         output_total,
-        owned(width, weight_rows),
-        inner_total[:, :, :hidden_cols].reshape(weight_rows, -1),
-        inner_total[:, :, hidden_cols:].reshape(weight_rows, -1),
+        feed_gain_total,
+        gate_total,
+        up_total,
         down_total,
     )
 

time: 1300 us -> 1340 us (1.031)
  blocking collectives: 232 us -> 18.5 us
  starting transfers between devices: 196 us -> 304 us
  local copies, waits for them, and re-layouts: 99 us -> 153 us
  waiting for transfers between devices: 474 us -> 505 us
  Pallas kernels: 58.1 us -> 87 us
    ppermute x0 -> x7, waiting for transfers between devices: none -> 191 us  [the longest x3 124 us: share_over_seq(): got = lax.ppermute(piece, 'seq', [(i, (i + r) % ns) for i in range(ns)])]
    all_to_all x1, blocking collectives: 168 us -> 18.5 us  [head_swap(): lax.all_to_all(values, 'fsdp', 0, 0, axis_index_groups=among, tiled=True)]
    ppermute x25 -> x47, starting transfers between devices: 97.7 us -> 194 us  [line_sums(): got = lax.ppermute(operand, 'seq', pairs)]
    ppermute x25 -> x47, waiting for transfers between devices: 244 us -> 148 us  [line_sums(): got = lax.ppermute(operand, 'seq', pairs)]
    reduce_scatter x1, waiting for transfers between devices: 72.7 us -> 0.01 us  [body(): lax.psum_scatter(mixed_part, 'fsdp', scatter_dimension=0, tiled=True)]
    all_gather x2 -> x0, blocking collectives: 64.7 us -> none  [the longest x1 48.1 us: body(): parts = lax.all_gather(parts, ('seq', 'fsdp'), axis=0)]
    ppermute x0 -> x7, starting transfers between devices: none -> 46.2 us  [the longest x4 42.3 us: swap(): return lax.ppermute(values, 'fsdp', [(i, i ^ k) for i in range(n)])]
    all_to_all x3 -> x5, starting transfers between devices: 67.7 us -> 23 us  [spread(): return lax.all_to_all(values, 'fsdp', 0, 0, tiled=True)]
  transfers between devices with their start and end apart: 42 -> 72, of which waited for: 16 -> 30; matrix products, arithmetic and copies ran while one was open for 18% -> 21% of each run, Pallas kernels for 5% -> 6%
where the time goes in v3:
time: 1340 us; the launch traced here: 1310 us
  waiting for transfers between devices  505 us (38%)
  starting transfers between devices  304 us (23%)
  local copies, waits for them, and re-layouts  153 us (11%)
  matrix products  124 us (9%)
  other arithmetic  108 us (8%)
  Pallas kernels  87 us (6%)
  blocking collectives  18.5 us (1%)
  between operations  15.3 us (1%)
    ppermute x47, starting transfers between devices, line_sums(): got = lax.ppermute(operand, 'seq', pairs)  194 us
    ppermute x47, waiting for transfers between devices, line_sums(): got = lax.ppermute(operand, 'seq', pairs)  148 us
    ppermute x3, waiting for transfers between devices, share_over_seq(): got = lax.ppermute(piece, 'seq', [(i, (i + r) % ns) for i in range(ns)])  124 us
    unnamed x146, local copies, waits for them, and re-layouts  79.6 us
    ppermute x4, waiting for transfers between devices, swap(): return lax.ppermute(values, 'fsdp', [(i, i ^ k) for i in range(n)])  66.8 us
    dot_general x4, matrix products, dot_tn(): lax.dot_general(left, right, (((0,), (0,)), ((), ())), preferred_element_...  47.9 us
    all_to_all x5, waiting for transfers between devices, spread(): return lax.all_to_all(values, 'fsdp', 0, 0, tiled=True)  46 us
    all_gather x1, waiting for transfers between devices, body(): normed_one = lax.all_gather(normed_own, 'fsdp', axis=0, tiled=True)  42.9 us
  transfers between devices with their start and end apart: 72, of which 30 were waited for; matrix products, arithmetic and copies ran while one was open for 21% of the time, Pallas kernels for 6%

profile of v3, /device:TPU:0, one launch (start us, length us, event | category | flops | bytes accessed | tf_op | source)
XLA Modules:
  0.0 1314.9 jit_solution(12854054963227666938)
XLA Ops:
  21.4 8.0 reshape.283
  40.6 9.5 collective-permute-start
  65.9 15.3 %all-to-all-done.2 = bf16[8,256,384]{2,1,0:T(8,128)(2,1)} async-done(((bf16[8,256,384]{2,1,0:T(8,128)(2,1)}), bf16[8,256,384]{2,1,0:T(8,128)(2,1)}, u32[]{:S(2)}, u32[]{:S(2)}) %all-to-all-start.2) | async-done | bytes 1572896 | tf_op jit(solution)/shard_map/all_to_all | solution.py:63
  89.8 22.4 %all-to-all-done.1 = bf16[8,256,512]{2,1,0:T(8,128)(2,1)} async-done(((bf16[8,256,512]{2,1,0:T(8,128)(2,1)}), bf16[8,256,512]{2,1,0:T(8,128)(2,1)}, u32[]{:S(2)}, u32[]{:S(2)}) %all-to-all-start.1) | async-done | bytes 2097184 | tf_op jit(solution)/shard_map/all_to_all | solution.py:63
  123.1 42.9 %all-gather.4.cloned.1.call-done.x_ref.refs_1_ = bf16[2048,2048]{1,0:T(8,128)(2,1)} async-done(((bf16[256,2048]{1,0:T(8,128)(2,1)}), bf16[2048,2048]{1,0:T(8,128)(2,1)}) %all-gather.4.cloned.1.call-update) | async-done | bytes 8388624 | tf_op jit(solution)/shard_map/all_gather | solution.py:521
  166.0 21.7 %attend.1 = (f32[2048,384]{1,0:T(8,128)}, bf16[2048,512]{1,0:T(8,128)(2,1)}, bf16[2048,256]{1,0:T(8,128)(2,1)}) custom-call(s32[10]{0:T(128)} %pad_add_fusion.1.lead_ref, bf16[2048,2048]{1,0:T(8,128)(2,1)} %all-gather.4.cloned.1.call-done.x_ref.refs_1_, bf16[2048,512]{1,0:T(8,128)(2,1)} %bitcast.6.refs_1_.w_ref, f32[1,128]{1,0:T(1,128)} %reshape.285.qg_ref, ...), custom_call_target="tpu_custom_call" | custom-call | flops 8589934592 | bytes 20971520 | tf_op jit(solution)/shard_map/attend/pallas_call | solution.py:527
  194.3 38.7 %all-gather.6.cloned.1.call-done = bf16[2048,2048]{1,0:T(8,128)(2,1)} async-done(((bf16[256,2048]{1,0:T(8,128)(2,1)}), bf16[2048,2048]{1,0:T(8,128)(2,1)}) %all-gather.6.cloned.1.call-update) | async-done | bytes 8388624 | tf_op jit(solution)/shard_map/all_gather | solution.py:486
  233.0 6.4 multiply_reduce_fusion
  245.8 20.2 %collective-permute-start.7 = (bf16[256,2048]{1,0:T(8,128)(2,1)}, bf16[256,2048]{1,0:T(8,128)(2,1)S(1)}, u32[]{:S(2)}, u32[]{:S(2)}) collective-permute-start(bf16[256,2048]{1,0:T(8,128)(2,1)} %after.58), channel_id=1, source_target_pairs={{0,6},{1,7},{2,4},{3,5},{4,2},{5,3},{6,0},{7,1},{8,14},{9,15},{10,... | collective-permute-start | bytes 3145736 | tf_op jit(solution)/shard_map/ppermute | solution.py:81
  266.0 21.3 %collective-permute-start.6 = (bf16[256,2048]{1,0:T(8,128)(2,1)}, bf16[256,2048]{1,0:T(8,128)(2,1)S(1)}, u32[]{:S(2)}, u32[]{:S(2)}) collective-permute-start(bf16[256,2048]{1,0:T(8,128)(2,1)} %after.58), channel_id=1, source_target_pairs={{0,4},{1,5},{2,6},{3,7},{4,0},{5,1},{6,2},{7,3},{8,12},{9,13},{10,... | collective-permute-start | bytes 3145736 | tf_op jit(solution)/shard_map/ppermute | solution.py:81
  287.3 25.3 %collective-permute-done.7 = bf16[256,2048]{1,0:T(8,128)(2,1)S(1)} collective-permute-done((bf16[256,2048]{1,0:T(8,128)(2,1)}, bf16[256,2048]{1,0:T(8,128)(2,1)S(1)}, u32[]{:S(2)}, u32[]{:S(2)}) %collective-permute-start.7) | collective-permute-done | bytes 1048608 | tf_op jit(solution)/shard_map/ppermute | solution.py:81
  312.6 41.5 %collective-permute-done.6 = bf16[256,2048]{1,0:T(8,128)(2,1)S(1)} collective-permute-done((bf16[256,2048]{1,0:T(8,128)(2,1)}, bf16[256,2048]{1,0:T(8,128)(2,1)S(1)}, u32[]{:S(2)}, u32[]{:S(2)}) %collective-permute-start.6) | collective-permute-done | bytes 1048608 | tf_op jit(solution)/shard_map/ppermute | solution.py:81
  370.0 26.5 %collective-permute-done.4 = bf16[2048,384]{1,0:T(8,128)(2,1)} collective-permute-done((bf16[2048,384]{1,0:T(8,128)(2,1)}, bf16[2048,384]{1,0:T(8,128)(2,1)}, u32[]{:S(2)}, u32[]{:S(2)}) %collective-permute-start.4) | collective-permute-done | bytes 1572896 | tf_op jit(solution)/shard_map/ppermute | solution.py:89
  399.1 97.3 %collective-permute-done.3 = bf16[2048,384]{1,0:T(8,128)(2,1)} collective-permute-done((bf16[2048,384]{1,0:T(8,128)(2,1)}, bf16[2048,384]{1,0:T(8,128)(2,1)}, u32[]{:S(2)}, u32[]{:S(2)}) %collective-permute-start.3) | collective-permute-done | bytes 1572896 | tf_op jit(solution)/shard_map/ppermute | solution.py:89
  525.2 19.3 %fusion.40 = f32[2048,1536]{1,0:T(8,128)} fusion(bf16[2048,2048]{1,0:T(8,128)(2,1)} %all-gather.8.cloned.1.call-done, bf16[2048,1536]{0,1:T(8,128)(2,1)} %bitcast.21), kind=kOutput, calls=%fused_computation.164 | convolution fusion | flops 12884901888 | bytes 27262976 | tf_op jit(solution)/shard_map/dot_general | solution.py:179
  544.5 15.5 %multiply_convert_fusion.1 = (bf16[2048,768]{1,0:T(8,128)(2,1)S(1)}, bf16[2048,768]{1,0:T(8,128)(2,1)S(1)}, bf16[2048,768]{1,0:T(8,128)(2,1)}) fusion(f32[2048,1536]{1,0:T(8,128)} %fusion.40, bf16[2048,2048]{1,0:T(8,128)(2,1)} %bitcast.26, bf16[768,2048]{1,0:T(8,128)(2,1)S(1)} %copy-done), kind=kOutput, calls=%fused_computation.6 | convolution fusion | flops 6467616768 | bytes 33554432 | tf_op jit(solution)/shard_map/dot_general | solution.py:183
  562.7 17.5 %convolution_convert_fusion.2 = bf16[2048,2048]{1,0:T(8,128)(2,1)} fusion(bf16[2048,1536]{0,1:T(8,128)(2,1)} %bitcast.21, bf16[2048,768]{1,0:T(8,128)(2,1)S(1)} %get-tuple-element.96, bf16[2048,768]{1,0:T(8,128)(2,1)S(1)} %get-tuple-element.95), kind=kOutput, calls=%fused_computation.2 | convolution fusion | flops 12901679104 | bytes 20971520 | tf_op jit(solution)/shard_map/dot_general | solution.py:183
  580.3 12.8 convolution_convert_fusion.4.refs_1_
  593.1 18.3 %convolution_convert_fusion.3.refs_2_ = bf16[2048,1536]{1,0:T(8,128)(2,1)} fusion(bf16[2048,2048]{1,0:T(8,128)(2,1)} %all-gather.8.cloned.1.call-done, bf16[2048,768]{1,0:T(8,128)(2,1)S(1)} %copy-done.48, bf16[2048,768]{1,0:T(8,128)(2,1)S(1)} %copy-done.46), kind=kOutput, calls=%fused_computation.3 | convolution fusion | flops 12900630528 | bytes 20971520 | tf_op jit(solution)/shard_map/dot_general | solution.py:187
  611.4 37.8 %reduce-scatter.5.cloned.1.call-done.refs_0_ = bf16[256,2048]{1,0:T(8,128)(2,1)} async-done(((bf16[2048,2048]{1,0:T(8,128)(2,1)}), bf16[256,2048]{1,0:T(8,128)(2,1)}) %reduce-scatter.5.cloned.1.call-update) | async-done | bytes 1048592 | tf_op jit(solution)/shard_map/reduce_scatter | solution.py:549
  655.4 6.8 convolution_convert_fusion
  662.3 6.4 convolution_convert_fusion.6
  668.8 18.5 %all_to_all.40 = bf16[8,256,256]{2,1,0:T(8,128)(2,1)} all-to-all(bf16[8,256,256]{2,1,0:T(8,128)(2,1)S(1)} %bitcast.88), channel_id=1, replica_groups=mesh['seq'=4,'fsdp'=8] {'fsdp'}, dimensions={0} | all-to-all | bytes 2097152 | tf_op jit(solution)/shard_map/all_to_all | solution.py:59
  687.2 36.5 %attend_back.1 = (bf16[2048,512]{1,0:T(8,128)(2,1)}, bf16[2048,2048]{1,0:T(8,128)(2,1)}, f32[8,128]{1,0:T(8,128)}) custom-call(s32[10]{0:T(128)} %pad_add_fusion.1.lead_ref, bf16[2048,256]{1,0:T(8,128)(2,1)} %bitcast.98, bf16[2048,512]{1,0:T(8,128)(2,1)} %get-tuple-element.48.qkv_ref, f32[2048,384]{1,0:T(8,128)} %get-tuple-element.49.proj_ref, ...), custom_call_target="tpu_custom_call" | custom-call | flops 17179869184 | bytes 31457280 | tf_op jit(solution)/shard_map/attend_back/pallas_call | solution.py:566
  738.4 14.8 %collective-permute-done.36.refs_1_ = bf16[192,2048]{1,0:T(8,128)(2,1)} collective-permute-done((bf16[192,2048]{1,0:T(8,128)(2,1)S(1)}, bf16[192,2048]{1,0:T(8,128)(2,1)}, u32[]{:S(2)}, u32[]{:S(2)}) %collective-permute-start.36) | collective-permute-done | bytes 786464 | tf_op jit(solution)/shard_map/ppermute | solution.py:123
  758.7 11.6 collective-permute-done.11.refs_1_
  774.7 12.4 collective-permute-done.37.refs_1_
  787.1 16.2 %collective-permute-done.12.refs_1_ = bf16[192,2048]{1,0:T(8,128)(2,1)S(1)} collective-permute-done((bf16[192,2048]{1,0:T(8,128)(2,1)}, bf16[192,2048]{1,0:T(8,128)(2,1)S(1)}, u32[]{:S(2)}, u32[]{:S(2)}) %collective-permute-start.12) | collective-permute-done | bytes 786464 | tf_op jit(solution)/shard_map/ppermute | solution.py:123
  819.3 17.5 %collective-permute-start.39 = (bf16[1,256,1536]{2,1,0:T(8,128)(2,1)}, bf16[1,256,1536]{2,1,0:T(8,128)(2,1)}, u32[]{:S(2)}, u32[]{:S(2)}) collective-permute-start(bf16[1,256,1536]{2,1,0:T(8,128)(2,1)} %after.87), channel_id=1, source_target_pairs={{0,8},{24,16},{1,9},{25,17},{2,10},{26,18},{3,11},{27,19},{4,12},{... | collective-permute-start | bytes 2359304 | tf_op jit(solution)/shard_map/ppermute | solution.py:123
  845.1 6.7 collective-permute-done.39.refs_1_
  855.1 7.3 collective-permute-done.40.refs_2_
  874.8 22.1 %collective-permute-start.42 = (bf16[1,256,1536]{2,1,0:T(8,128)(2,1)}, bf16[1,256,1536]{2,1,0:T(8,128)(2,1)}, u32[]{:S(2)}, u32[]{:S(2)}) collective-permute-start(bf16[1,256,1536]{2,1,0:T(8,128)(2,1)} %after.90), channel_id=1, source_target_pairs={{0,8},{24,16},{1,9},{25,17},{2,10},{26,18},{3,11},{27,19},{4,12},{... | collective-permute-start | bytes 2359304 | tf_op jit(solution)/shard_map/ppermute | solution.py:123
  907.8 8.7 collective-permute-start.14
  924.4 10.8 convolution_convert_fusion.1
  943.3 11.3 collective-permute-done.46.refs_1_.got_ref
  961.9 7.5 collective-permute-done.17.refs_1_
  969.4 8.4 collective-permute-done.47.refs_1_.got_ref
  1000.9 29.9 %collective-permute-start.21 = (bf16[1,256,1536]{2,1,0:T(8,128)(2,1)}, bf16[1,256,1536]{2,1,0:T(8,128)(2,1)}, u32[]{:S(2)}, u32[]{:S(2)}) collective-permute-start(bf16[1,256,1536]{2,1,0:T(8,128)(2,1)} %after.70), channel_id=1, source_target_pairs={{0,8},{24,16},{8,0},{16,24},{1,9},{25,17},{9,1},{17,25},{2,10},{26... | collective-permute-start | bytes 2359304 | tf_op jit(solution)/shard_map/ppermute | solution.py:123
  1045.1 10.0 convolution_convert_fusion.5
  1088.9 12.9 collective-permute-start.49
  1129.4 6.6 collective-permute-done.24.refs_1_
  1146.6 7.2 collective-permute-start.27
  1160.9 9.5 collective-permute-start.10
  1170.4 9.5 collective-permute-start.9
  1179.9 18.2 %collective-permute-start.30 = (bf16[2,256,512]{2,1,0:T(8,128)(2,1)}, bf16[2,256,512]{2,1,0:T(8,128)(2,1)}, u32[]{:S(2)}, u32[]{:S(2)}) collective-permute-start(bf16[2,256,512]{2,1,0:T(8,128)(2,1)} %after.79), channel_id=1, source_target_pairs={{0,8},{24,16},{1,9},{25,17},{2,10},{26,18},{3,11},{27,19},{4,12},{... | collective-permute-start | bytes 1572872 | tf_op jit(solution)/shard_map/ppermute | solution.py:123
  1261.6 8.8 collective-permute-done.56.refs_1_.got_ref
  1274.6 7.0 collective-permute-done.34.refs_1_.got_ref
  1294.8 6.4 collective-permute-done.35.got_ref
  (438 shorter events, 431.9 us)
Async XLA Ops:
  36.3 44.9 %all-to-all-start.2 = ((bf16[8,256,384]{2,1,0:T(8,128)(2,1)}), bf16[8,256,384]{2,1,0:T(8,128)(2,1)}, u32[]{:S(2)}, u32[]{:S(2)}) async-start(bf16[8,256,384]{2,1,0:T(8,128)(2,1)} %after.54), calls=%async_computation.2 | async-start | bytes 3145728 | tf_op jit(solution)/shard_map/all_to_all | solution.py:63
  40.6 45.1 %collective-permute-start = (bf16[256,2048]{1,0:T(8,128)(2,1)}, bf16[256,2048]{1,0:T(8,128)(2,1)}, u32[]{:S(2)}, u32[]{:S(2)}) collective-permute-start(bf16[256,2048]{1,0:T(8,128)(2,1)} %bitcast.112), channel_id=1, source_target_pairs={{0,0},{1,27},{2,10},{3,17},{4,20},{5,15},{6,30},{7,5},{8,2},{9,25}... | collective-permute-start | bytes 3145736 | tf_op jit(solution)/shard_map/ppermute | solution.py:35
  81.2 31.0 %all-to-all-start.1 = ((bf16[8,256,512]{2,1,0:T(8,128)(2,1)}), bf16[8,256,512]{2,1,0:T(8,128)(2,1)}, u32[]{:S(2)}, u32[]{:S(2)}) async-start(bf16[8,256,512]{2,1,0:T(8,128)(2,1)} %after.53), calls=%async_computation.1 | async-start | bytes 4194304 | tf_op jit(solution)/shard_map/all_to_all | solution.py:63
  85.5 80.4 %all-gather.4.cloned.1.call-start = ((), (), s32[]{:S(2)}) async-start(), calls=%async_computation.12 | async-start | bytes 9437184 | tf_op jit(solution)/shard_map/all_gather | solution.py:521
  112.2 120.8 %all-gather.6.cloned.1.call-start = ((), (), s32[]{:S(2)}) async-start(), calls=%async_computation.13 | async-start | bytes 9437184 | tf_op jit(solution)/shard_map/all_gather | solution.py:486
  190.0 43.0 %all-to-all-start.3 = ((bf16[8,256,256]{1,2,0:T(8,128)(2,1)}), bf16[8,256,256]{1,2,0:T(8,128)(2,1)}, u32[]{:S(2)}, u32[]{:S(2)}) async-start(bf16[8,256,256]{1,2,0:T(8,128)(2,1)} %copy.157), calls=%async_computation.3 | async-start | bytes 2097152 | tf_op jit(solution)/shard_map/all_to_all | solution.py:59
  194.2 331.0 %all-gather.8.cloned.1.call-start = ((), (), s32[]{:S(2)}) async-start(), calls=%async_computation.14 | async-start | bytes 9437184 | tf_op jit(solution)/shard_map/all_gather | solution.py:536
  241.9 407.3 %reduce-scatter.5.cloned.1.call-start = ((), (), s32[]{:S(2)}) async-start(), calls=%async_computation.15 | async-start | bytes 9437184 | tf_op jit(solution)/shard_map/reduce_scatter | solution.py:549
  245.8 66.8 %collective-permute-start.7 = (bf16[256,2048]{1,0:T(8,128)(2,1)}, bf16[256,2048]{1,0:T(8,128)(2,1)S(1)}, u32[]{:S(2)}, u32[]{:S(2)}) collective-permute-start(bf16[256,2048]{1,0:T(8,128)(2,1)} %after.58), channel_id=1, source_target_pairs={{0,6},{1,7},{2,4},{3,5},{4,2},{5,3},{6,0},{7,1},{8,14},{9,15},{10,... | collective-permute-start | bytes 3145736 | tf_op jit(solution)/shard_map/ppermute | solution.py:81
  266.0 88.0 %collective-permute-start.6 = (bf16[256,2048]{1,0:T(8,128)(2,1)}, bf16[256,2048]{1,0:T(8,128)(2,1)S(1)}, u32[]{:S(2)}, u32[]{:S(2)}) collective-permute-start(bf16[256,2048]{1,0:T(8,128)(2,1)} %after.58), channel_id=1, source_target_pairs={{0,4},{1,5},{2,6},{3,7},{4,0},{5,1},{6,2},{7,3},{8,12},{9,13},{10,... | collective-permute-start | bytes 3145736 | tf_op jit(solution)/shard_map/ppermute | solution.py:81
  287.3 66.8 %collective-permute-start.5 = (bf16[256,2048]{1,0:T(8,128)(2,1)}, bf16[256,2048]{1,0:T(8,128)(2,1)S(1)}, u32[]{:S(2)}, u32[]{:S(2)}) collective-permute-start(bf16[256,2048]{1,0:T(8,128)(2,1)} %after.58), channel_id=1, source_target_pairs={{0,2},{1,3},{2,0},{3,1},{4,6},{5,7},{6,4},{7,5},{8,10},{9,11},{10,... | collective-permute-start | bytes 3145736 | tf_op jit(solution)/shard_map/ppermute | solution.py:81
  357.8 154.7 %collective-permute-start.8 = (bf16[4,256,2048]{2,1,0:T(8,128)(2,1)}, bf16[4,256,2048]{2,1,0:T(8,128)(2,1)}, u32[]{:S(2)}, u32[]{:S(2)}) collective-permute-start(bf16[4,256,2048]{2,1,0:T(8,128)(2,1)} %pad_maximum_fusion.1), channel_id=1, source_target_pairs={{0,1},{1,0},{2,3},{3,2},{4,5},{5,4},{6,7},{7,6},{8,9},{9,8},{10,11... | collective-permute-start | bytes 12582920 | tf_op jit(solution)/shard_map/ppermute | solution.py:81
  358.6 37.9 %collective-permute-start.4 = (bf16[2048,384]{1,0:T(8,128)(2,1)}, bf16[2048,384]{1,0:T(8,128)(2,1)}, u32[]{:S(2)}, u32[]{:S(2)}) collective-permute-start(bf16[2048,384]{1,0:T(8,128)(2,1)} %after.57), channel_id=1, source_target_pairs={{0,24},{8,0},{16,8},{24,16},{1,25},{9,1},{17,9},{25,17},{2,26},{10... | collective-permute-start | bytes 4718600 | tf_op jit(solution)/shard_map/ppermute | solution.py:89
  361.3 135.1 %collective-permute-start.3 = (bf16[2048,384]{1,0:T(8,128)(2,1)}, bf16[2048,384]{1,0:T(8,128)(2,1)}, u32[]{:S(2)}, u32[]{:S(2)}) collective-permute-start(bf16[2048,384]{1,0:T(8,128)(2,1)} %after.57), channel_id=1, source_target_pairs={{0,16},{8,24},{16,0},{24,8},{1,17},{9,25},{17,1},{25,9},{2,18},{10... | collective-permute-start | bytes 4718600 | tf_op jit(solution)/shard_map/ppermute | solution.py:89
  361.3 137.8 %collective-permute-start.2 = (bf16[2048,384]{1,0:T(8,128)(2,1)}, bf16[2048,384]{1,0:T(8,128)(2,1)}, u32[]{:S(2)}, u32[]{:S(2)}) collective-permute-start(bf16[2048,384]{1,0:T(8,128)(2,1)} %after.57), channel_id=1, source_target_pairs={{0,8},{8,16},{16,24},{24,0},{1,9},{9,17},{17,25},{25,1},{2,10},{10... | collective-permute-start | bytes 4718600 | tf_op jit(solution)/shard_map/ppermute | solution.py:89
  580.2 521.5 %reduce-scatter.11.cloned.1.call-start = ((), (), s32[]{:S(2)}) async-start(), calls=%async_computation.18 | async-start | bytes 9437184 | tf_op jit(solution)/shard_map/reduce_scatter | solution.py:563
  662.2 457.9 %reduce-scatter.9.cloned.1.call-start = ((), (), s32[]{:S(2)}) async-start(), calls=%async_computation.17 | async-start | bytes 9437184 | tf_op jit(solution)/shard_map/reduce_scatter | solution.py:579
  723.7 93.5 %all-to-all-start.7 = ((bf16[8,256,1536]{2,1,0:T(8,128)(2,1)}), bf16[8,256,1536]{2,1,0:T(8,128)(2,1)}, u32[]{:S(2)}, u32[]{:S(2)}) async-start(bf16[8,256,1536]{2,1,0:T(8,128)(2,1)} %bitcast.84), calls=%async_computation.11 | async-start | bytes 12582912 | tf_op jit(solution)/shard_map/all_to_all | solution.py:63
  728.5 425.3 %reduce-scatter.7.cloned.1.call-start = ((), (), s32[]{:S(2)}) async-start(), calls=%async_computation.16 | async-start | bytes 9437184 | tf_op jit(solution)/shard_map/reduce_scatter | solution.py:593
  736.3 34.0 %collective-permute-start.11 = (bf16[192,2048]{1,0:T(8,128)(2,1)}, bf16[192,2048]{1,0:T(8,128)(2,1)}, u32[]{:S(2)}, u32[]{:S(2)}) collective-permute-start(bf16[192,2048]{1,0:T(8,128)(2,1)} %get-tuple-element.115), channel_id=1, source_target_pairs={{0,8},{24,16},{1,9},{25,17},{2,10},{26,18},{3,11},{27,19},{4,12},{... | collective-permute-start | bytes 2359304 | tf_op jit(solution)/shard_map/ppermute | solution.py:123
  753.3 33.8 %collective-permute-start.37 = (bf16[192,2048]{1,0:T(8,128)(2,1)}, bf16[192,2048]{1,0:T(8,128)(2,1)}, u32[]{:S(2)}, u32[]{:S(2)}) collective-permute-start(bf16[192,2048]{1,0:T(8,128)(2,1)} %after.85), channel_id=1, source_target_pairs={{0,8},{24,16},{1,9},{25,17},{2,10},{26,18},{3,11},{27,19},{4,12},{... | collective-permute-start | bytes 2359304 | tf_op jit(solution)/shard_map/ppermute | solution.py:123
  770.2 33.1 %collective-permute-start.12 = (bf16[192,2048]{1,0:T(8,128)(2,1)}, bf16[192,2048]{1,0:T(8,128)(2,1)S(1)}, u32[]{:S(2)}, u32[]{:S(2)}) collective-permute-start(bf16[192,2048]{1,0:T(8,128)(2,1)} %after.61), channel_id=1, source_target_pairs={{0,8},{24,16},{1,9},{25,17},{2,10},{26,18},{3,11},{27,19},{4,12},{... | collective-permute-start | bytes 2359304 | tf_op jit(solution)/shard_map/ppermute | solution.py:123
  819.3 32.5 %collective-permute-start.39 = (bf16[1,256,1536]{2,1,0:T(8,128)(2,1)}, bf16[1,256,1536]{2,1,0:T(8,128)(2,1)}, u32[]{:S(2)}, u32[]{:S(2)}) collective-permute-start(bf16[1,256,1536]{2,1,0:T(8,128)(2,1)} %after.87), channel_id=1, source_target_pairs={{0,8},{24,16},{1,9},{25,17},{2,10},{26,18},{3,11},{27,19},{4,12},{... | collective-permute-start | bytes 2359304 | tf_op jit(solution)/shard_map/ppermute | solution.py:123
  868.6 32.9 %collective-permute-start.13 = (bf16[192,2048]{1,0:T(8,128)(2,1)}, bf16[192,2048]{1,0:T(8,128)(2,1)}, u32[]{:S(2)}, u32[]{:S(2)}) collective-permute-start(bf16[192,2048]{1,0:T(8,128)(2,1)} %after.62), channel_id=1, source_target_pairs={{8,16},{16,8},{9,17},{17,9},{10,18},{18,10},{11,19},{19,11},{12,20... | collective-permute-start | bytes 2359304 | tf_op jit(solution)/shard_map/ppermute | solution.py:123
  874.8 41.8 %collective-permute-start.42 = (bf16[1,256,1536]{2,1,0:T(8,128)(2,1)}, bf16[1,256,1536]{2,1,0:T(8,128)(2,1)}, u32[]{:S(2)}, u32[]{:S(2)}) collective-permute-start(bf16[1,256,1536]{2,1,0:T(8,128)(2,1)} %after.90), channel_id=1, source_target_pairs={{0,8},{24,16},{1,9},{25,17},{2,10},{26,18},{3,11},{27,19},{4,12},{... | collective-permute-start | bytes 2359304 | tf_op jit(solution)/shard_map/ppermute | solution.py:123
  905.0 31.4 %collective-permute-start.15 = (bf16[192,2048]{1,0:T(8,128)(2,1)}, bf16[192,2048]{1,0:T(8,128)(2,1)}, u32[]{:S(2)}, u32[]{:S(2)}) collective-permute-start(bf16[192,2048]{1,0:T(8,128)(2,1)} %after.64), channel_id=1, source_target_pairs={{8,0},{16,24},{9,1},{17,25},{10,2},{18,26},{11,3},{19,27},{12,4},{... | collective-permute-start | bytes 2359304 | tf_op jit(solution)/shard_map/ppermute | solution.py:123
  906.3 30.1 %collective-permute-start.16 = (bf16[192,2048]{1,0:T(8,128)(2,1)}, bf16[192,2048]{1,0:T(8,128)(2,1)}, u32[]{:S(2)}, u32[]{:S(2)}) collective-permute-start(bf16[192,2048]{1,0:T(8,128)(2,1)} %after.65), channel_id=1, source_target_pairs={{8,16},{16,8},{9,17},{17,9},{10,18},{18,10},{11,19},{19,11},{12,20... | collective-permute-start | bytes 2359304 | tf_op jit(solution)/shard_map/ppermute | solution.py:123
  907.8 28.6 %collective-permute-start.14 = (bf16[1,256,1536]{2,1,0:T(8,128)(2,1)}, bf16[1,256,1536]{2,1,0:T(8,128)(2,1)}, u32[]{:S(2)}, u32[]{:S(2)}) collective-permute-start(bf16[1,256,1536]{2,1,0:T(8,128)(2,1)} %after.63), channel_id=1, source_target_pairs={{0,8},{24,16},{1,9},{25,17},{2,10},{26,18},{3,11},{27,19},{4,12},{... | collective-permute-start | bytes 2359304 | tf_op jit(solution)/shard_map/ppermute | solution.py:123
  936.4 33.0 %collective-permute-start.17 = (bf16[1,256,1536]{2,1,0:T(8,128)(2,1)}, bf16[1,256,1536]{2,1,0:T(8,128)(2,1)}, u32[]{:S(2)}, u32[]{:S(2)}) collective-permute-start(bf16[1,256,1536]{2,1,0:T(8,128)(2,1)} %after.66), channel_id=1, source_target_pairs={{0,8},{24,16},{1,9},{25,17},{2,10},{26,18},{3,11},{27,19},{4,12},{... | collective-permute-start | bytes 2359304 | tf_op jit(solution)/shard_map/ppermute | solution.py:123
  960.6 27.4 %collective-permute-start.18 = (bf16[192,2048]{1,0:T(8,128)(2,1)}, bf16[192,2048]{1,0:T(8,128)(2,1)}, u32[]{:S(2)}, u32[]{:S(2)}) collective-permute-start(bf16[192,2048]{1,0:T(8,128)(2,1)} %after.67), channel_id=1, source_target_pairs={{8,0},{16,24},{9,1},{17,25},{10,2},{18,26},{11,3},{19,27},{12,4},{... | collective-permute-start | bytes 2359304 | tf_op jit(solution)/shard_map/ppermute | solution.py:123
  994.8 41.0 %collective-permute-start.48 = (bf16[1,256,1536]{2,1,0:T(8,128)(2,1)}, bf16[1,256,1536]{2,1,0:T(8,128)(2,1)}, u32[]{:S(2)}, u32[]{:S(2)}) collective-permute-start(bf16[1,256,1536]{2,1,0:T(8,128)(2,1)} %after.96), channel_id=1, source_target_pairs={{8,16},{16,8},{9,17},{17,9},{10,18},{18,10},{11,19},{19,11},{12,20... | collective-permute-start | bytes 2359304 | tf_op jit(solution)/shard_map/ppermute | solution.py:123
  1000.9 42.3 %collective-permute-start.21 = (bf16[1,256,1536]{2,1,0:T(8,128)(2,1)}, bf16[1,256,1536]{2,1,0:T(8,128)(2,1)}, u32[]{:S(2)}, u32[]{:S(2)}) collective-permute-start(bf16[1,256,1536]{2,1,0:T(8,128)(2,1)} %after.70), channel_id=1, source_target_pairs={{0,8},{24,16},{8,0},{16,24},{1,9},{25,17},{9,1},{17,25},{2,10},{26... | collective-permute-start | bytes 2359304 | tf_op jit(solution)/shard_map/ppermute | solution.py:123
  1035.9 34.6 %collective-permute-start.51 = (bf16[1,256,1536]{2,1,0:T(8,128)(2,1)}, bf16[1,256,1536]{2,1,0:T(8,128)(2,1)}, u32[]{:S(2)}, u32[]{:S(2)}) collective-permute-start(bf16[1,256,1536]{2,1,0:T(8,128)(2,1)} %after.99), channel_id=1, source_target_pairs={{8,16},{16,8},{9,17},{17,9},{10,18},{18,10},{11,19},{19,11},{12,20... | collective-permute-start | bytes 2359304 | tf_op jit(solution)/shard_map/ppermute | solution.py:123
  1055.0 31.0 %all-to-all-start.6 = ((bf16[8,256,512]{2,1,0:T(8,128)(2,1)}), bf16[8,256,512]{2,1,0:T(8,128)(2,1)}, u32[]{:S(2)}, u32[]{:S(2)}) async-start(bf16[8,256,512]{2,1,0:T(8,128)(2,1)} %bitcast.93), calls=%async_computation.9 | async-start | bytes 4194304 | tf_op jit(solution)/shard_map/all_to_all | solution.py:63
  1069.2 40.5 %collective-permute-start.50 = (bf16[1,256,1536]{2,1,0:T(8,128)(2,1)}, bf16[1,256,1536]{2,1,0:T(8,128)(2,1)}, u32[]{:S(2)}, u32[]{:S(2)}) collective-permute-start(bf16[1,256,1536]{2,1,0:T(8,128)(2,1)} %after.98), channel_id=1, source_target_pairs={{8,0},{16,24},{9,1},{17,25},{10,2},{18,26},{11,3},{19,27},{12,4},{... | collective-permute-start | bytes 2359304 | tf_op jit(solution)/shard_map/ppermute | solution.py:123
  1075.9 30.4 %collective-permute-start.26 = (bf16[1,256,1536]{2,1,0:T(8,128)(2,1)}, bf16[1,256,1536]{2,1,0:T(8,128)(2,1)}, u32[]{:S(2)}, u32[]{:S(2)}) collective-permute-start(bf16[1,256,1536]{2,1,0:T(8,128)(2,1)} %after.75), channel_id=1, source_target_pairs={{8,16},{16,8},{9,17},{17,9},{10,18},{18,10},{11,19},{19,11},{12,20... | collective-permute-start | bytes 2359304 | tf_op jit(solution)/shard_map/ppermute | solution.py:123
  1080.8 48.6 %collective-permute-start.25 = (bf16[1,256,1536]{2,1,0:T(8,128)(2,1)}, bf16[1,256,1536]{2,1,0:T(8,128)(2,1)}, u32[]{:S(2)}, u32[]{:S(2)}) collective-permute-start(bf16[1,256,1536]{2,1,0:T(8,128)(2,1)} %after.74), channel_id=1, source_target_pairs={{8,0},{16,24},{9,1},{17,25},{10,2},{18,26},{11,3},{19,27},{12,4},{... | collective-permute-start | bytes 2359304 | tf_op jit(solution)/shard_map/ppermute | solution.py:123
  1104.1 31.9 %collective-permute-start.24 = (bf16[256,2048]{1,0:T(8,128)(2,1)}, bf16[256,2048]{1,0:T(8,128)(2,1)}, u32[]{:S(2)}, u32[]{:S(2)}) collective-permute-start(bf16[256,2048]{1,0:T(8,128)(2,1)} %after.73), channel_id=1, source_target_pairs={{0,8},{24,16},{1,9},{25,17},{2,10},{26,18},{3,11},{27,19},{4,12},{... | collective-permute-start | bytes 3145736 | tf_op jit(solution)/shard_map/ppermute | solution.py:123
  1113.6 88.5 %collective-permute-start.52 = (bf16[2,256,512]{2,1,0:T(8,128)(2,1)}, bf16[2,256,512]{2,1,0:T(8,128)(2,1)}, u32[]{:S(2)}, u32[]{:S(2)}) collective-permute-start(bf16[2,256,512]{2,1,0:T(8,128)(2,1)} %after.100), channel_id=1, source_target_pairs={{0,8},{24,16},{1,9},{25,17},{2,10},{26,18},{3,11},{27,19},{4,12},{... | collective-permute-start | bytes 1572872 | tf_op jit(solution)/shard_map/ppermute | solution.py:123
  1118.9 116.8 %collective-permute-start.53 = (bf16[1,256,1536]{2,1,0:T(8,128)(2,1)}, bf16[1,256,1536]{2,1,0:T(8,128)(2,1)}, u32[]{:S(2)}, u32[]{:S(2)}) collective-permute-start(bf16[1,256,1536]{2,1,0:T(8,128)(2,1)} %after.101), channel_id=1, source_target_pairs={{8,0},{16,24},{9,1},{17,25},{10,2},{18,26},{11,3},{19,27},{12,4},{... | collective-permute-start | bytes 2359304 | tf_op jit(solution)/shard_map/ppermute | solution.py:123
  1123.4 110.3 %all-to-all-start.5 = ((f32[32,1,640]{2,1,0:T(1,128)}), f32[32,1,640]{2,1,0:T(1,128)S(1)}, u32[]{:S(2)}, u32[]{:S(2)}) async-start(f32[32,1,640]{2,1,0:T(1,128)} %reshape.295), calls=%async_computation.8 | async-start | bytes 163840 | tf_op jit(solution)/shard_map/all_to_all | solution.py:624
  1136.0 34.4 %collective-permute-start.28 = (bf16[1,256,1536]{2,1,0:T(8,128)(2,1)}, bf16[1,256,1536]{2,1,0:T(8,128)(2,1)}, u32[]{:S(2)}, u32[]{:S(2)}) collective-permute-start(bf16[1,256,1536]{2,1,0:T(8,128)(2,1)} %after.77), channel_id=1, source_target_pairs={{8,0},{16,24},{9,1},{17,25},{10,2},{18,26},{11,3},{19,27},{12,4},{... | collective-permute-start | bytes 2359304 | tf_op jit(solution)/shard_map/ppermute | solution.py:123
  1141.2 38.7 %collective-permute-start.29 = (bf16[256,2048]{1,0:T(8,128)(2,1)}, bf16[256,2048]{1,0:T(8,128)(2,1)}, u32[]{:S(2)}, u32[]{:S(2)}) collective-permute-start(bf16[256,2048]{1,0:T(8,128)(2,1)} %after.78), channel_id=1, source_target_pairs={{8,16},{16,8},{9,17},{17,9},{10,18},{18,10},{11,19},{19,11},{12,20... | collective-permute-start | bytes 3145736 | tf_op jit(solution)/shard_map/ppermute | solution.py:123
  1160.9 82.5 %collective-permute-start.10 = (bf16[256,2048]{1,0:T(8,128)(2,1)}, bf16[256,2048]{1,0:T(8,128)(2,1)}, u32[]{:S(2)}, u32[]{:S(2)}) collective-permute-start(bf16[256,2048]{1,0:T(8,128)(2,1)} %fusion.9), channel_id=1, source_target_pairs={{0,0},{27,1},{10,2},{17,3},{20,4},{15,5},{30,6},{5,7},{2,8},{25,9}... | collective-permute-start | bytes 3145736 | tf_op jit(solution)/shard_map/ppermute | solution.py:35
  1170.4 73.0 %collective-permute-start.9 = (bf16[256,2048]{1,0:T(8,128)(2,1)}, bf16[256,2048]{1,0:T(8,128)(2,1)}, u32[]{:S(2)}, u32[]{:S(2)}) collective-permute-start(bf16[256,2048]{1,0:T(8,128)(2,1)} %add_convert_fusion.2), channel_id=1, source_target_pairs={{0,0},{27,1},{10,2},{17,3},{20,4},{15,5},{30,6},{5,7},{2,8},{25,9}... | collective-permute-start | bytes 3145736 | tf_op jit(solution)/shard_map/ppermute | solution.py:35
  1179.9 26.9 %collective-permute-start.30 = (bf16[2,256,512]{2,1,0:T(8,128)(2,1)}, bf16[2,256,512]{2,1,0:T(8,128)(2,1)}, u32[]{:S(2)}, u32[]{:S(2)}) collective-permute-start(bf16[2,256,512]{2,1,0:T(8,128)(2,1)} %after.79), channel_id=1, source_target_pairs={{0,8},{24,16},{1,9},{25,17},{2,10},{26,18},{3,11},{27,19},{4,12},{... | collective-permute-start | bytes 1572872 | tf_op jit(solution)/shard_map/ppermute | solution.py:123
  1202.0 50.8 %collective-permute-start.31 = (bf16[256,2048]{1,0:T(8,128)(2,1)}, bf16[256,2048]{1,0:T(8,128)(2,1)}, u32[]{:S(2)}, u32[]{:S(2)}) collective-permute-start(bf16[256,2048]{1,0:T(8,128)(2,1)} %after.80), channel_id=1, source_target_pairs={{8,0},{16,24},{9,1},{17,25},{10,2},{18,26},{11,3},{19,27},{12,4},{... | collective-permute-start | bytes 3145736 | tf_op jit(solution)/shard_map/ppermute | solution.py:123
  1212.1 35.1 %collective-permute-start.54 = (bf16[2,256,512]{2,1,0:T(8,128)(2,1)}, bf16[2,256,512]{2,1,0:T(8,128)(2,1)}, u32[]{:S(2)}, u32[]{:S(2)}) collective-permute-start(bf16[2,256,512]{2,1,0:T(8,128)(2,1)} %after.102), channel_id=1, source_target_pairs={{8,16},{16,8},{9,17},{17,9},{10,18},{18,10},{11,19},{19,11},{12,20... | collective-permute-start | bytes 1572872 | tf_op jit(solution)/shard_map/ppermute | solution.py:123
  (73 other events, 1160.7 us)
Sparse Core Ops, SparseCore 0:
  112.3 53.6 all-gather.3
  167.8 65.0 all-gather.5
  242.0 112.0 all-gather.7
  580.4 68.8 reduce-scatter.4
  662.4 72.3 reduce-scatter.10
  738.0 105.8 reduce-scatter.8
  935.3 70.9 reduce-scatter.6
